TPU v7x, 32 devices: a whole 2x2x4 slice. The times are simulated.
32 devices in a mesh: tower: 2 (over y), dp: 16 (over z, x, core).
Axes of the slice: x: 2, y: 2, z: 4, core: 2. Of those that a mesh axis runs over, the one named last changes fastest.
Arguments:
- tokens: bfloat16 [2, 4096, 768], P('tower', 'dp'), may hold values from -6 to 6
- query_lengths: int32 [64], P('dp'), may hold values from 8 to 64, as said below
- doc_lengths: int32 [16], P('dp'), may hold values from 32 to 256, as said below
- positives: int32 [64], replicated, may hold values from 0 to 15
- w_qkv: bfloat16 [768, 2304], P('dp'), may hold values from -0.21875 to 0.21875
- w_out: bfloat16 [768, 768], P('dp'), may hold values from -0.21875 to 0.21875
- w_gate: bfloat16 [768, 3072], P('dp'), may hold values from -0.21875 to 0.21875
- w_up: bfloat16 [768, 3072], P('dp'), may hold values from -0.21875 to 0.21875
- w_down: bfloat16 [3072, 768], P('dp'), may hold values from -0.109375 to 0.109375
- ln1_gain: bfloat16 [768], P('dp'), may hold values from 0.5 to 1.5
- first_layernorm_shift: bfloat16 [768], P('dp'), may hold values from -0.59765625 to 0.59765625
- ln2_gain: bfloat16 [768], P('dp'), may hold values from 0.5 to 1.5
- ln2_bias: bfloat16 [768], P('dp'), may hold values from -0.6 to 0.6
Outputs:
- loss: float32 [], replicated
- query_embeddings: float32 [64, 768], P('dp')
- doc_embeddings: float32 [16, 768], P('dp')
- token_grad: float32 [2, 4096, 768], P('tower', 'dp')
- w_qkv_grad: float32 [768, 2304], P('dp')
- w_out_grad: float32 [768, 768], P('dp')
- w_gate_grad: float32 [768, 3072], P('dp')
- w_up_grad: float32 [768, 3072], P('dp')
- w_down_grad: float32 [3072, 768], P('dp')
- ln1_gain_grad: float32 [768], P('dp')
- ln1_bias_grad: float32 [768], P('dp')
- ln2_gain_grad: float32 [768], P('dp')
- ln2_bias_grad: float32 [768], P('dp')
Inputs may be any that keep to these rules, and one draw needn't show every extreme that they name: `query_lengths`: each query has 8 to 64 real tokens in the first slots of its block; some query has 64. `doc_lengths`: each document has 32 to 256 real tokens in the first slots; some document has 256.
All inputs are finite; a program needn't handle non-finite values.
Results may differ from a plain program's by a relative error of at most 0.0085.
Values may be sent and summed in bfloat16 or wider, within the bound.
A program may use at most 128 MiB of HBM per device.

v0:
```python
import jax
import jax.numpy as jnp
from jax import lax
from jax.sharding import PartitionSpec as P

D = 768
HEADS = 12
HEAD = 64
QLEN = 64
QPD = 4


exact_product_accuracy = lax.Precision.HIGHEST
rope_base = 1000.0
contrast_sharpness_factor = 0.02


def product(left, right):
    return jnp.dot(left, right, preferred_element_type=jnp.float32)


def rotary_tables(places):
    freqs = jnp.power(rope_base, -2.0 * jnp.arange(HEAD // 2).astype(jnp.float32) / HEAD)
    angles = places[:, None] * freqs[None, :]
    return (jnp.cos(angles)[:, None, :], jnp.sin(angles)[:, None, :])


def rotate(values, cosines, sines):
    half_dim = values.shape[-1] // 2
    first = values[..., :half_dim]
    second = values[..., half_dim:]
    return jnp.concatenate(
        [first * cosines - second * sines, second * cosines + first * sines], axis=-1
    )


def layer_norm(hidden, gain, offset):
    average = jnp.mean(hidden, -1, keepdims=True)
    centred = hidden - average
    variance = jnp.mean(centred * centred, -1, keepdims=True)
    return centred * lax.rsqrt(variance + 1e-05) * gain + offset


def normalize(pooled):
    return pooled * lax.rsqrt(jnp.sum(pooled * pooled, -1, keepdims=True) + 1e-06)


def layout(tower_id, query_len, doc_len, count):
    places = jnp.arange(count)
    span = jnp.where(tower_id == 0, QLEN, count)
    segment = places // span
    offset_in = places - segment * span
    slots = jnp.arange(QPD)
    seg_limit = jnp.where(tower_id == 0, query_len, doc_len[0] * jnp.ones_like(query_len))
    limit = jnp.sum(jnp.where(segment[:, None] == slots[None, :], seg_limit[None, :], 0), axis=1)
    valid = offset_in < limit
    allowed = (segment[:, None] == segment[None, :]) & valid[None, :]
    member = (segment[None, :] == slots[:, None]) & valid[None, :]
    pool_matrix = jnp.where(member, 1.0 / seg_limit[:, None].astype(jnp.float32), 0.0)
    return (offset_in.astype(jnp.float32), allowed, pool_matrix)


def swish_product(left, right):
    return jax.nn.silu(left) * right


def on_device(
    tokens,
    query_lengths,
    doc_lengths,
    positives,
    w_qkv,
    w_out,
    w_gate,
    w_up,
    w_down,
    ln1_gain,
    first_layernorm_shift,
    ln2_gain,
    ln2_bias,
):
    tower_id = lax.axis_index("tower")
    device_id = lax.axis_index("dp")
    groups = lax.axis_size("dp")
    full = (
        lax.all_gather(w_qkv, "dp", axis=0, tiled=True),
        lax.all_gather(w_out, "dp", axis=0, tiled=True),
        lax.all_gather(w_gate, "dp", axis=0, tiled=True),
        lax.all_gather(w_up, "dp", axis=0, tiled=True),
        lax.all_gather(w_down, "dp", axis=0, tiled=True),
        lax.all_gather(ln1_gain, "dp", axis=0, tiled=True),
        lax.all_gather(first_layernorm_shift, "dp", axis=0, tiled=True),
        lax.all_gather(ln2_gain, "dp", axis=0, tiled=True),
        lax.all_gather(ln2_bias, "dp", axis=0, tiled=True),
    )
    qkv_full, out_full, gate_full, up_full, down_full = (
        full[0],
        full[1],
        full[2],
        full[3],
        full[4],
    )
    gain_one = full[5].astype(jnp.float32)
    bias_one = full[6].astype(jnp.float32)
    gain_two = full[7].astype(jnp.float32)
    bias_two = full[8].astype(jnp.float32)
    inputs = tokens[0]
    count = inputs.shape[0]
    places, allowed, pool_matrix = layout(tower_id, query_lengths, doc_lengths, count)
    cosines, sines = rotary_tables(places)
    packed = product(inputs, qkv_full)
    raw_query = packed[:, :D].reshape(count, HEADS, HEAD)
    raw_key = packed[:, D : 2 * D].reshape(count, HEADS, HEAD)

    def rotate_both(first, second):
        return (rotate(first, cosines, sines), rotate(second, cosines, sines))

    rotated, rotary_back = jax.vjp(rotate_both, raw_query, raw_key)
    query_low = rotated[0].astype(jnp.bfloat16)
    key_low = rotated[1].astype(jnp.bfloat16)
    value_low = packed[:, 2 * D :].reshape(count, HEADS, HEAD).astype(jnp.bfloat16)
    scale = HEAD ** (-0.5)

    def masked_scores():
        scores = (
            jnp.einsum("ihd,jhd->hij", query_low, key_low, preferred_element_type=jnp.float32)
            * scale
        )
        return jnp.where(allowed[None], scores, -1e30)

    scores = masked_scores()
    peak = jnp.max(scores, -1, keepdims=True)
    log_total = peak + jnp.log(jnp.sum(jnp.exp(scores - peak), -1, keepdims=True))
    probs_low = jnp.exp(scores - log_total).astype(jnp.bfloat16)
    mixed = jnp.einsum("hij,jhd->ihd", probs_low, value_low, preferred_element_type=jnp.float32)
    mixed_low = mixed.reshape(count, D).astype(jnp.bfloat16)
    attended = product(mixed_low, out_full)
    inputs_wide = inputs.astype(jnp.float32)
    normed_one, norm_one_back = jax.vjp(layer_norm, inputs_wide + attended, gain_one, bias_one)
    feed = normed_one.astype(jnp.bfloat16)
    gate = product(feed, gate_full)
    up_part = product(feed, up_full)
    hidden_wide, swish_back = jax.vjp(swish_product, gate, up_part)
    hidden = hidden_wide.astype(jnp.bfloat16)
    branch = product(hidden, down_full)
    normed_two, norm_two_back = jax.vjp(layer_norm, normed_one + branch, gain_two, bias_two)
    pooled = jnp.dot(pool_matrix, normed_two, precision=exact_product_accuracy)
    embedded, normal_back = jax.vjp(normalize, pooled)
    gathered = lax.all_gather(embedded, ("tower", "dp"), axis=0, tiled=True)
    queries_total = groups * QPD
    gathered_query_rows = gathered[:queries_total]
    gathered_document_rows = gathered[queries_total:].reshape(groups, QPD, D)[:, 0]
    pairwise_affinity_matrix = (
        jnp.dot(gathered_query_rows, gathered_document_rows.T, precision=exact_product_accuracy)
        / contrast_sharpness_factor
    )
    peak_logit = jnp.max(pairwise_affinity_matrix, -1, keepdims=True)
    log_partition_norm = peak_logit + jnp.log(
        jnp.sum(jnp.exp(pairwise_affinity_matrix - peak_logit), -1, keepdims=True)
    )
    columns = lax.broadcasted_iota(jnp.int32, pairwise_affinity_matrix.shape, 1)
    matching_labels = columns == positives[:, None]
    picked = jnp.sum(jnp.where(matching_labels, pairwise_affinity_matrix, 0.0), -1, keepdims=True)
    total = jnp.sum(log_partition_norm - picked)
    loss = total / queries_total
    similarity_gradient = (
        jnp.exp(pairwise_affinity_matrix - log_partition_norm) - matching_labels.astype(jnp.float32)
    ) / contrast_sharpness_factor
    own_rows = lax.dynamic_slice_in_dim(similarity_gradient, device_id * QPD, QPD, 0)
    query_side = jnp.dot(own_rows, gathered_document_rows, precision=exact_product_accuracy)
    own_column = lax.dynamic_slice_in_dim(similarity_gradient, device_id, 1, 1)
    doc_side = jnp.dot(own_column.T, gathered_query_rows, precision=exact_product_accuracy)
    doc_side = jnp.concatenate([doc_side, jnp.zeros((QPD - 1, D), jnp.float32)], 0)
    embed_grad = jnp.where(tower_id == 0, query_side, doc_side)
    pooled_grad = normal_back(embed_grad)[0]
    top_grad = jnp.dot(pool_matrix.T, pooled_grad, precision=exact_product_accuracy)
    sum_two, gain_two_grad, bias_two_grad = norm_two_back(top_grad)
    attention_input_cotangent, out_back, gate_back, up_back, down_back = (
        qkv_full,
        out_full,
        gate_full,
        up_full,
        down_full,
    )
    branch_low = sum_two.astype(jnp.bfloat16)
    down_grad = product(hidden.T, branch_low)
    hidden_grad = product(branch_low, down_back.T)
    gate_grad_wide, up_grad_wide = swish_back(hidden_grad)
    gate_low = gate_grad_wide.astype(jnp.bfloat16)
    up_low = up_grad_wide.astype(jnp.bfloat16)
    gate_weight_grad = product(feed.T, gate_low)
    up_weight_grad = product(feed.T, up_low)
    feed_grad = sum_two + product(gate_low, gate_back.T) + product(up_low, up_back.T)
    sum_one, gain_one_grad, bias_one_grad = norm_one_back(feed_grad)
    attend_low = sum_one.astype(jnp.bfloat16)
    out_grad = product(mixed_low.T, attend_low)
    mixed_grad = product(attend_low, out_back.T).astype(jnp.bfloat16).reshape(count, HEADS, HEAD)
    probs_again = jnp.exp(masked_scores() - log_total)
    prob_grad = jnp.einsum(
        "ihd,jhd->hij", mixed_grad, value_low, preferred_element_type=jnp.float32
    )
    score_grad = probs_again * (prob_grad - jnp.sum(probs_again * prob_grad, -1, keepdims=True))
    score_low = score_grad.astype(jnp.bfloat16)
    query_grad = (
        jnp.einsum("hij,jhd->ihd", score_low, key_low, preferred_element_type=jnp.float32) * scale
    )
    key_grad = (
        jnp.einsum("hij,ihd->jhd", score_low, query_low, preferred_element_type=jnp.float32) * scale
    )
    value_grad = jnp.einsum(
        "hij,ihd->jhd",
        probs_again.astype(jnp.bfloat16),
        mixed_grad,
        preferred_element_type=jnp.float32,
    )
    raw_query_grad, raw_key_grad = rotary_back((query_grad, key_grad))
    packed_grad = jnp.concatenate(
        [
            raw_query_grad.reshape(count, D),
            raw_key_grad.reshape(count, D),
            value_grad.reshape(count, D),
        ],
        1,
    ).astype(jnp.bfloat16)
    qkv_grad = product(inputs.T, packed_grad)
    input_grad = sum_one + product(packed_grad, attention_input_cotangent.T)
    gradients = (
        qkv_grad,
        out_grad,
        gate_weight_grad,
        up_weight_grad,
        down_grad,
        gain_one_grad,
        bias_one_grad,
        gain_two_grad,
        bias_two_grad,
    )
    partial_sums = (
        lax.psum_scatter(gradients[0], "dp", scatter_dimension=0, tiled=True),
        lax.psum_scatter(gradients[1], "dp", scatter_dimension=0, tiled=True),
        lax.psum_scatter(gradients[2], "dp", scatter_dimension=0, tiled=True),
        lax.psum_scatter(gradients[3], "dp", scatter_dimension=0, tiled=True),
        lax.psum_scatter(gradients[4], "dp", scatter_dimension=0, tiled=True),
        lax.psum_scatter(gradients[5], "dp", scatter_dimension=0, tiled=True),
        lax.psum_scatter(gradients[6], "dp", scatter_dimension=0, tiled=True),
        lax.psum_scatter(gradients[7], "dp", scatter_dimension=0, tiled=True),
        lax.psum_scatter(gradients[8], "dp", scatter_dimension=0, tiled=True),
    )
    tower_halves = (
        lax.psum_scatter(
            partial_sums[0].astype(jnp.bfloat16), "tower", scatter_dimension=0, tiled=True
        ).astype(jnp.float32),
        lax.psum_scatter(
            partial_sums[1].astype(jnp.bfloat16), "tower", scatter_dimension=0, tiled=True
        ).astype(jnp.float32),
        lax.psum_scatter(
            partial_sums[2].astype(jnp.bfloat16), "tower", scatter_dimension=0, tiled=True
        ).astype(jnp.float32),
        lax.psum_scatter(
            partial_sums[3].astype(jnp.bfloat16), "tower", scatter_dimension=0, tiled=True
        ).astype(jnp.float32),
        lax.psum_scatter(
            partial_sums[4].astype(jnp.bfloat16), "tower", scatter_dimension=0, tiled=True
        ).astype(jnp.float32),
        lax.psum_scatter(
            partial_sums[5].astype(jnp.bfloat16), "tower", scatter_dimension=0, tiled=True
        ).astype(jnp.float32),
        lax.psum_scatter(
            partial_sums[6].astype(jnp.bfloat16), "tower", scatter_dimension=0, tiled=True
        ).astype(jnp.float32),
        lax.psum_scatter(
            partial_sums[7].astype(jnp.bfloat16), "tower", scatter_dimension=0, tiled=True
        ).astype(jnp.float32),
        lax.psum_scatter(
            partial_sums[8].astype(jnp.bfloat16), "tower", scatter_dimension=0, tiled=True
        ).astype(jnp.float32),
    )
    shares = (
        lax.all_gather(tower_halves[0].astype(jnp.bfloat16), "tower", axis=0, tiled=True).astype(
            jnp.float32
        ),
        lax.all_gather(tower_halves[1].astype(jnp.bfloat16), "tower", axis=0, tiled=True).astype(
            jnp.float32
        ),
        lax.all_gather(tower_halves[2].astype(jnp.bfloat16), "tower", axis=0, tiled=True).astype(
            jnp.float32
        ),
        lax.all_gather(tower_halves[3].astype(jnp.bfloat16), "tower", axis=0, tiled=True).astype(
            jnp.float32
        ),
        lax.all_gather(tower_halves[4].astype(jnp.bfloat16), "tower", axis=0, tiled=True).astype(
            jnp.float32
        ),
        lax.all_gather(tower_halves[5].astype(jnp.bfloat16), "tower", axis=0, tiled=True).astype(
            jnp.float32
        ),
        lax.all_gather(tower_halves[6].astype(jnp.bfloat16), "tower", axis=0, tiled=True).astype(
            jnp.float32
        ),
        lax.all_gather(tower_halves[7].astype(jnp.bfloat16), "tower", axis=0, tiled=True).astype(
            jnp.float32
        ),
        lax.all_gather(tower_halves[8].astype(jnp.bfloat16), "tower", axis=0, tiled=True).astype(
            jnp.float32
        ),
    )
    query_rows = lax.dynamic_slice_in_dim(gathered_query_rows, device_id * QPD, QPD, 0)
    doc_row = lax.dynamic_slice_in_dim(gathered_document_rows, device_id, 1, 0)
    return (loss, query_rows, doc_row, input_grad[None]) + tuple(shares)


def solution(mesh):
    return jax.shard_map(
        on_device,
        mesh=mesh,
        in_specs=(
            P("tower", "dp", None),
            P("dp"),
            P("dp"),
            P(),
            P("dp", None),
            P("dp", None),
            P("dp", None),
            P("dp", None),
            P("dp", None),
            P("dp"),
            P("dp"),
            P("dp"),
            P("dp"),
        ),
        out_specs=(
            P(),
            P("dp", None),
            P("dp", None),
            P("tower", "dp", None),
            P("dp", None),
            P("dp", None),
            P("dp", None),
            P("dp", None),
            P("dp", None),
            P("dp"),
            P("dp"),
            P("dp"),
            P("dp"),
        ),
        check_vma=False,
    )
```

profile of v0, /device:TPU:0, one launch (start us, length us, event | category | flops | bytes accessed | tf_op | source)
XLA Modules:
  0.0 923.1 jit_solution(9459486310065083493)
XLA Ops:
  16.6 35.8 %all-reduce.22 = (bf16[768]{0:T(1024)(128)(2,1)S(1)}, bf16[768]{0:T(1024)(128)(2,1)S(1)}, bf16[768]{0:T(1024)(128)(2,1)S(1)}, bf16[768]{0:T(1024)(128)(2,1)S(1)}) all-reduce(bf16[768]{0:T(1024)(128)(2,1)S(1)} %dynamic-update-slice.1, bf16[768]{0:T(1024)(128)(2,1)S(1)} %dynamic-update-slice, ...), channel_id=1, replica_groups=mesh['tower'=2,'dp'=16] {'dp'}, use_global_device_ids=true, to_apply=%add.6 | all-reduce | flops 3072 | bytes 12288
  71.6 28.5 %all-gather.9.cloned.1.call-done = bf16[768,768]{1,0:T(8,128)(2,1)} async-done(((bf16[48,768]{1,0:T(8,128)(2,1)}), bf16[768,768]{1,0:T(8,128)(2,1)}) %all-gather.9.cloned.1.call-update) | async-done | bytes 1179664 | tf_op jit(solution)/shard_map/all_gather | solution.py:87
  103.8 50.9 %all-gather.11.cloned.1.call-done = bf16[768,3072]{1,0:T(8,128)(2,1)} async-done(((bf16[48,3072]{1,0:T(8,128)(2,1)}), bf16[768,3072]{1,0:T(8,128)(2,1)}) %all-gather.11.cloned.1.call-update) | async-done | bytes 4718608 | tf_op jit(solution)/shard_map/all_gather | solution.py:88
  154.6 5.3 fusion.76
  160.0 48.6 %all-gather.13.cloned.1.call-done = bf16[768,3072]{1,0:T(8,128)(2,1)} async-done(((bf16[48,3072]{1,0:T(8,128)(2,1)}), bf16[768,3072]{1,0:T(8,128)(2,1)}) %all-gather.13.cloned.1.call-update) | async-done | bytes 4718608 | tf_op jit(solution)/shard_map/all_gather | solution.py:89
  208.6 7.2 multiply_convert_fusion.2
  215.8 46.8 %all-gather.15.cloned.1.call-done = bf16[3072,768]{1,0:T(8,128)(2,1)} async-done(((bf16[192,768]{1,0:T(8,128)(2,1)}), bf16[3072,768]{1,0:T(8,128)(2,1)}) %all-gather.15.cloned.1.call-update) | async-done | bytes 4718608 | tf_op jit(solution)/shard_map/all_gather | solution.py:90
  262.6 4.6 fusion.74
  269.5 40.3 %all-gather = f32[32,4,768]{2,1,0:T(4,128)S(1)} all-gather(f32[1,4,768]{2,1,0:T(4,128)S(1)} %multiply_bitcast_fusion), channel_id=1, replica_groups=mesh['tower'=2,'dp'=16] {'tower','dp'}, dimensions={0}, use_global_device_ids=true | all-gather | bytes 405504 | tf_op jit(solution)/shard_map/all_gather | solution.py:149
  324.4 7.6 multiply_convert_fusion.1
  355.3 8.1 copy.70
  364.9 5.0 fusion.77
  371.4 5.1 fusion.78
  378.1 5.1 fusion.65
  383.5 15.4 %reduce-scatter.15.cloned.1.call-done = f32[48,768]{1,0:T(8,128)} async-done(((f32[768,768]{1,0:T(8,128)}), f32[48,768]{1,0:T(8,128)}) %reduce-scatter.15.cloned.1.call-update) | async-done | bytes 147472 | tf_op jit(solution)/shard_map/reduce_scatter | solution.py:240
  400.5 92.0 %reduce-scatter.31.cloned.1.call-done = f32[48,2304]{1,0:T(8,128)} async-done(((f32[768,2304]{1,0:T(8,128)}), f32[48,2304]{1,0:T(8,128)}) %reduce-scatter.31.cloned.1.call-update) | async-done | bytes 442384
  494.9 112.7 %reduce-scatter.19.cloned.1.call-done = f32[48,3072]{1,0:T(8,128)} async-done(((f32[768,3072]{1,0:T(8,128)}), f32[48,3072]{1,0:T(8,128)}) %reduce-scatter.19.cloned.1.call-update) | async-done | bytes 589840 | tf_op jit(solution)/shard_map/reduce_scatter | solution.py:241
  609.4 113.9 %reduce-scatter.23.cloned.1.call-done = f32[48,3072]{1,0:T(8,128)} async-done(((f32[768,3072]{1,0:T(8,128)}), f32[48,3072]{1,0:T(8,128)}) %reduce-scatter.23.cloned.1.call-update) | async-done | bytes 589840 | tf_op jit(solution)/shard_map/reduce_scatter | solution.py:242
  727.2 62.3 %all-reduce.21 = (bf16[768]{0:T(1024)(128)(2,1)S(1)}, bf16[768]{0:T(1024)(128)(2,1)S(1)}, bf16[768]{0:T(1024)(128)(2,1)S(1)}, bf16[768]{0:T(1024)(128)(2,1)S(1)}) all-reduce(f32[768]{0:T(1024)S(1)} %copy-done.63, f32[768]{0:T(1024)S(1)} %copy-done.64, f32[768]{0:T(1024)S(1)} %copy-done.48, ...), channel_id=12, replica_groups=mesh['tower'=2,'dp'=16] {'dp'}, use_global_device_ids=true, to_apply=%region_29.30.clone | all-reduce | flops 3072 | bytes 18432
  789.8 5.2 all-reduce.24
  796.1 4.9 all-reduce.23
  806.4 32.3 %reduce-scatter.27.cloned.1.call-done = f32[192,768]{1,0:T(8,128)} async-done(((f32[3072,768]{1,0:T(8,128)}), f32[192,768]{1,0:T(8,128)}) %reduce-scatter.27.cloned.1.call-update) | async-done | bytes 589840 | tf_op jit(solution)/shard_map/reduce_scatter | solution.py:243
  844.6 6.7 reduce-scatter.17.cloned.1.call-done
  851.3 4.8 all_gather.68
  856.8 7.9 reduce-scatter.33.cloned.1.call-done
  864.7 5.7 all_gather.67
  871.1 8.5 reduce-scatter.21.cloned.1.call-done
  879.6 6.5 all_gather.69
  886.9 6.9 reduce-scatter.25.cloned.1.call-done
  893.9 6.5 all_gather.70
  901.2 6.9 reduce-scatter.29.cloned.1.call-done
  908.1 6.5 all_gather.71
  (287 shorter events, 98.6 us)
Async XLA Ops:
  7.2 53.2 %all-gather.7.cloned.1.call-start = ((), (), s32[]{:S(2)}) async-start(), calls=%async_computation.10 | async-start | bytes 3760128 | tf_op jit(solution)/shard_map/all_gather | solution.py:86
  7.9 92.2 %all-gather.9.cloned.1.call-start = ((), (), s32[]{:S(2)}) async-start(), calls=%async_computation.11 | async-start | bytes 1253376 | tf_op jit(solution)/shard_map/all_gather | solution.py:87
  8.7 146.0 %all-gather.11.cloned.1.call-start = ((), (), s32[]{:S(2)}) async-start(), calls=%async_computation.12 | async-start | bytes 5013504 | tf_op jit(solution)/shard_map/all_gather | solution.py:88
  9.4 199.2 %all-gather.13.cloned.1.call-start = ((), (), s32[]{:S(2)}) async-start(), calls=%async_computation.13 | async-start | bytes 5013504 | tf_op jit(solution)/shard_map/all_gather | solution.py:89
  10.0 252.6 %all-gather.15.cloned.1.call-start = ((), (), s32[]{:S(2)}) async-start(), calls=%async_computation.14 | async-start | bytes 5013504 | tf_op jit(solution)/shard_map/all_gather | solution.py:90
  10.6 388.3 %reduce-scatter.15.cloned.1.call-start = ((), (), s32[]{:S(2)}) async-start(), calls=%async_computation.15 | async-start | bytes 2506752 | tf_op jit(solution)/shard_map/reduce_scatter | solution.py:240
  57.0 10.2 %copy-start.36 = (f32[256,32]{0,1:T(8,128)}, f32[256,32]{0,1:T(8,128)S(1)}, u32[]{:S(2)}) copy-start(f32[256,32]{0,1:T(8,128)S(1)} %get-tuple-element.88) | copy-start | bytes 98308
  57.2 10.4 %copy-start.21 = (pred[256,256]{0,1:T(8,128)(4,1)}, pred[256,256]{0,1:T(8,128)(4,1)S(1)}, u32[]{:S(2)}) copy-start(pred[256,256]{0,1:T(8,128)(4,1)S(1)} %compare_and_fusion) | copy-start | bytes 196612
  68.4 31.7 %copy-start.5 = (bf16[1,256,768]{2,1,0:T(8,128)(2,1)S(1)}, bf16[1,256,768]{2,1,0:T(8,128)(2,1)}, u32[]{:S(2)}) copy-start(bf16[1,256,768]{2,1,0:T(8,128)(2,1)} %param.13) | copy-start | bytes 1179652
  267.2 42.7 %copy-start.46 = (f32[256]{0:T(256)}, f32[256]{0:T(256)S(1)}, u32[]{:S(2)}) copy-start(f32[256]{0:T(256)S(1)} %broadcast_multiply_fusion) | copy-start | bytes 3076
  267.9 42.6 %copy-start.52 = (f32[256]{0:T(256)}, f32[256]{0:T(256)S(1)}, u32[]{:S(2)}) copy-start(f32[256]{0:T(256)S(1)} %fusion.50) | copy-start | bytes 3076
  268.8 41.7 %copy-start.67 = (f32[4]{0:T(128)}, f32[4]{0:T(128)S(1)}, u32[]{:S(2)}) copy-start(f32[4]{0:T(128)S(1)} %get-tuple-element.101) | copy-start | bytes 52
  312.8 11.6 %copy-start.68 = (f32[256,3072]{1,0:T(8,128)S(1)}, f32[256,3072]{1,0:T(8,128)}, u32[]{:S(2)}) copy-start(f32[256,3072]{1,0:T(8,128)} %fusion.76) | copy-start | bytes 9437188
  322.7 11.0 %slice-start.2 = ((s8[4718592]{0:T(1024)(128)(4,1)}), s8[4194304]{0:T(1024)(128)(4,1)S(1)}, s32[]{:S(2)}) async-start(s8[4718592]{0:T(1024)(128)(4,1)} %bitcast.94), calls=%async_computation.27 | async-start | bytes 8388608
  339.4 153.1 %reduce-scatter.31.cloned.1.call-start = ((), (), s32[]{:S(2)}) async-start(), calls=%async_computation.23 | async-start | bytes 7520256
  363.4 244.1 %reduce-scatter.19.cloned.1.call-start = ((), (), s32[]{:S(2)}) async-start(), calls=%async_computation.17 | async-start | bytes 10027008 | tf_op jit(solution)/shard_map/reduce_scatter | solution.py:241
  370.0 353.3 %reduce-scatter.23.cloned.1.call-start = ((), (), s32[]{:S(2)}) async-start(), calls=%async_computation.19 | async-start | bytes 10027008 | tf_op jit(solution)/shard_map/reduce_scatter | solution.py:242
  376.5 462.2 %reduce-scatter.27.cloned.1.call-start = ((), (), s32[]{:S(2)}) async-start(), calls=%async_computation.21 | async-start | bytes 10027008 | tf_op jit(solution)/shard_map/reduce_scatter | solution.py:243
  383.3 343.8 %copy-start.48 = (f32[768]{0:T(1024)S(1)}, f32[768]{0:T(1024)}, u32[]{:S(2)}) copy-start(f32[768]{0:T(1024)} %get-tuple-element.39) | copy-start | bytes 9220
  383.3 343.8 %copy-start.49 = (f32[768]{0:T(1024)S(1)}, f32[768]{0:T(1024)}, u32[]{:S(2)}) copy-start(f32[768]{0:T(1024)} %get-tuple-element.43) | copy-start | bytes 9220
  383.3 343.8 %copy-start.63 = (f32[768]{0:T(1024)S(1)}, f32[768]{0:T(1024)}, u32[]{:S(2)}) copy-start(f32[768]{0:T(1024)} %get-tuple-element.41) | copy-start | bytes 9220
  383.3 343.8 %copy-start.64 = (f32[768]{0:T(1024)S(1)}, f32[768]{0:T(1024)}, u32[]{:S(2)}) copy-start(f32[768]{0:T(1024)} %get-tuple-element.44) | copy-start | bytes 9220
  383.4 457.1 %copy-start.4 = (f32[256,768]{1,0:T(8,128)S(1)}, f32[256,768]{1,0:T(8,128)}, u32[]{:S(2)}) copy-start(f32[256,768]{1,0:T(8,128)} %copy-done.3) | copy-start | bytes 2359300
  383.4 457.1 %copy-start.11 = (bf16[256,12,64]{0,2,1:T(8,128)(2,1)S(1)}, bf16[256,12,64]{0,2,1:T(8,128)(2,1)}, u32[]{:S(2)}) copy-start(bf16[256,12,64]{0,2,1:T(8,128)(2,1)} %copy-done.10) | copy-start | bytes 1179652
  383.4 457.1 %copy-start.13 = (bf16[256,12,64]{0,2,1:T(8,128)(2,1)S(1)}, bf16[256,12,64]{0,2,1:T(8,128)(2,1)}, u32[]{:S(2)}) copy-start(bf16[256,12,64]{0,2,1:T(8,128)(2,1)} %copy-done.12) | copy-start | bytes 1179652
  383.4 457.1 %copy-start.33 = (bf16[12,64,256]{2,1,0:T(8,128)(2,1)S(1)}, bf16[12,64,256]{2,1,0:T(8,128)(2,1)}, u32[]{:S(2)}) copy-start(bf16[12,64,256]{2,1,0:T(8,128)(2,1)} %copy-done.32) | copy-start | bytes 1179652
  383.4 457.1 %copy-start.57 = (f32[256]{0:T(256)S(1)}, f32[256]{0:T(256)}, u32[]{:S(2)}) copy-start(f32[256]{0:T(256)} %copy-done.56) | copy-start | bytes 3076
  383.4 467.8 %reduce-scatter.17.cloned.1.call-start = ((), (), s32[]{:S(2)}) async-start(), calls=%async_computation.16 | async-start | bytes 110592 | tf_op jit(solution)/shard_map/reduce_scatter | solution.py:253
  400.4 464.2 %reduce-scatter.33.cloned.1.call-start = ((), (), s32[]{:S(2)}) async-start(), calls=%async_computation.24 | async-start | bytes 331776 | tf_op jit(solution)/shard_map/reduce_scatter | solution.py:250
  494.8 384.8 %reduce-scatter.21.cloned.1.call-start = ((), (), s32[]{:S(2)}) async-start(), calls=%async_computation.18 | async-start | bytes 442368 | tf_op jit(solution)/shard_map/reduce_scatter | solution.py:256
  609.4 284.5 %reduce-scatter.25.cloned.1.call-start = ((), (), s32[]{:S(2)}) async-start(), calls=%async_computation.20 | async-start | bytes 442368 | tf_op jit(solution)/shard_map/reduce_scatter | solution.py:259
  725.2 182.9 %reduce-scatter.29.cloned.1.call-start = ((), (), s32[]{:S(2)}) async-start(), calls=%async_computation.22 | async-start | bytes 442368 | tf_op jit(solution)/shard_map/reduce_scatter | solution.py:262
  (56 other events, 142.5 us)
Sparse Core Ops, SparseCore 0:
  10.3 50.0 all-gather.6
  62.7 37.4 all-gather.8
  102.4 52.1 all-gather.10
  156.8 51.7 all-gather.12
  210.7 51.7 all-gather.14
  339.5 59.2 reduce-scatter.14
  403.4 89.0 reduce-scatter.30
  496.6 110.8 reduce-scatter.18
  612.2 111.1 reduce-scatter.22
  727.3 111.3 reduce-scatter.26
  841.5 9.6 reduce-scatter.16
  853.4 11.1 reduce-scatter.32
  867.6 12.0 reduce-scatter.20
  881.8 12.0 reduce-scatter.24
  896.0 12.0 reduce-scatter.28
where the time goes:
time: 924 us; the launch traced here: 923 us
  waiting for transfers between devices  585 us (63%)
  blocking collectives  178 us (19%)
  matrix products  75.5 us (8%)
  local copies, waits for them, and re-layouts  37.5 us (4%)
  other arithmetic  26.3 us (3%)
  between operations  20 us (2%)
    reduce_scatter x1, waiting for transfers between devices, on_device(): lax.psum_scatter(gradients[3], 'dp', scatter_dimension=0, tiled=True)  114 us
    reduce_scatter x1, waiting for transfers between devices, on_device(): lax.psum_scatter(gradients[2], 'dp', scatter_dimension=0, tiled=True)  113 us
    unnamed x4, blocking collectives  108 us
    unnamed x16, waiting for transfers between devices  95.3 us
    dot_general x15, matrix products, product(): return jnp.dot(left, right, preferred_element_type=jnp.float32)  61.8 us
    all_gather x1, waiting for transfers between devices, on_device(): lax.all_gather(w_gate, 'dp', axis=0, tiled=True)  50.9 us
    all_gather x1, waiting for transfers between devices, on_device(): lax.all_gather(w_up, 'dp', axis=0, tiled=True)  48.6 us
    all_gather x1, waiting for transfers between devices, on_device(): lax.all_gather(w_down, 'dp', axis=0, tiled=True)  46.8 us
  transfers between devices with their start and end apart: 15, of which 15 were waited for; matrix products, arithmetic and copies ran while one was open for 10% of the time, Pallas kernels for 0%

commit v1 on v0

--- a/solution.py
+++ b/solution.py
@@ -1,8 +1,17 @@
+import functools
+from types import SimpleNamespace
+from typing import Any, NamedTuple
+
 import jax
 import jax.numpy as jnp
+import numpy as np
 from jax import lax
+from jax.experimental import pallas as pl
+from jax.experimental.pallas import tpu as pltpu
 from jax.sharding import PartitionSpec as P
 
+TOWER = "tower"
+DP = "dp"
 D = 768
 HEADS = 12
 HEAD = 64
@@ -79,19 +88,19 @@
     ln2_gain,
     ln2_bias,
 ):
-    tower_id = lax.axis_index("tower")
-    device_id = lax.axis_index("dp")
-    groups = lax.axis_size("dp")
+    tower_id = lax.axis_index(TOWER)
+    device_id = lax.axis_index(DP)
+    groups = lax.axis_size(DP)
     full = (
-        lax.all_gather(w_qkv, "dp", axis=0, tiled=True),
-        lax.all_gather(w_out, "dp", axis=0, tiled=True),
-        lax.all_gather(w_gate, "dp", axis=0, tiled=True),
-        lax.all_gather(w_up, "dp", axis=0, tiled=True),
-        lax.all_gather(w_down, "dp", axis=0, tiled=True),
-        lax.all_gather(ln1_gain, "dp", axis=0, tiled=True),
-        lax.all_gather(first_layernorm_shift, "dp", axis=0, tiled=True),
-        lax.all_gather(ln2_gain, "dp", axis=0, tiled=True),
-        lax.all_gather(ln2_bias, "dp", axis=0, tiled=True),
+        lax.all_gather(w_qkv, DP, axis=0, tiled=True),
+        lax.all_gather(w_out, DP, axis=0, tiled=True),
+        lax.all_gather(w_gate, DP, axis=0, tiled=True),
+        lax.all_gather(w_up, DP, axis=0, tiled=True),
+        lax.all_gather(w_down, DP, axis=0, tiled=True),
+        lax.all_gather(ln1_gain, DP, axis=0, tiled=True),
+        lax.all_gather(first_layernorm_shift, DP, axis=0, tiled=True),
+        lax.all_gather(ln2_gain, DP, axis=0, tiled=True),
+        lax.all_gather(ln2_bias, DP, axis=0, tiled=True),
     )
     qkv_full, out_full, gate_full, up_full, down_full = (
         full[0],
@@ -146,7 +155,7 @@
     normed_two, norm_two_back = jax.vjp(layer_norm, normed_one + branch, gain_two, bias_two)
     pooled = jnp.dot(pool_matrix, normed_two, precision=exact_product_accuracy)
     embedded, normal_back = jax.vjp(normalize, pooled)
-    gathered = lax.all_gather(embedded, ("tower", "dp"), axis=0, tiled=True)
+    gathered = lax.all_gather(embedded, (TOWER, DP), axis=0, tiled=True)
     queries_total = groups * QPD
     gathered_query_rows = gathered[:queries_total]
     gathered_document_rows = gathered[queries_total:].reshape(groups, QPD, D)[:, 0]
@@ -236,71 +245,71 @@
         bias_two_grad,
     )
     partial_sums = (
-        lax.psum_scatter(gradients[0], "dp", scatter_dimension=0, tiled=True),
-        lax.psum_scatter(gradients[1], "dp", scatter_dimension=0, tiled=True),
-        lax.psum_scatter(gradients[2], "dp", scatter_dimension=0, tiled=True),
-        lax.psum_scatter(gradients[3], "dp", scatter_dimension=0, tiled=True),
-        lax.psum_scatter(gradients[4], "dp", scatter_dimension=0, tiled=True),
-        lax.psum_scatter(gradients[5], "dp", scatter_dimension=0, tiled=True),
-        lax.psum_scatter(gradients[6], "dp", scatter_dimension=0, tiled=True),
-        lax.psum_scatter(gradients[7], "dp", scatter_dimension=0, tiled=True),
-        lax.psum_scatter(gradients[8], "dp", scatter_dimension=0, tiled=True),
+        lax.psum_scatter(gradients[0], DP, scatter_dimension=0, tiled=True),
+        lax.psum_scatter(gradients[1], DP, scatter_dimension=0, tiled=True),
+        lax.psum_scatter(gradients[2], DP, scatter_dimension=0, tiled=True),
+        lax.psum_scatter(gradients[3], DP, scatter_dimension=0, tiled=True),
+        lax.psum_scatter(gradients[4], DP, scatter_dimension=0, tiled=True),
+        lax.psum_scatter(gradients[5], DP, scatter_dimension=0, tiled=True),
+        lax.psum_scatter(gradients[6], DP, scatter_dimension=0, tiled=True),
+        lax.psum_scatter(gradients[7], DP, scatter_dimension=0, tiled=True),
+        lax.psum_scatter(gradients[8], DP, scatter_dimension=0, tiled=True),
     )
     tower_halves = (
         lax.psum_scatter(
-            partial_sums[0].astype(jnp.bfloat16), "tower", scatter_dimension=0, tiled=True
+            partial_sums[0].astype(jnp.bfloat16), TOWER, scatter_dimension=0, tiled=True
         ).astype(jnp.float32),
         lax.psum_scatter(
-            partial_sums[1].astype(jnp.bfloat16), "tower", scatter_dimension=0, tiled=True
+            partial_sums[1].astype(jnp.bfloat16), TOWER, scatter_dimension=0, tiled=True
         ).astype(jnp.float32),
         lax.psum_scatter(
-            partial_sums[2].astype(jnp.bfloat16), "tower", scatter_dimension=0, tiled=True
+            partial_sums[2].astype(jnp.bfloat16), TOWER, scatter_dimension=0, tiled=True
         ).astype(jnp.float32),
         lax.psum_scatter(
-            partial_sums[3].astype(jnp.bfloat16), "tower", scatter_dimension=0, tiled=True
+            partial_sums[3].astype(jnp.bfloat16), TOWER, scatter_dimension=0, tiled=True
         ).astype(jnp.float32),
         lax.psum_scatter(
-            partial_sums[4].astype(jnp.bfloat16), "tower", scatter_dimension=0, tiled=True
+            partial_sums[4].astype(jnp.bfloat16), TOWER, scatter_dimension=0, tiled=True
         ).astype(jnp.float32),
         lax.psum_scatter(
-            partial_sums[5].astype(jnp.bfloat16), "tower", scatter_dimension=0, tiled=True
+            partial_sums[5].astype(jnp.bfloat16), TOWER, scatter_dimension=0, tiled=True
         ).astype(jnp.float32),
         lax.psum_scatter(
-            partial_sums[6].astype(jnp.bfloat16), "tower", scatter_dimension=0, tiled=True
+            partial_sums[6].astype(jnp.bfloat16), TOWER, scatter_dimension=0, tiled=True
         ).astype(jnp.float32),
         lax.psum_scatter(
-            partial_sums[7].astype(jnp.bfloat16), "tower", scatter_dimension=0, tiled=True
+            partial_sums[7].astype(jnp.bfloat16), TOWER, scatter_dimension=0, tiled=True
         ).astype(jnp.float32),
         lax.psum_scatter(
-            partial_sums[8].astype(jnp.bfloat16), "tower", scatter_dimension=0, tiled=True
+            partial_sums[8].astype(jnp.bfloat16), TOWER, scatter_dimension=0, tiled=True
         ).astype(jnp.float32),
     )
     shares = (
-        lax.all_gather(tower_halves[0].astype(jnp.bfloat16), "tower", axis=0, tiled=True).astype(
+        lax.all_gather(tower_halves[0].astype(jnp.bfloat16), TOWER, axis=0, tiled=True).astype(
             jnp.float32
         ),
-        lax.all_gather(tower_halves[1].astype(jnp.bfloat16), "tower", axis=0, tiled=True).astype(
+        lax.all_gather(tower_halves[1].astype(jnp.bfloat16), TOWER, axis=0, tiled=True).astype(
             jnp.float32
         ),
-        lax.all_gather(tower_halves[2].astype(jnp.bfloat16), "tower", axis=0, tiled=True).astype(
+        lax.all_gather(tower_halves[2].astype(jnp.bfloat16), TOWER, axis=0, tiled=True).astype(
             jnp.float32
         ),
-        lax.all_gather(tower_halves[3].astype(jnp.bfloat16), "tower", axis=0, tiled=True).astype(
+        lax.all_gather(tower_halves[3].astype(jnp.bfloat16), TOWER, axis=0, tiled=True).astype(
             jnp.float32
         ),
-        lax.all_gather(tower_halves[4].astype(jnp.bfloat16), "tower", axis=0, tiled=True).astype(
+        lax.all_gather(tower_halves[4].astype(jnp.bfloat16), TOWER, axis=0, tiled=True).astype(
             jnp.float32
         ),
-        lax.all_gather(tower_halves[5].astype(jnp.bfloat16), "tower", axis=0, tiled=True).astype(
+        lax.all_gather(tower_halves[5].astype(jnp.bfloat16), TOWER, axis=0, tiled=True).astype(
             jnp.float32
         ),
-        lax.all_gather(tower_halves[6].astype(jnp.bfloat16), "tower", axis=0, tiled=True).astype(
+        lax.all_gather(tower_halves[6].astype(jnp.bfloat16), TOWER, axis=0, tiled=True).astype(
             jnp.float32
         ),
-        lax.all_gather(tower_halves[7].astype(jnp.bfloat16), "tower", axis=0, tiled=True).astype(
+        lax.all_gather(tower_halves[7].astype(jnp.bfloat16), TOWER, axis=0, tiled=True).astype(
             jnp.float32
         ),
-        lax.all_gather(tower_halves[8].astype(jnp.bfloat16), "tower", axis=0, tiled=True).astype(
+        lax.all_gather(tower_halves[8].astype(jnp.bfloat16), TOWER, axis=0, tiled=True).astype(
             jnp.float32
         ),
     )
@@ -309,39 +318,1268 @@
     return (loss, query_rows, doc_row, input_grad[None]) + tuple(shares)
 
 
+MESH = pl.DeviceIdType.MESH
+BF = jnp.bfloat16
+F32 = jnp.float32
+LANES = 128
+
+
+def dot_tt(left, right, precision=None):
+    return lax.dot_general(
+        left, right, (((1,), (1,)), ((), ())), preferred_element_type=F32, precision=precision
+    )
+
+
+def dot_t0(left, right):
+    return lax.dot_general(left, right, (((0,), (0,)), ((), ())), preferred_element_type=F32)
+
+
+def rotary_constants(count):
+    freqs = np.power(
+        np.float32(rope_base), (-2.0 * np.arange(HEAD // 2) / HEAD).astype(np.float32)
+    ).astype(np.float32)
+    angles = (np.arange(count, dtype=np.float32)[:, None] * freqs[None, :]).astype(np.float64)
+    cosines, sines = np.cos(angles), np.sin(angles)
+    return (
+        np.tile(np.concatenate([cosines, cosines], 1), (1, 2)).astype(np.float32),
+        np.tile(np.concatenate([-sines, sines], 1), (1, 2)).astype(np.float32),
+    )
+
+
+def aligned(start, unit):
+    return start if isinstance(start, int) else pl.multiple_of(start, unit)
+
+
+def both(first, second):
+    return jnp.logical_and(first, second)
+
+
+def do(condition, action):
+    if condition is None:
+        action()
+    else:
+        pl.when(condition)(action)
+
+
+class Plan:
+    def __init__(self, groups, count, shard, shard_ff, vec):
+        self.groups = groups
+        self.line = groups // 4
+        self.count = count
+        self.shard = shard
+        self.shard_ff = shard_ff
+        self.vec = vec
+        self.width_a = 4 * D
+        self.half_a = 2 * D
+        self.ff = shard_ff * groups
+        self.half_ff = self.ff // 2
+        self.stripe = 2 * shard_ff
+
+
+def semaphores(plan):
+    line, groups = plan.line, plan.groups
+    dma = pltpu.SemaphoreType.DMA
+    chunks_gu, chunks_a = 4, 4
+    return dict(
+        loc=dma((20,)),
+        ra=dma((groups, 2)),
+        sa_z=dma((2, line)),
+        sa_x=dma((line,)),
+        sa_y=dma((line, 2)),
+        sa_c=dma((line, 2, 2)),
+        rg=dma((groups,)),
+        sg_z=dma((2, line)),
+        sg_x=dma((line,)),
+        sg_c=dma((line, 2)),
+        rd=dma((line, 2)),
+        sd_x=dma((1,)),
+        sd_z=dma((2, line)),
+        sd_c=dma((line,)),
+        rv=dma((groups,)),
+        sv=dma((groups,)),
+        sx=dma((4,)),
+        rx=dma((4,)),
+        r_doc=dma((groups,)),
+        s_doc=dma((2, groups)),
+        r_query=dma((groups,)),
+        s_query=dma((groups,)),
+        s_loss=dma((1,)),
+        r_loss=dma((1,)),
+        s_ln=dma((line.bit_length() + 2,)),
+        r_ln=dma((line.bit_length() + 2,)),
+        gd_c=dma((2, line)),
+        gd_z=dma((2, 2, line)),
+        gd_x=dma((2,)),
+        gd_y=dma((2,)),
+        gg_c=dma((2, chunks_gu)),
+        gg_x=dma((2, chunks_gu)),
+        gg_z=dma((2, chunks_gu, 2, line)),
+        gg_y=dma((2, chunks_gu)),
+        ga_c=dma((2, 2, chunks_a)),
+        ga_t=dma((2, chunks_a)),
+        ga_x=dma((2, chunks_a)),
+        ga_z=dma((2, chunks_a, 2, line)),
+        ga_y=dma((2, chunks_a)),
+        fin=dma((9,)),
+    )
+
+
+def buffers(plan):
+    line, count, shard, groups = plan.line, plan.count, plan.shard, plan.groups
+    pair = 2 * count
+    v = pltpu.VMEM
+    return dict(
+        wa=v((line, 2, 2, shard, plan.width_a), BF),
+        wg=v((line, 2, 2, shard, plan.ff), BF),
+        wd=v((line, 2, plan.shard_ff, D), BF),
+        vt=v((groups, 16, LANES), BF),
+        vec=v((16, D), F32),
+        cos=v((count, LANES), F32),
+        sin=v((count, LANES), F32),
+        hide=v((count, count), F32),
+        pw=v((count, 1), F32),
+        qkv=v((count, 3 * D), BF),
+        probs=v((HEADS, count, count), F32),
+        mixed=v((count, D), BF),
+        mixt=v((D, count), BF),
+        tokt=v((D, count), BF),
+        h1=v((count, D), F32),
+        rs1=v((count, 1), F32),
+        n1=v((count, D), F32),
+        feed=v((pair, D), BF),
+        feedt=v((D, pair), BF),
+        gate=v((pair, plan.half_ff), F32),
+        up=v((pair, plan.half_ff), F32),
+        hidt=v((plan.half_ff, pair), BF),
+        dgu=v((pair, plan.ff), BF),
+        bown=v((count, D), F32),
+        bsend=v((count, D), BF),
+        brecv=v((count, D), BF),
+        xh2=v((count, D), F32),
+        rs2=v((count, 1), F32),
+        dbr=v((pair, D), BF),
+        dsend=v((count, D), BF),
+        drecv=v((count, D), BF),
+        datt=v((count, D), BF),
+        pool=v((8, D), F32),
+        dpool=v((8, D), F32),
+        emb=v((8, D), F32),
+        embd=v((1, D), F32),
+        embq=v((QPD, D), F32),
+        dbuf=v((groups, 1, D), F32),
+        qbuf=v((groups, QPD, D), F32),
+        dflat=v((groups, D), F32),
+        qflat=v((groups * QPD, D), F32),
+        loss=v((8, LANES), F32),
+        lossr=v((8, LANES), F32),
+        ln=v((line.bit_length() + 3, 8, D), F32),
+        lnr=v((line.bit_length() + 2, 8, D), F32),
+        gd=v((line, 2, plan.shard_ff, D), BF),
+        gd_rc=v((line, plan.shard_ff, D), BF),
+        gd_rz=v((line + 1, plan.shard_ff, D), BF),
+        gd_rx=v((plan.shard_ff, D), BF),
+        gd_f=v((plan.shard_ff, D), BF),
+        gg=v((line, 2, 2, shard, plan.ff), BF),
+        gg_rc=v((line, 2, shard, plan.ff), BF),
+        gg_rx=v((line, shard, plan.ff), BF),
+        gg_rz=v((line + 1, shard, plan.ff), BF),
+        gg_f=v((shard, plan.ff), BF),
+        ga_rc=v((line, 2, shard, plan.width_a), BF),
+        ga_rt=v((line, 2, shard, plan.half_a), BF),
+        ga_rx=v((line, shard, plan.half_a), BF),
+        ga_rz=v((line + 1, shard, plan.half_a), BF),
+        ga_f=v((shard, plan.half_a), BF),
+    )
+
+
+class Operands(NamedTuple):
+    qlen: Any
+    dlen: Any
+    pos: Any
+    posv: Any
+    tok: Any
+    tcos: Any
+    tsin: Any
+    tile: Any
+    i_qkv: Any
+    i_out: Any
+    i_gate: Any
+    i_up: Any
+    i_down: Any
+
+
+class Results(NamedTuple):
+    o_tok: Any
+    o_a: Any
+    o_gu: Any
+    o_dn: Any
+    o_vec: Any
+    o_q: Any
+    o_d: Any
+    o_loss: Any
+
+
+def whole_step(plan, *refs):
+    names = (Operands._fields + Results._fields + tuple(buffers(plan)) + tuple(semaphores(plan)))
+    r = SimpleNamespace(**dict(zip(names, refs, strict=True)))
+    line, groups, count = plan.line, plan.groups, plan.count
+    shard, shard_ff, stripe = plan.shard, plan.shard_ff, plan.stripe
+    half_a, half_ff, ff = plan.half_a, plan.half_ff, plan.ff
+    quarter = QLEN
+    shift = QLEN.bit_length() - 1
+
+    t = lax.axis_index(TOWER)
+    me = lax.axis_index(DP)
+    z = me // 4
+    x = (me // 2) % 2
+    c = me % 2
+
+    def at(zz, xx, cc):
+        return (zz * 2 + xx) * 2 + cc
+
+    dev_x = {TOWER: t, DP: at(z, 1 - x, c)}
+    dev_c = {TOWER: t, DP: at(z, x, 1 - c)}
+    dev_y = {TOWER: 1 - t, DP: me}
+
+    def dev_z(zz):
+        return {TOWER: t, DP: at(zz, x, c)}
+
+    pending, tail = [], []
+
+    def copy(src, dst, ssem, rsem, dev):
+        return pltpu.make_async_remote_copy(
+            src_ref=src, dst_ref=dst, send_sem=ssem, recv_sem=rsem,
+            device_id=dev, device_id_type=MESH,
+        )
+
+    def send(cond, what, keep=pending):
+        do(cond, what.start)
+        keep.append((cond, what))
+
+    def settle(keep):
+        for cond, what in keep:
+            do(cond, what.wait_send)
+        keep.clear()
+
+    def got(cond, ref, rsem):
+        do(cond, copy(ref, ref, r.s_loss.at[0], rsem, dev_x).wait_recv)
+
+    wa, wg, wd = r.wa, r.wg, r.wd
+    out_w = half_a - 3 * D // 2
+    local = []
+
+    def near(src, dst, cond=None):
+        what = pltpu.make_async_copy(src, dst, r.loc.at[len(local)])
+        do(cond, what.start)
+        local.append((cond, what))
+
+    third = 3 * D // 2
+    for h in range(2):
+        near(r.i_qkv.at[:, pl.ds(h * third, third)],
+             wa.at[z, x, c, :, pl.ds(h * half_a, third)])
+        near(r.i_out.at[:, pl.ds(h * out_w, out_w)],
+             wa.at[z, x, c, :, pl.ds(h * half_a + third, out_w)])
+    near(r.i_down, wd.at[z, c], x == t)
+    near(r.tile, r.vt.at[me])
+    for s in range(line):
+        for k, ref in enumerate((r.i_gate, r.i_up)):
+            near(ref.at[:, pl.ds(aligned((2 * s + t) * stripe, LANES), stripe)],
+                 wg.at[z, x, c, :, pl.ds(k * half_ff + s * stripe, stripe)])
+
+    barrier = pltpu.get_barrier_semaphore()
+
+    def greet(j, carry):
+        other = jnp.logical_or(j // groups != t, j % groups != me)
+
+        @pl.when(other)
+        def _():
+            pl.semaphore_signal(
+                barrier, inc=1, device_id={TOWER: j // groups, DP: j % groups},
+                device_id_type=MESH,
+            )
+
+        return carry
+
+    lax.fori_loop(0, 2 * groups, greet, 0)
+    pl.semaphore_wait(barrier, 2 * groups - 1)
+    for cond, what in local:
+        do(cond, what.wait)
+
+    def piece_a(zz, xx, cc, h):
+        return wa.at[zz, xx, cc, :, pl.ds(aligned(h * half_a, LANES), half_a)]
+
+    def send_a(cond, sem, zz, xx, h, dev):
+        ref = piece_a(zz, xx, c, h)
+        send(cond, copy(ref, ref, sem, r.ra.at[at(zz, xx, c), h], dev))
+
+    def got_a(cond, zz, xx, cc, h):
+        got(cond, piece_a(zz, xx, cc, h), r.ra.at[at(zz, xx, cc), h])
+
+    def sides(step):
+        yield z - step, z >= step, z < line - 1, z + 1, 0
+        yield z + step, z < line - step, z > 0, z - 1, 1
+
+    def a_round(step):
+        for zz, there, on, nxt, way in sides(step):
+            if step:
+                got_a(there, zz, x, c, t)
+            send_a(both(there, on), r.sa_z.at[way, zz], zz, x, t, dev_z(nxt))
+            if step or way == 0:
+                send_a(there, r.sa_x.at[zz], zz, x, t, dev_x)
+                if step:
+                    send_a(there, r.sa_y.at[zz, x], zz, x, t, dev_y)
+                send_a(there, r.sa_c.at[zz, x, t], zz, x, t, dev_c)
+        if step == 0:
+            send_a(None, r.sa_c.at[z, x, 1 - t], z, x, 1 - t, dev_c)
+
+    def around(step):
+        return list(sides(step))[: 1 if step == 0 else 2]
+
+    def a_cross(step):
+        for zz, there, _, _, _ in around(step):
+            got_a(there, zz, 1 - x, c, t)
+            send_a(there, r.sa_y.at[zz, 1 - x], zz, 1 - x, t, dev_y)
+            send_a(there, r.sa_c.at[zz, 1 - x, t], zz, 1 - x, t, dev_c)
+
+    def a_tower(step):
+        for zz, there, _, _, _ in around(step):
+            for xx in (x, 1 - x)[1 if step == 0 else 0:]:
+                got_a(there, zz, xx, c, 1 - t)
+                send_a(there, r.sa_c.at[zz, xx, 1 - t], zz, xx, 1 - t, dev_c)
+
+    def a_sibling():
+        for zz in range(line):
+            for xx in range(2):
+                for h in range(2):
+                    got_a(None, zz, xx, 1 - c, h)
+
+    def send_g(cond, sem, zz, xx, dev):
+        ref = wg.at[zz, xx, c]
+        send(cond, copy(ref, ref, sem, r.rg.at[at(zz, xx, c)], dev))
+
+    def got_g(cond, zz, xx, cc):
+        got(cond, wg.at[zz, xx, cc], r.rg.at[at(zz, xx, cc)])
+
+    def g_round(step):
+        for zz, there, on, nxt, way in sides(step):
+            if step:
+                got_g(there, zz, x, c)
+            send_g(both(there, on), r.sg_z.at[way, zz], zz, x, dev_z(nxt))
+            if step or way == 0:
+                send_g(there, r.sg_x.at[zz], zz, x, dev_x)
+                send_g(there, r.sg_c.at[zz, x], zz, x, dev_c)
+
+    def g_cross(step):
+        for zz, there, _, _, _ in around(step):
+            got_g(there, zz, 1 - x, c)
+            send_g(there, r.sg_c.at[zz, 1 - x], zz, 1 - x, dev_c)
+
+    def g_sibling():
+        for zz in range(line):
+            for xx in range(2):
+                got_g(None, zz, xx, 1 - c)
+
+    def send_d(cond, sem, zz, dev):
+        ref = wd.at[zz, c]
+        send(cond, copy(ref, ref, sem, r.rd.at[zz, c], dev))
+
+    def got_d(cond, zz, cc):
+        got(cond, wd.at[zz, cc], r.rd.at[zz, cc])
+
+    def d_cross():
+        send_d(x == t, r.sd_x.at[0], z, dev_x)
+
+    def d_round(step):
+        for zz, there, on, nxt, way in sides(step):
+            if step:
+                got_d(there, zz, c)
+            elif way == 0:
+                got_d(x != t, z, c)
+            send_d(both(there, on), r.sd_z.at[way, zz], zz, dev_z(nxt))
+            if step or way == 0:
+                send_d(there, r.sd_c.at[zz], zz, dev_c)
+
+    def d_sibling():
+        for zz in range(line):
+            got_d(None, zz, 1 - c)
+
+    def v_send(j, carry):
+        @pl.when(j != me)
+        def _():
+            copy(r.vt.at[me], r.vt.at[me], r.sv.at[j], r.rv.at[me],
+                 {TOWER: t, DP: j}).start()
+
+        return carry
+
+    def v_wait(j, carry):
+        @pl.when(j != me)
+        def _():
+            copy(r.vt.at[me], r.vt.at[j], r.sv.at[j], r.rv.at[j],
+                 {TOWER: t, DP: j}).wait()
+
+        return carry
+
+    a_round(0)
+    d_cross()
+    lax.fori_loop(0, groups, v_send, 0)
+
+    tok = r.tok
+    rows = lax.broadcasted_iota(jnp.int32, (count, count), 0)
+    cols = lax.broadcasted_iota(jnp.int32, (count, count), 1)
+    seg = cols >> shift
+    limit = jnp.zeros_like(cols)
+    for s in range(QPD):
+        limit = jnp.where(seg == s, r.qlen[s], limit)
+    limit = limit * (1 - t) + r.dlen[0] * t
+    place = cols - seg * (quarter * (1 - t))
+    apart = ((rows >> shift) - seg) * (1 - t)
+    seen = both(apart == 0, place < limit)
+    r.hide[...] = jnp.where(seen, 0.0, 1.0)
+    for s in range(QPD):
+        part = pl.ds(s * quarter, quarter)
+        length = jnp.full((quarter, 1), r.qlen[s] * (1 - t) + r.dlen[0] * t, jnp.int32)
+        slot = lax.broadcasted_iota(jnp.int32, (quarter, 1), 0) + s * quarter * t
+        r.pw[part, :] = jnp.where(slot < length, 1.0 / length.astype(F32), 0.0)
+        begin = aligned(s * quarter * t, quarter)
+        r.cos[part, :] = r.tcos[pl.ds(begin, quarter), :]
+        r.sin[part, :] = r.tsin[pl.ds(begin, quarter), :]
+    lanes = lax.broadcasted_iota(jnp.int32, (count, LANES), 1)
+    first_head = lanes < HEAD
+    low_half = (lanes & (HEAD - 1)) < HEAD // 2
+
+    def swap(a):
+        return jnp.where(low_half, pltpu.roll(a, LANES - HEAD // 2, 1), pltpu.roll(a, HEAD // 2, 1))
+
+    def turn(a):
+        return a * r.cos[...] + swap(a) * r.sin[...]
+
+    def turn_back(a):
+        return a * r.cos[...] - swap(a) * r.sin[...]
+
+    def transpose_into(dst, src, width):
+        def body(j, carry):
+            o = aligned(j * LANES, LANES)
+            dst[pl.ds(o, LANES), :] = src[:, pl.ds(o, LANES)].T
+            return carry
+
+        lax.fori_loop(0, width // LANES, body, 0)
+
+    def wide(ref, lo, n):
+        return ref[:, :, :, :, pl.ds(lo, n)].reshape(groups * shard, n)
+
+    def qkv_lane(u):
+        split = 3 * D // 2 // LANES
+        return aligned(jnp.where(u < split, u, u + out_w // LANES) * LANES, LANES)
+
+    a_round(1)
+    g_round(0)
+    transpose_into(r.tokt, tok, D)
+    for step in range(2, line):
+        a_round(step)
+    for step in range(line):
+        a_cross(step)
+    d_round(0)
+    g_round(1)
+    for step in range(line):
+        a_tower(step)
+    g_round(2)
+    a_sibling()
+    pairs = D // LANES
+
+    def project(p, carry):
+        w = jnp.concatenate(
+            [wide(wa, qkv_lane(p + k * pairs), LANES) for k in range(3)], axis=1
+        )
+        packed = jnp.dot(tok[...], w, preferred_element_type=F32)
+        o = aligned(p * LANES, LANES)
+        r.qkv[:, pl.ds(o, LANES)] = turn(packed[:, :LANES]).astype(BF)
+        r.qkv[:, pl.ds(D + o, LANES)] = turn(packed[:, LANES : 2 * LANES]).astype(BF)
+        r.qkv[:, pl.ds(2 * D + o, LANES)] = packed[:, 2 * LANES :].astype(BF)
+        return carry
+
+    scale = HEAD ** (-0.5)
+
+    def triple(p):
+        o = aligned(p * LANES, LANES)
+        return tuple(r.qkv[:, pl.ds(k * D + o, LANES)] for k in range(3))
+
+    def only(h, a):
+        return jnp.where(first_head if h == 0 else jnp.logical_not(first_head), a, jnp.zeros_like(a))
+
+    def attend(p, carry):
+        q2, k2, v2 = triple(p)
+        outs = []
+        for h in range(2):
+            scores = dot_tt(only(h, q2), k2) * scale
+            scores = jnp.where(r.hide[...] > 0.5, -1e30, scores)
+            grown = jnp.exp(scores - jnp.max(scores, -1, keepdims=True))
+            probs = grown * (1.0 / jnp.sum(grown, -1, keepdims=True))
+            r.probs[2 * p + h] = probs
+            outs.append(jnp.dot(probs.astype(BF), v2, preferred_element_type=F32))
+        o = aligned(p * LANES, LANES)
+        r.mixed[:, pl.ds(o, LANES)] = jnp.where(first_head, outs[0], outs[1]).astype(BF)
+        return carry
+
+    lax.fori_loop(0, pairs, project, 0)
+    d_round(1)
+    for step in range(3, line):
+        g_round(step)
+    for step in range(line):
+        g_cross(step)
+    lax.fori_loop(0, pairs // 2, attend, 0)
+    d_round(2)
+    lax.fori_loop(pairs // 2, pairs, attend, 0)
+    for step in range(3, line):
+        d_round(step)
+
+    lax.fori_loop(0, groups, v_wait, 0)
+
+    def widen_vec(j, acc):
+        row = lax.broadcasted_iota(jnp.int32, (LANES, D), 0)
+        col = lax.broadcasted_iota(jnp.int32, (LANES, D), 1)
+        pick = jnp.where(col == row + j * plan.vec, 1.0, 0.0).astype(BF)
+        return acc + jnp.dot(r.vt[j], pick, preferred_element_type=F32)
+
+    r.vec[...] = lax.fori_loop(0, groups, widen_vec, jnp.zeros((16, D), F32))
+
+    for h in range(2):
+        part = jnp.dot(r.mixed[...], wide(wa, h * half_a + 3 * D // 2, out_w),
+                       preferred_element_type=F32)
+        r.h1[:, pl.ds(h * out_w, out_w)] = tok[:, pl.ds(h * out_w, out_w)].astype(F32) + part
+
+    def moments(h):
+        centred = h - jnp.mean(h, -1, keepdims=True)
+        return centred, lax.rsqrt(jnp.mean(centred * centred, -1, keepdims=True) + 1e-05)
+
+    blocks = count // quarter
+
+    def norm_one(b, carry):
+        part = pl.ds(aligned(b * quarter, quarter), quarter)
+        centred, inverse = moments(r.h1[part, :])
+        hat = centred * inverse
+        normed = hat * r.vec[0:1, :] + r.vec[1:2, :]
+        r.h1[part, :] = hat
+        r.rs1[part, :] = inverse
+        r.n1[part, :] = normed
+        r.feed[pl.ds(aligned(t * count + b * quarter, quarter), quarter), :] = (
+            normed.astype(BF))
+        return carry
+
+    lax.fori_loop(0, blocks, norm_one, 0)
+    mine = pl.ds(aligned(t * count, count), count)
+    theirs = pl.ds(aligned((1 - t) * count, count), count)
+
+    def swap_rows(k, src, dst):
+        send(None, copy(src, dst, r.sx.at[k], r.rx.at[k], dev_y), tail)
+
+    def got_rows(k, ref):
+        got(None, ref, r.rx.at[k])
+
+    swap_rows(0, r.feed.at[mine], r.feed.at[mine])
+    transpose_into(r.mixt, r.mixed, D)
+    got_rows(0, r.feed.at[theirs])
+    transpose_into(r.feedt, r.feed, D)
+    g_sibling()
+
+    step_ff = 2 * LANES
+
+    def gated(j, carry):
+        o = aligned(j * step_ff, step_ff)
+        gate = jnp.dot(r.feed[...], wide(wg, o, step_ff), preferred_element_type=F32)
+        up = jnp.dot(r.feed[...], wide(wg, half_ff + o, step_ff), preferred_element_type=F32)
+        r.gate[:, pl.ds(o, step_ff)] = gate
+        r.up[:, pl.ds(o, step_ff)] = up
+        hidden = (gate * jax.nn.sigmoid(gate) * up).astype(BF)
+        r.dgu[:, pl.ds(o, step_ff)] = hidden
+        r.hidt[pl.ds(o, step_ff), :] = hidden.T
+        return carry
+
+    lax.fori_loop(0, half_ff // step_ff, gated, 0)
+    d_sibling()
+
+    def down(rows_of, store):
+        def body(j, carry):
+            o = aligned(j * step_ff, step_ff)
+            w = wd[:, :, :, pl.ds(o, step_ff)].reshape(half_ff, step_ff)
+            store(o, jnp.dot(r.dgu[rows_of, pl.ds(0, half_ff)], w, preferred_element_type=F32))
+            return carry
+
+        lax.fori_loop(0, D // step_ff, body, 0)
+
+    def keep_send(o, val):
+        r.bsend[:, pl.ds(o, step_ff)] = val.astype(BF)
+
+    def keep_own(o, val):
+        r.bown[:, pl.ds(o, step_ff)] = val
+
+    down(theirs, keep_send)
+    swap_rows(1, r.bsend, r.brecv)
+    down(mine, keep_own)
+    got_rows(1, r.brecv)
+
+    r.pool[...] = jnp.zeros((8, D), F32)
+
+    def norm_two(b, carry):
+        part = pl.ds(aligned(b * quarter, quarter), quarter)
+        h = r.n1[part, :] + (r.bown[part, :] + r.brecv[part, :].astype(F32))
+        centred, inverse = moments(h)
+        hat = centred * inverse
+        normed = hat * r.vec[2:3, :] + r.vec[3:4, :]
+        r.xh2[part, :] = hat
+        r.rs2[part, :] = inverse
+        r.pool[pl.ds(b, 1), :] = jnp.sum(normed * r.pw[part, :], 0, keepdims=True)
+        return carry
+
+    lax.fori_loop(0, blocks, norm_two, 0)
+    row8 = lax.broadcasted_iota(jnp.int32, (8, D), 0)
+
+    @pl.when(t == 1)
+    def _():
+        all_rows = jnp.sum(r.pool[...], 0, keepdims=True)
+        r.pool[...] = jnp.where(row8 == 0, all_rows, 0.0)
+
+    pooled = r.pool[...]
+    shrink = lax.rsqrt(jnp.sum(pooled * pooled, -1, keepdims=True) + 1e-06)
+    r.emb[...] = pooled * shrink
+
+    @pl.when(t == 0)
+    def _():
+        r.embq[...] = r.emb[0:QPD, :]
+
+        def give(step, carry):
+            j = (me + step) % groups
+            copy(r.embq, r.qbuf.at[me], r.s_query.at[j], r.r_query.at[me],
+                 {TOWER: 1, DP: j}).start()
+            return carry
+
+        def take(j, carry):
+            copy(r.embd, r.dbuf.at[j], r.s_doc.at[0, 0], r.r_doc.at[j],
+                 {TOWER: 1, DP: j}).wait_recv()
+            return carry
+
+        lax.fori_loop(0, groups, give, 0)
+        lax.fori_loop(0, groups, take, 0)
+
+    @pl.when(t == 1)
+    def _():
+        r.embd[...] = r.emb[0:1, :]
+        r.dbuf[me] = r.emb[0:1, :]
+
+        def give(step, carry):
+            j = (me + step) % groups
+            copy(r.embd, r.dbuf.at[me], r.s_doc.at[0, j], r.r_doc.at[me],
+                 {TOWER: 0, DP: j}).start()
+
+            @pl.when(j != me)
+            def _():
+                copy(r.embd, r.dbuf.at[me], r.s_doc.at[1, j], r.r_doc.at[me],
+                     {TOWER: 1, DP: j}).start()
+
+            return carry
+
+        def take(j, carry):
+            copy(r.embq, r.qbuf.at[j], r.s_query.at[0], r.r_query.at[j],
+                 {TOWER: 0, DP: j}).wait_recv()
+
+            @pl.when(j != me)
+            def _():
+                copy(r.embd, r.dbuf.at[j], r.s_doc.at[0, 0], r.r_doc.at[j],
+                     {TOWER: 0, DP: j}).wait_recv()
+
+            return carry
+
+        lax.fori_loop(0, groups, give, 0)
+        lax.fori_loop(0, groups, take, 0)
+
+    for j in range(groups):
+        r.dflat[pl.ds(j, 1), :] = r.dbuf[j]
+    best = exact_product_accuracy
+    r.dpool[...] = jnp.zeros((8, D), F32)
+
+    @pl.when(t == 0)
+    def _():
+        docs = r.dflat[...]
+        logits = dot_tt(r.embq[...], docs, best) / contrast_sharpness_factor
+        peak = jnp.max(logits, -1, keepdims=True)
+        lse = peak + jnp.log(jnp.sum(jnp.exp(logits - peak), -1, keepdims=True))
+        col = lax.broadcasted_iota(jnp.int32, (QPD, groups), 1)
+        row = lax.broadcasted_iota(jnp.int32, (QPD, groups), 0)
+        label = jnp.zeros((QPD, groups), jnp.int32)
+        for s in range(QPD):
+            label = jnp.where(row == s, r.pos[me * QPD + s], label)
+        hot = jnp.where(col == label, 1.0, 0.0)
+        slope = (jnp.exp(logits - lse) - hot) / contrast_sharpness_factor
+        r.dpool[0:QPD, :] = jnp.dot(slope, docs, preferred_element_type=F32, precision=best)
+
+    @pl.when(t == 1)
+    def _():
+        for j in range(groups):
+            r.qflat[pl.ds(j * QPD, QPD), :] = r.qbuf[j]
+        docs, queries = r.dflat[...], r.qflat[...]
+        logits = dot_tt(docs, queries, best) / contrast_sharpness_factor
+        peak = jnp.max(logits, 0, keepdims=True)
+        lse = peak + jnp.log(jnp.sum(jnp.exp(logits - peak), 0, keepdims=True))
+        row = lax.broadcasted_iota(jnp.int32, (groups, groups * QPD), 0)
+        hit = row == r.posv[...]
+        picked = jnp.sum(jnp.where(hit, logits, 0.0), 0, keepdims=True)
+        total = jnp.sum(lse - picked, -1, keepdims=True)
+        r.loss[...] = jnp.broadcast_to(total / (groups * QPD), (8, LANES))
+        slope = (jnp.exp(logits - lse) - jnp.where(hit, 1.0, 0.0)) / contrast_sharpness_factor
+        line_of = jnp.sum(jnp.where(row == me, slope, 0.0), 0, keepdims=True)
+        r.dpool[0:1, :] = jnp.dot(line_of, queries, preferred_element_type=F32, precision=best)
+
+    slope = r.dpool[...]
+    emb = r.emb[...]
+    dpool = shrink * (slope - emb * jnp.sum(slope * emb, -1, keepdims=True))
+
+    @pl.when(t == 0)
+    def _():
+        r.dpool[...] = dpool
+
+    @pl.when(t == 1)
+    def _():
+        r.dpool[...] = jnp.broadcast_to(dpool[0:1, :], (8, D))
+
+    def norm_two_back(b, sums):
+        part = pl.ds(aligned(b * quarter, quarter), quarter)
+        top = r.pw[part, :] * r.dpool[pl.ds(b, 1), :]
+        hat = r.xh2[part, :]
+        inner = top * r.vec[2:3, :]
+        grad = r.rs2[part, :] * (
+            inner - jnp.mean(inner, -1, keepdims=True)
+            - hat * jnp.mean(inner * hat, -1, keepdims=True))
+        r.n1[part, :] = grad
+        r.dbr[pl.ds(aligned(t * count + b * quarter, quarter), quarter), :] = (
+            grad.astype(BF))
+        return (sums[0] + jnp.sum(top * hat, 0, keepdims=True),
+                sums[1] + jnp.sum(top, 0, keepdims=True))
+
+    zero_row = jnp.zeros((1, D), F32)
+    gain_two, bias_two = lax.fori_loop(0, blocks, norm_two_back, (zero_row, zero_row))
+    swap_rows(2, r.dbr.at[mine], r.dbr.at[mine])
+
+    send(t == 1, copy(r.loss, r.lossr, r.s_loss.at[0], r.r_loss.at[0], dev_y), tail)
+    r.ln[0] = jnp.where(row8 == 2, gain_two, 0.0) + jnp.where(row8 == 3, bias_two, 0.0)
+
+    def hidden_back(rows_of):
+        def body(j, carry):
+            o = aligned(j * stripe, LANES)
+            w = wd[j].reshape(stripe, D)
+            slope = dot_tt(r.dbr[rows_of, :], w)
+            gate = r.gate[rows_of, pl.ds(o, stripe)]
+            up = r.up[rows_of, pl.ds(o, stripe)]
+            sig = jax.nn.sigmoid(gate)
+            r.dgu[rows_of, pl.ds(o, stripe)] = (
+                slope * up * (sig * (1.0 + gate * (1.0 - sig)))).astype(BF)
+            r.dgu[rows_of, pl.ds(half_ff + o, stripe)] = (slope * (gate * sig)).astype(BF)
+            return carry
+
+        lax.fori_loop(0, line, body, 0)
+
+    hidden_back(mine)
+    got_rows(2, r.dbr.at[theirs])
+
+    def along(step):
+        for s in range(1, line):
+            yield line - s, both(z == step, z < line - s), z + 1, 0
+        for s in range(line - 1):
+            yield s, both(z == line - 1 - step, z > s), z - 1, 1
+
+    def added(refs):
+        total = refs[0][...].astype(F32)
+        for ref in refs[1:]:
+            total = total + ref[...].astype(F32)
+        return total
+
+    def line_step(step, parts, sem, slot):
+        for dest, cond, nxt, way in along(step):
+            into = slot(dest + 1 if way == 0 else dest)
+            refs = parts(dest)
+
+            def move(into=into, refs=refs, dest=dest, way=way):
+                if step:
+                    copy(into, into, r.s_loss.at[0], sem(1, way, dest), dev_x).wait_recv()
+                    refs[0][...] = added(refs + (into,)).astype(BF)
+                else:
+                    refs[0][...] = added(refs).astype(BF)
+
+            do(cond, move)
+            send(cond, copy(refs[0], into, sem(0, way, dest), sem(1, way, dest),
+                            dev_z(nxt)), tail)
+
+    def line_end(parts, sem, slot, put):
+        for cond, ways in ((z == 0, (1,)), (z == line - 1, (0,)),
+                           (both(z > 0, z < line - 1), (0, 1))):
+            def finish(ways=ways):
+                refs = parts(z)
+                for way in ways:
+                    into = slot(z + 1 if way == 0 else z)
+                    copy(into, into, r.s_loss.at[0], sem(1, way, z), dev_x).wait_recv()
+                    refs = refs + (into,)
+                put[...] = added(refs).astype(BF)
+
+            do(cond, finish)
+
+    gd = r.gd
+
+    def down_grad(s):
+        gd[s] = jnp.dot(r.hidt[pl.ds(s * stripe, stripe), :], r.dbr[...],
+                        preferred_element_type=F32).astype(BF).reshape(2, shard_ff, D)
+        send(None, copy(gd.at[s, 1 - c], r.gd_rc.at[s], r.gd_c.at[0, s],
+                        r.gd_c.at[1, s], dev_c), tail)
+
+    def down_parts(dest):
+        return gd.at[dest, c], r.gd_rc.at[dest]
+
+    def down_arrive():
+        for s in range(line):
+            got(None, r.gd_rc.at[s], r.gd_c.at[1, s])
+
+    def down_line(step):
+        line_step(step, down_parts, lambda *i: r.gd_z.at[i], lambda k: r.gd_rz.at[k])
+
+    def down_end():
+        line_end(down_parts, lambda *i: r.gd_z.at[i], lambda k: r.gd_rz.at[k], r.gd_f)
+        send(x != t, copy(r.gd_f, r.gd_rx, r.gd_x.at[0], r.gd_x.at[1], dev_x), tail)
+
+    out_copies = []
+
+    def keep_out(k, src, dst, cond=None):
+        what = pltpu.make_async_copy(src, dst, r.fin.at[k])
+        do(cond, what.start)
+        out_copies.append((cond, what))
+
+    def down_out():
+        def total():
+            copy(r.gd_rx, r.gd_rx, r.s_loss.at[0], r.gd_x.at[1], dev_x).wait_recv()
+            r.gd_f[...] = added((r.gd_f, r.gd_rx)).astype(BF)
+
+        do(x == t, total)
+        keep_out(0, r.gd_f, r.o_dn, x == t)
+        send(x == t, copy(r.gd_f, r.o_dn, r.gd_y.at[0], r.gd_y.at[1], dev_y), tail)
+
+    gg = r.gg
+    part_gu = ff // 4
+
+    def gate_grad(k):
+        span = pl.ds(k * part_gu, part_gu)
+        val = jnp.dot(r.feedt[...], r.dgu[:, span], preferred_element_type=F32)
+        gg[:, :, :, :, span] = val.astype(BF).reshape(line, 2, 2, shard, part_gu)
+        send(None, copy(gg.at[:, :, 1 - c, :, span], r.gg_rc.at[:, :, :, span],
+                        r.gg_c.at[0, k], r.gg_c.at[1, k], dev_c), tail)
+
+    def gate_cross(k):
+        span = pl.ds(k * part_gu, part_gu)
+        got(None, r.gg_rc.at[:, :, :, span], r.gg_c.at[1, k])
+        for s in range(line):
+            mine_k = gg.at[s, 1 - x, c, :, span]
+            mine_k[...] = added((mine_k, r.gg_rc.at[s, 1 - x, :, span])).astype(BF)
+        send(None, copy(gg.at[:, 1 - x, c, :, span], r.gg_rx.at[:, :, span],
+                        r.gg_x.at[0, k], r.gg_x.at[1, k], dev_x), tail)
+
+    def gate_parts(k):
+        span = pl.ds(k * part_gu, part_gu)
+        return lambda dest: (gg.at[dest, x, c, :, span], r.gg_rc.at[dest, x, :, span],
+                             r.gg_rx.at[dest, :, span])
+
+    def gate_line(k, step):
+        span = pl.ds(k * part_gu, part_gu)
+        if step == 0:
+            got(None, r.gg_rx.at[:, :, span], r.gg_x.at[1, k])
+        line_step(step, gate_parts(k), lambda a, *i: r.gg_z.at[(a, k) + i], lambda s: r.gg_rz.at[s, :, span])
+
+    def gate_end(k):
+        span = pl.ds(k * part_gu, part_gu)
+        line_end(gate_parts(k), lambda a, *i: r.gg_z.at[(a, k) + i], lambda s: r.gg_rz.at[s, :, span],
+                 r.gg_f.at[:, span])
+        keep_out(1 + k, r.gg_f.at[:, span], r.o_gu.at[t, :, span])
+        send(None, copy(r.gg_f.at[:, span], r.o_gu.at[t, :, span], r.gg_y.at[0, k],
+                        r.gg_y.at[1, k], dev_y), tail)
+
+    ga = wg
+    part_a = half_a // 4
+
+    def cols_a(k, h):
+        return pl.ds(aligned(h * half_a + k * part_a, LANES), part_a)
+
+    def store_a(k, left, right):
+        for h in range(2):
+            val = jnp.dot(left[...], right[h], preferred_element_type=F32)
+            ga[:, :, :, :, cols_a(k, h)] = val.astype(BF).reshape(line, 2, 2, shard, part_a)
+            send(None, copy(ga.at[:, :, 1 - c, :, cols_a(k, h)],
+                            r.ga_rc.at[:, :, :, cols_a(k, h)],
+                            r.ga_c.at[0, h, k], r.ga_c.at[1, h, k], dev_c), tail)
+
+    def span_a(k):
+        return pl.ds(k * part_a, part_a)
+
+    def tower_a(k):
+        for h in range(2):
+            got(None, r.ga_rc.at[:, :, :, cols_a(k, h)], r.ga_c.at[1, h, k])
+        gone = cols_a(k, 1 - t)
+        for s in range(line):
+            for xx in range(2):
+                ref = ga.at[s, xx, c, :, gone]
+                ref[...] = added((ref, r.ga_rc.at[s, xx, :, gone])).astype(BF)
+        send(None, copy(ga.at[:, :, c, :, gone], r.ga_rt.at[:, :, :, span_a(k)],
+                        r.ga_t.at[0, k], r.ga_t.at[1, k], dev_y), tail)
+
+    def cross_a(k):
+        got(None, r.ga_rt.at[:, :, :, span_a(k)], r.ga_t.at[1, k])
+        here = cols_a(k, t)
+        for s in range(line):
+            ref = ga.at[s, 1 - x, c, :, here]
+            ref[...] = added((ref, r.ga_rc.at[s, 1 - x, :, here],
+                              r.ga_rt.at[s, 1 - x, :, span_a(k)])).astype(BF)
+        send(None, copy(ga.at[:, 1 - x, c, :, here], r.ga_rx.at[:, :, span_a(k)],
+                        r.ga_x.at[0, k], r.ga_x.at[1, k], dev_x), tail)
+
+    def parts_a(k):
+        here = cols_a(k, t)
+        return lambda dest: (ga.at[dest, x, c, :, here], r.ga_rc.at[dest, x, :, here],
+                             r.ga_rt.at[dest, x, :, span_a(k)],
+                             r.ga_rx.at[dest, :, span_a(k)])
+
+    def line_a(k, step):
+        if step == 0:
+            got(None, r.ga_rx.at[:, :, span_a(k)], r.ga_x.at[1, k])
+        line_step(step, parts_a(k), lambda a, *i: r.ga_z.at[(a, k) + i], lambda s: r.ga_rz.at[s, :, span_a(k)])
+
+    def end_a(k):
+        line_end(parts_a(k), lambda a, *i: r.ga_z.at[(a, k) + i], lambda s: r.ga_rz.at[s, :, span_a(k)],
+                 r.ga_f.at[:, span_a(k)])
+        keep_out(5 + k, r.ga_f.at[:, span_a(k)], r.o_a.at[:, cols_a(k, t)])
+        send(None, copy(r.ga_f.at[:, span_a(k)], r.o_a.at[:, cols_a(k, t)],
+                        r.ga_y.at[0, k], r.ga_y.at[1, k], dev_y), tail)
+
+    some = 2 * 4 * shard
+
+    def rows_of_weight(ref, j, lo, n):
+        return ref[pl.ds(2 * j, 2), :, :, :, pl.ds(lo, n)].reshape(some, n)
+
+    def feed_back(rows_of, store):
+        def body(j, carry):
+            store(pl.ds(aligned(j * some, LANES), some),
+                  dot_tt(r.dgu[rows_of, :], rows_of_weight(wg, j, 0, ff)))
+            return carry
+
+        lax.fori_loop(0, line // 2, body, 0)
+
+    def back_send(span, val):
+        r.dsend[:, span] = val.astype(BF)
+
+    def back_own(span, val):
+        r.bown[:, span] = val
+
+    for s in range(line):
+        down_grad(s)
+    hidden_back(theirs)
+    down_arrive()
+    down_line(0)
+    feed_back(theirs, back_send)
+    swap_rows(3, r.dsend, r.drecv)
+    gate_grad(0)
+    gate_grad(1)
+    gate_cross(0)
+    down_line(1)
+    gate_grad(2)
+    gate_cross(1)
+    gate_line(0, 0)
+    gate_grad(3)
+    gate_cross(2)
+    for step in range(2, line - 1):
+        down_line(step)
+    gate_line(1, 0)
+    gate_line(0, 1)
+    feed_back(mine, back_own)
+    gate_cross(3)
+    down_end()
+    settle(pending)
+    gate_line(2, 0)
+    gate_line(1, 1)
+    gate_line(0, 2)
+    got_rows(3, r.drecv)
+
+    def norm_one_back(b, sums):
+        part = pl.ds(aligned(b * quarter, quarter), quarter)
+        top = r.n1[part, :] + r.bown[part, :] + r.drecv[part, :].astype(F32)
+        hat = r.h1[part, :]
+        inner = top * r.vec[0:1, :]
+        grad = r.rs1[part, :] * (
+            inner - jnp.mean(inner, -1, keepdims=True)
+            - hat * jnp.mean(inner * hat, -1, keepdims=True))
+        r.n1[part, :] = grad
+        r.datt[part, :] = grad.astype(BF)
+        return (sums[0] + jnp.sum(top * hat, 0, keepdims=True),
+                sums[1] + jnp.sum(top, 0, keepdims=True))
+
+    gain_one, bias_one = lax.fori_loop(0, blocks, norm_one_back, (zero_row, zero_row))
+    r.ln[0] = (r.ln[0] + jnp.where(row8 == 0, gain_one, 0.0)
+                  + jnp.where(row8 == 1, bias_one, 0.0))
+
+    ln_peers = [dev_c, dev_x, dev_y]
+    for bit in range(line.bit_length() - 1):
+        apart = 1 << bit
+        ln_peers.append(dev_z(z + apart * (1 - 2 * ((z // apart) % 2))))
+    last = len(ln_peers)
+
+    def ln_send(k):
+        send(None, copy(r.ln.at[k], r.lnr.at[k], r.s_ln.at[k], r.r_ln.at[k],
+                        ln_peers[k]), tail)
+
+    def ln_add(k):
+        got(None, r.lnr.at[k], r.r_ln.at[k])
+        r.ln[k + 1] = r.ln[k] + r.lnr[k]
+
+    dqkv = r.dgu.at[pl.ds(0, count), pl.ds(0, 3 * D)]
+    dmix = r.dgu.at[pl.ds(count, count), pl.ds(0, D)]
+
+    ln_send(0)
+    store_a(3, r.mixt, [r.datt[:, pl.ds(h * out_w, out_w)] for h in range(2)])
+
+    def mixed_back(j, carry):
+        val = sum(dot_tt(r.datt[:, pl.ds(h * out_w, out_w)],
+                         rows_of_weight(wa, j, h * half_a + third, out_w)) for h in range(2))
+        dmix[:, pl.ds(aligned(j * some, LANES), some)] = val.astype(BF)
+        return carry
+
+    lax.fori_loop(0, line // 2, mixed_back, 0)
+    ln_add(0)
+    ln_send(1)
+    tower_a(3)
+    gate_line(3, 0)
+    gate_line(2, 1)
+    gate_line(1, 2)
+    down_out()
+    gate_end(0)
+
+    def attend_back(p, carry):
+        q2, k2, v2 = triple(p)
+        o = aligned(p * LANES, LANES)
+        dm2 = dmix[:, pl.ds(o, LANES)]
+        parts = []
+        for h in range(2):
+            probs = r.probs[2 * p + h]
+            dprobs = dot_tt(only(h, dm2), v2)
+            mean = jnp.sum(probs * dprobs, -1, keepdims=True)
+            dscores = (probs * (dprobs - mean)).astype(BF)
+            parts.append((jnp.dot(dscores, k2, preferred_element_type=F32),
+                          dot_t0(dscores, q2), dot_t0(probs.astype(BF), dm2)))
+        dq, dk, dv = (jnp.where(first_head, a, b) for a, b in zip(*parts))
+        dqkv[:, pl.ds(o, LANES)] = turn_back(dq * scale).astype(BF)
+        dqkv[:, pl.ds(D + o, LANES)] = turn_back(dk * scale).astype(BF)
+        dqkv[:, pl.ds(2 * D + o, LANES)] = dv.astype(BF)
+        return carry
+
+    lax.fori_loop(0, 2, attend_back, 0)
+    ln_add(1)
+    ln_send(2)
+    gate_line(3, 1)
+    gate_line(2, 2)
+    gate_end(1)
+    lax.fori_loop(2, 4, attend_back, 0)
+    ln_add(2)
+    ln_send(3)
+    cross_a(3)
+    gate_line(3, 2)
+    gate_end(2)
+    lax.fori_loop(4, pairs, attend_back, 0)
+    ln_add(3)
+    ln_send(4)
+    line_a(3, 0)
+    gate_end(3)
+    for k in range(3):
+        store_a(k, r.tokt, [dqkv[:, pl.ds(h * third + k * part_a, part_a)]
+                               for h in range(2)])
+    line_a(3, 1)
+    for k in range(3):
+        tower_a(k)
+    for k in range(4, last):
+        ln_add(k)
+        if k + 1 < last:
+            ln_send(k + 1)
+    r.o_vec[...] = r.ln[last]
+
+    def token_back(j, carry):
+        val = sum(dot_tt(dqkv[:, pl.ds(h * third, third)],
+                         rows_of_weight(wa, j, h * half_a, third)) for h in range(2))
+        span = pl.ds(aligned(j * some, LANES), some)
+        r.o_tok[:, span] = r.n1[:, span] + val
+        return carry
+
+    lax.fori_loop(0, line // 2, token_back, 0)
+    line_a(3, 2)
+    for k in range(3):
+        cross_a(k)
+    end_a(3)
+    for step in range(line - 1):
+        for k in range(3):
+            line_a(k, step)
+    for k in range(3):
+        end_a(k)
+
+    @pl.when(t == 0)
+    def _():
+        got(None, r.lossr, r.r_loss.at[0])
+        r.o_loss[...] = r.lossr[...]
+        r.o_q[...] = r.embq[...]
+
+    @pl.when(t == 1)
+    def _():
+        r.o_loss[...] = r.loss[...]
+        r.o_q[...] = r.qbuf[me]
+
+    r.o_d[...] = r.dbuf[me]
+
+    @pl.when(t == 0)
+    def _():
+        def sent(j, carry):
+            copy(r.embq, r.qbuf.at[me], r.s_query.at[j], r.r_query.at[me],
+                 {TOWER: 1, DP: j}).wait_send()
+            return carry
+
+        lax.fori_loop(0, groups, sent, 0)
+
+    @pl.when(t == 1)
+    def _():
+        def sent(j, carry):
+            copy(r.embd, r.dbuf.at[me], r.s_doc.at[0, j], r.r_doc.at[me],
+                 {TOWER: 0, DP: j}).wait_send()
+
+            @pl.when(j != me)
+            def _():
+                copy(r.embd, r.dbuf.at[me], r.s_doc.at[1, j], r.r_doc.at[me],
+                     {TOWER: 1, DP: j}).wait_send()
+
+            return carry
+
+        lax.fori_loop(0, groups, sent, 0)
+
+    got(x != t, r.o_dn, r.gd_y.at[1])
+    for k in range(4):
+        got(None, r.o_gu.at[1 - t, :, pl.ds(k * part_gu, part_gu)], r.gg_y.at[1, k])
+        got(None, r.o_a.at[:, cols_a(k, 1 - t)], r.ga_y.at[1, k])
+    for cond, what in out_copies:
+        do(cond, what.wait)
+    settle(tail)
+
+
+def finish(plan, *refs):
+    (a_ref, gu_ref, dn_ref, vec_ref, tok_ref, q_ref, d_ref, loss_ref,
+     o_loss, o_q, o_d, o_tok, o_qkv, o_out, o_gate, o_up, o_down, *o_vecs) = refs
+    third, half_a, half_ff, stripe = 3 * D // 2, plan.half_a, plan.half_ff, plan.stripe
+    out_w = half_a - third
+    for h in range(2):
+        o_qkv[:, h * third : (h + 1) * third] = a_ref[:, h * half_a : h * half_a + third].astype(F32)
+        o_out[:, h * out_w : (h + 1) * out_w] = (
+            a_ref[:, h * half_a + third : (h + 1) * half_a].astype(F32))
+        for s in range(plan.line):
+            to = pl.ds((2 * s + h) * stripe, stripe)
+            o_gate[:, to] = gu_ref[h, :, pl.ds(s * stripe, stripe)].astype(F32)
+            o_up[:, to] = gu_ref[h, :, pl.ds(half_ff + s * stripe, stripe)].astype(F32)
+    o_down[...] = dn_ref[...].astype(F32)
+    o_tok[0] = tok_ref[...]
+    o_q[...] = q_ref[...]
+    o_d[...] = d_ref[...]
+    o_loss[...] = loss_ref[0:1, 0:1]
+    first = lax.axis_index(DP) * plan.vec
+    row = lax.broadcasted_iota(jnp.int32, (D, LANES), 0)
+    col = lax.broadcasted_iota(jnp.int32, (D, LANES), 1)
+    pick = jnp.where(row == first + col, 1.0, 0.0)
+    own = jnp.dot(vec_ref[...], pick, preferred_element_type=F32, precision=exact_product_accuracy)
+    for k, out in enumerate(o_vecs):
+        out[...] = own[k : k + 1, 0 : plan.vec]
+
+
+def on_device_kernel(plan, tokens, query_lengths, doc_lengths, positives, w_qkv, w_out, w_gate,
+                     w_up, w_down, ln1_gain, first_layernorm_shift, ln2_gain, ln2_bias):
+    count, groups, shard, vec = plan.count, plan.groups, plan.shard, plan.vec
+    cosines, sines = rotary_constants(count)
+    tile = jnp.pad(jnp.stack([ln1_gain, first_layernorm_shift, ln2_gain, ln2_bias]),
+                   ((0, 12), (0, LANES - vec)))
+    vmem = pl.BlockSpec(memory_space=pltpu.VMEM)
+    smem = pl.BlockSpec(memory_space=pltpu.SMEM)
+    hbm = pl.BlockSpec(memory_space=pl.ANY)
+    shape = jax.ShapeDtypeStruct
+    made = pl.pallas_call(
+        functools.partial(whole_step, plan),
+        out_shape=(
+            shape((count, D), F32), shape((shard, plan.width_a), BF), shape((2, shard, plan.ff), BF),
+            shape((plan.shard_ff, D), BF), shape((8, D), F32), shape((QPD, D), F32),
+            shape((1, D), F32), shape((8, LANES), F32),
+        ),
+        in_specs=[smem, smem, smem, vmem, vmem, vmem, vmem, vmem] + [hbm] * 5,
+        out_specs=(vmem, hbm, hbm, hbm, vmem, vmem, vmem, vmem),
+        scratch_shapes=list(buffers(plan).values()) + list(semaphores(plan).values()),
+        compiler_params=pltpu.CompilerParams(
+            collective_id=0, has_side_effects=True, vmem_limit_bytes=63 * 1000 * 1000),
+        name="whole_step",
+    )(query_lengths, doc_lengths, positives, positives[None], tokens[0], cosines, sines, tile,
+      w_qkv, w_out, w_gate, w_up, w_down)
+    o_tok, o_a, o_gu, o_dn, o_vec, o_q, o_d, o_loss = made
+    outs = pl.pallas_call(
+        functools.partial(finish, plan),
+        out_shape=(
+            shape((1, 1), F32), shape((QPD, D), F32), shape((1, D), F32),
+            shape((1, count, D), F32), shape((shard, 3 * D), F32), shape((shard, D), F32),
+            shape((shard, plan.ff), F32), shape((shard, plan.ff), F32),
+            shape((plan.shard_ff, D), F32),
+        ) + (shape((1, vec), F32),) * 4,
+        in_specs=[vmem] * 8,
+        out_specs=[vmem] * 13,
+        name="finish",
+    )(o_a, o_gu, o_dn, o_vec, o_tok, o_q, o_d, o_loss)
+    return (outs[0].reshape(()),) + tuple(outs[1:9]) + tuple(v.reshape(vec) for v in outs[9:])
+
+
+def fits(plan, towers):
+    line = plan.line
+    return (towers == 2 and plan.groups % 4 == 0 and line & (line - 1) == 0 and line > 1
+            and plan.shard % 16 == 0 and plan.shard_ff % 16 == 0 and plan.stripe % LANES == 0
+            and plan.count == QPD * QLEN)
+
+
 def solution(mesh):
+    groups = mesh.shape[DP]
+
+    def local_step(*args):
+        plan = Plan(groups, args[0].shape[1], args[4].shape[0], args[8].shape[0], args[9].shape[0])
+        if fits(plan, mesh.shape[TOWER]):
+            return on_device_kernel(plan, *args)
+        return on_device(*args)
+
     return jax.shard_map(
-        on_device,
+        local_step,
         mesh=mesh,
         in_specs=(
-            P("tower", "dp", None),
-            P("dp"),
-            P("dp"),
+            P(TOWER, DP, None),
+            P(DP),
+            P(DP),
             P(),
-            P("dp", None),
-            P("dp", None),
-            P("dp", None),
-            P("dp", None),
-            P("dp", None),
-            P("dp"),
-            P("dp"),
-            P("dp"),
-            P("dp"),
+            P(DP, None),
+            P(DP, None),
+            P(DP, None),
+            P(DP, None),
+            P(DP, None),
+            P(DP),
+            P(DP),
+            P(DP),
+            P(DP),
         ),
         out_specs=(
             P(),
-            P("dp", None),
-            P("dp", None),
-            P("tower", "dp", None),
-            P("dp", None),
-            P("dp", None),
-            P("dp", None),
-            P("dp", None),
-            P("dp", None),
-            P("dp"),
-            P("dp"),
-            P("dp"),
-            P("dp"),
+            P(DP, None),
+            P(DP, None),
+            P(TOWER, DP, None),
+            P(DP, None),
+            P(DP, None),
+            P(DP, None),
+            P(DP, None),
+            P(DP, None),
+            P(DP),
+            P(DP),
+            P(DP),
+            P(DP),
         ),
         check_vma=False,
     )

time: 924 us -> 228 us (0.25)
  waiting for transfers between devices: 585 us -> 0 us
  Pallas kernels: 0 us -> 225 us
  blocking collectives: 178 us -> 0 us
  matrix products: 75.5 us -> 0 us
  local copies, waits for them, and re-layouts: 37.5 us -> 0.67 us
  other arithmetic: 26.3 us -> 0.6 us
  between operations: 20 us -> 1.45 us
    reduce_scatter x9 -> x0, waiting for transfers between devices: 311 us -> none  [the longest x1 114 us: on_device(): lax.psum_scatter(gradients[3], 'dp', scatter_dimension=0, tiled=True)]
    pallas_call x0 -> x2, Pallas kernels: none -> 225 us  [the longest x1 221 us: on_device_kernel(): pl.pallas_call(functools.partial(whole_step, plan), out_shape=(shape((cou...]
    all_gather x5 -> x0, waiting for transfers between devices: 178 us -> none  [the longest x1 50.9 us: on_device(): lax.all_gather(w_gate, 'dp', axis=0, tiled=True)]
    unnamed x4 -> x0, blocking collectives: 108 us -> none
    unnamed x16 -> x0, waiting for transfers between devices: 95.3 us -> none
    dot_general x26 -> x0, matrix products: 75.5 us -> none  [the longest x15 61.8 us: product(): return jnp.dot(left, right, preferred_element_type=jnp.float32)]
    all_gather x6 -> x0, blocking collectives: 70.2 us -> none  [the longest x1 40.3 us: on_device(): gathered = lax.all_gather(embedded, ('tower', 'dp'), axis=0, tiled=True)]
    unnamed x174 -> x8, local copies, waits for them, and re-layouts: 26.4 us -> 0.67 us
  transfers between devices with their start and end apart: 15 -> 0, of which waited for: 15 -> 0; matrix products, arithmetic and copies ran while one was open for 10% -> 0% of each run, Pallas kernels for 0% -> 0%
where the time goes in v1:
time: 228 us; the launch traced here: 227 us
  Pallas kernels  225 us (99%)
    pallas_call x1, Pallas kernels, on_device_kernel(): pl.pallas_call(functools.partial(whole_step, plan), out_shape=(shape((cou...  221 us

profile of v1, /device:TPU:0, one launch (start us, length us, event | category | flops | bytes accessed | tf_op | source)
XLA Modules:
  0.0 227.4 jit_solution(14798041941333392314)
XLA Ops:
  1.3 0.0 copy-start.3
  1.3 0.0 copy-start
  1.3 0.0 copy-start.1
  1.3 0.0 copy-start.2
  1.3 0.6 copy-done.3
  1.9 0.0 copy-done
  2.0 0.0 copy-done.1
  2.0 0.0 copy-done.2
  2.0 0.6 fusion.8.refs_7_
  2.6 221.2 %whole_step.1 = (f32[256,768]{1,0:T(8,128)}, bf16[48,3072]{1,0:T(8,128)(2,1)}, bf16[2,48,3072]{2,1,0:T(8,128)(2,1)}, bf16[192,768]{1,0:T(8,128)(2,1)}, f32[8,768...) custom-call(s32[4]{0:T(128)} %refs_0_.1, s32[1]{0:T(128)S(6)} %copy.28.refs_1_, s32[64]{0:T(128)} %refs_2_.1, ...), custom_call_target="tpu_custom_call" | custom-call | tf_op jit(solution)/shard_map/whole_step/pallas_call | solution.py:1504
  223.8 3.5 %finish.1 = (f32[1,1]{1,0:T(1,128)}, f32[4,768]{1,0:T(4,128)}, f32[1,768]{1,0:T(1,128)}, f32[1,256,768]{2,1,0:T(8,128)}, f32[48,2304]{1,0:T(8,128)}, /*index=5*/...) custom-call(bf16[48,3072]{1,0:T(8,128)(2,1)} %get-tuple-element.34.r, ...), custom_call_target="tpu_custom_call" | custom-call | tf_op jit(solution)/shard_map/finish/pallas_call | solution.py:1520
Async XLA Ops:
  1.3 0.7 copy-start.3
  1.3 0.7 copy-start
  1.3 0.7 copy-start.1
  1.3 0.7 copy-start.2

commit v2 on v1

--- a/solution.py
+++ b/solution.py
@@ -330,8 +330,10 @@
     )
 
 
-def dot_t0(left, right):
-    return lax.dot_general(left, right, (((0,), (0,)), ((), ())), preferred_element_type=F32)
+def dot_t0(left, right, precision=None):
+    return lax.dot_general(
+        left, right, (((0,), (0,)), ((), ())), preferred_element_type=F32, precision=precision
+    )
 
 
 def rotary_constants(count):
@@ -384,7 +386,7 @@
         loc=dma((20,)),
         ra=dma((groups, 2)),
         sa_z=dma((2, line)),
-        sa_x=dma((line,)),
+        sa_x=dma((line, 2)),
         sa_y=dma((line, 2)),
         sa_c=dma((line, 2, 2)),
         rg=dma((groups,)),
@@ -400,11 +402,11 @@
         sx=dma((4,)),
         rx=dma((4,)),
         r_doc=dma((groups,)),
-        s_doc=dma((2, groups)),
-        r_query=dma((groups,)),
-        s_query=dma((groups,)),
-        s_loss=dma((1,)),
-        r_loss=dma((1,)),
+        s_doc=dma((groups,)),
+        r_slope=dma((groups,)),
+        s_slope=dma((groups,)),
+        r_query=dma((1,)),
+        s_query=dma((1,)),
         s_ln=dma((line.bit_length() + 2,)),
         r_ln=dma((line.bit_length() + 2,)),
         gd_c=dma((2, line)),
@@ -467,11 +469,10 @@
         embd=v((1, D), F32),
         embq=v((QPD, D), F32),
         dbuf=v((groups, 1, D), F32),
-        qbuf=v((groups, QPD, D), F32),
+        cbuf=v((groups, 1, D), F32),
+        csend=v((groups, 1, D), F32),
+        qrecv=v((QPD, D), F32),
         dflat=v((groups, D), F32),
-        qflat=v((groups * QPD, D), F32),
-        loss=v((8, LANES), F32),
-        lossr=v((8, LANES), F32),
         ln=v((line.bit_length() + 3, 8, D), F32),
         lnr=v((line.bit_length() + 2, 8, D), F32),
         gd=v((line, 2, plan.shard_ff, D), BF),
@@ -562,7 +563,7 @@
         keep.clear()
 
     def got(cond, ref, rsem):
-        do(cond, copy(ref, ref, r.s_loss.at[0], rsem, dev_x).wait_recv)
+        do(cond, copy(ref, ref, r.s_query.at[0], rsem, dev_x).wait_recv)
 
     wa, wg, wd = r.wa, r.wg, r.wd
     out_w = half_a - 3 * D // 2
@@ -625,9 +626,11 @@
                 got_a(there, zz, x, c, t)
             send_a(both(there, on), r.sa_z.at[way, zz], zz, x, t, dev_z(nxt))
             if step or way == 0:
-                send_a(there, r.sa_x.at[zz], zz, x, t, dev_x)
+                send_a(there, r.sa_x.at[zz, t], zz, x, t, dev_x)
                 if step:
                     send_a(there, r.sa_y.at[zz, x], zz, x, t, dev_y)
+                else:
+                    send_a(None, r.sa_x.at[zz, 1 - t], zz, x, 1 - t, dev_x)
                 send_a(there, r.sa_c.at[zz, x, t], zz, x, t, dev_c)
         if step == 0:
             send_a(None, r.sa_c.at[z, x, 1 - t], z, x, 1 - t, dev_c)
@@ -638,12 +641,16 @@
     def a_cross(step):
         for zz, there, _, _, _ in around(step):
             got_a(there, zz, 1 - x, c, t)
-            send_a(there, r.sa_y.at[zz, 1 - x], zz, 1 - x, t, dev_y)
+            if step:
+                send_a(there, r.sa_y.at[zz, 1 - x], zz, 1 - x, t, dev_y)
+            else:
+                got_a(None, zz, 1 - x, c, 1 - t)
+                send_a(None, r.sa_c.at[zz, 1 - x, 1 - t], zz, 1 - x, 1 - t, dev_c)
             send_a(there, r.sa_c.at[zz, 1 - x, t], zz, 1 - x, t, dev_c)
 
     def a_tower(step):
-        for zz, there, _, _, _ in around(step):
-            for xx in (x, 1 - x)[1 if step == 0 else 0:]:
+        for zz, there, _, _, _ in sides(step):
+            for xx in (x, 1 - x):
                 got_a(there, zz, xx, c, 1 - t)
                 send_a(there, r.sa_c.at[zz, xx, 1 - t], zz, xx, 1 - t, dev_c)
 
@@ -660,14 +667,16 @@
     def got_g(cond, zz, xx, cc):
         got(cond, wg.at[zz, xx, cc], r.rg.at[at(zz, xx, cc)])
 
-    def g_round(step):
+    def g_line(step):
         for zz, there, on, nxt, way in sides(step):
             if step:
                 got_g(there, zz, x, c)
             send_g(both(there, on), r.sg_z.at[way, zz], zz, x, dev_z(nxt))
-            if step or way == 0:
-                send_g(there, r.sg_x.at[zz], zz, x, dev_x)
-                send_g(there, r.sg_c.at[zz, x], zz, x, dev_c)
+
+    def g_spread(step):
+        for zz, there, _, _, _ in around(step):
+            send_g(there, r.sg_x.at[zz], zz, x, dev_x)
+            send_g(there, r.sg_c.at[zz, x], zz, x, dev_c)
 
     def g_cross(step):
         for zz, there, _, _, _ in around(step):
@@ -720,7 +729,6 @@
         return carry
 
     a_round(0)
-    d_cross()
     lax.fori_loop(0, groups, v_send, 0)
 
     tok = r.tok
@@ -734,7 +742,7 @@
     place = cols - seg * (quarter * (1 - t))
     apart = ((rows >> shift) - seg) * (1 - t)
     seen = both(apart == 0, place < limit)
-    r.hide[...] = jnp.where(seen, 0.0, 1.0)
+    r.hide[...] = jnp.where(seen, 0.0, -1e30)
     for s in range(QPD):
         part = pl.ds(s * quarter, quarter)
         length = jnp.full((quarter, 1), r.qlen[s] * (1 - t) + r.dlen[0] * t, jnp.int32)
@@ -771,20 +779,35 @@
         split = 3 * D // 2 // LANES
         return aligned(jnp.where(u < split, u, u + out_w // LANES) * LANES, LANES)
 
+    def widen_vec(j, acc):
+        row = lax.broadcasted_iota(jnp.int32, (LANES, D), 0)
+        col = lax.broadcasted_iota(jnp.int32, (LANES, D), 1)
+        pick = jnp.where(col == row + j * plan.vec, 1.0, 0.0).astype(BF)
+        return acc + jnp.dot(r.vt[j], pick, preferred_element_type=F32)
+
+    transpose_into(r.tokt, tok, D)
     a_round(1)
-    g_round(0)
-    transpose_into(r.tokt, tok, D)
+    a_cross(0)
     for step in range(2, line):
         a_round(step)
-    for step in range(line):
-        a_cross(step)
+        if step == 2:
+            g_line(0)
+        a_cross(step - 1)
+    g_spread(0)
+    d_cross()
+    lax.fori_loop(0, groups, v_wait, 0)
+    r.vec[...] = lax.fori_loop(0, groups, widen_vec, jnp.zeros((16, D), F32))
+    a_tower(1)
+    a_cross(line - 1)
+    g_line(1)
+    g_spread(1)
     d_round(0)
-    g_round(1)
-    for step in range(line):
+    for step in range(2, line):
         a_tower(step)
-    g_round(2)
     a_sibling()
     pairs = D // LANES
+
+    scale = HEAD ** (-0.5)
 
     def project(p, carry):
         w = jnp.concatenate(
@@ -792,12 +815,10 @@
         )
         packed = jnp.dot(tok[...], w, preferred_element_type=F32)
         o = aligned(p * LANES, LANES)
-        r.qkv[:, pl.ds(o, LANES)] = turn(packed[:, :LANES]).astype(BF)
+        r.qkv[:, pl.ds(o, LANES)] = (turn(packed[:, :LANES]) * scale).astype(BF)
         r.qkv[:, pl.ds(D + o, LANES)] = turn(packed[:, LANES : 2 * LANES]).astype(BF)
         r.qkv[:, pl.ds(2 * D + o, LANES)] = packed[:, 2 * LANES :].astype(BF)
         return carry
-
-    scale = HEAD ** (-0.5)
 
     def triple(p):
         o = aligned(p * LANES, LANES)
@@ -810,8 +831,7 @@
         q2, k2, v2 = triple(p)
         outs = []
         for h in range(2):
-            scores = dot_tt(only(h, q2), k2) * scale
-            scores = jnp.where(r.hide[...] > 0.5, -1e30, scores)
+            scores = dot_tt(only(h, q2), k2) + r.hide[...]
             grown = jnp.exp(scores - jnp.max(scores, -1, keepdims=True))
             probs = grown * (1.0 / jnp.sum(grown, -1, keepdims=True))
             r.probs[2 * p + h] = probs
@@ -821,26 +841,17 @@
         return carry
 
     lax.fori_loop(0, pairs, project, 0)
+    g_line(2)
+    g_cross(0)
+    g_spread(2)
+    lax.fori_loop(0, pairs // 2, attend, 0)
+    for step in range(3, line):
+        g_line(step)
     d_round(1)
+    g_cross(1)
     for step in range(3, line):
-        g_round(step)
-    for step in range(line):
-        g_cross(step)
-    lax.fori_loop(0, pairs // 2, attend, 0)
-    d_round(2)
+        g_spread(step)
     lax.fori_loop(pairs // 2, pairs, attend, 0)
-    for step in range(3, line):
-        d_round(step)
-
-    lax.fori_loop(0, groups, v_wait, 0)
-
-    def widen_vec(j, acc):
-        row = lax.broadcasted_iota(jnp.int32, (LANES, D), 0)
-        col = lax.broadcasted_iota(jnp.int32, (LANES, D), 1)
-        pick = jnp.where(col == row + j * plan.vec, 1.0, 0.0).astype(BF)
-        return acc + jnp.dot(r.vt[j], pick, preferred_element_type=F32)
-
-    r.vec[...] = lax.fori_loop(0, groups, widen_vec, jnp.zeros((16, D), F32))
 
     for h in range(2):
         part = jnp.dot(r.mixed[...], wide(wa, h * half_a + 3 * D // 2, out_w),
@@ -877,8 +888,9 @@
 
     swap_rows(0, r.feed.at[mine], r.feed.at[mine])
     transpose_into(r.mixt, r.mixed, D)
-    got_rows(0, r.feed.at[theirs])
-    transpose_into(r.feedt, r.feed, D)
+    for step in range(2, line):
+        g_cross(step)
+        d_round(step)
     g_sibling()
 
     step_ff = 2 * LANES
@@ -894,6 +906,7 @@
         r.hidt[pl.ds(o, step_ff), :] = hidden.T
         return carry
 
+    got_rows(0, r.feed.at[theirs])
     lax.fori_loop(0, half_ff // step_ff, gated, 0)
     d_sibling()
 
@@ -915,6 +928,7 @@
     down(theirs, keep_send)
     swap_rows(1, r.bsend, r.brecv)
     down(mine, keep_own)
+    transpose_into(r.feedt, r.feed, D)
     got_rows(1, r.brecv)
 
     r.pool[...] = jnp.zeros((8, D), F32)
@@ -942,64 +956,44 @@
     shrink = lax.rsqrt(jnp.sum(pooled * pooled, -1, keepdims=True) + 1e-06)
     r.emb[...] = pooled * shrink
 
-    @pl.when(t == 0)
-    def _():
-        r.embq[...] = r.emb[0:QPD, :]
-
+    best = exact_product_accuracy
+    r.dpool[...] = jnp.zeros((8, D), F32)
+    r.ln[0] = jnp.zeros((8, D), F32)
+
+    def to_all(tower, src, dst, ssem, rsem):
         def give(step, carry):
             j = (me + step) % groups
-            copy(r.embq, r.qbuf.at[me], r.s_query.at[j], r.r_query.at[me],
-                 {TOWER: 1, DP: j}).start()
+            copy(src(j), dst.at[me], ssem.at[j], rsem.at[me], {TOWER: tower, DP: j}).start()
             return carry
 
+        lax.fori_loop(0, groups, give, 0)
+
+    def from_all(dst, ssem, rsem):
         def take(j, carry):
-            copy(r.embd, r.dbuf.at[j], r.s_doc.at[0, 0], r.r_doc.at[j],
-                 {TOWER: 1, DP: j}).wait_recv()
+            copy(dst.at[j], dst.at[j], ssem.at[j], rsem.at[j], dev_x).wait_recv()
             return carry
 
-        lax.fori_loop(0, groups, give, 0)
         lax.fori_loop(0, groups, take, 0)
 
     @pl.when(t == 1)
     def _():
         r.embd[...] = r.emb[0:1, :]
         r.dbuf[me] = r.emb[0:1, :]
-
-        def give(step, carry):
-            j = (me + step) % groups
-            copy(r.embd, r.dbuf.at[me], r.s_doc.at[0, j], r.r_doc.at[me],
-                 {TOWER: 0, DP: j}).start()
-
-            @pl.when(j != me)
-            def _():
-                copy(r.embd, r.dbuf.at[me], r.s_doc.at[1, j], r.r_doc.at[me],
-                     {TOWER: 1, DP: j}).start()
-
-            return carry
-
-        def take(j, carry):
-            copy(r.embq, r.qbuf.at[j], r.s_query.at[0], r.r_query.at[j],
-                 {TOWER: 0, DP: j}).wait_recv()
-
-            @pl.when(j != me)
-            def _():
-                copy(r.embd, r.dbuf.at[j], r.s_doc.at[0, 0], r.r_doc.at[j],
-                     {TOWER: 0, DP: j}).wait_recv()
-
-            return carry
-
-        lax.fori_loop(0, groups, give, 0)
-        lax.fori_loop(0, groups, take, 0)
-
-    for j in range(groups):
-        r.dflat[pl.ds(j, 1), :] = r.dbuf[j]
-    best = exact_product_accuracy
-    r.dpool[...] = jnp.zeros((8, D), F32)
+        to_all(0, lambda j: r.embd, r.dbuf, r.s_doc, r.r_doc)
+        from_all(r.cbuf, r.s_slope, r.r_slope)
+        total = r.cbuf[0]
+        for j in range(1, groups):
+            total = total + r.cbuf[j]
+        r.dpool[0:1, :] = total
 
     @pl.when(t == 0)
     def _():
-        docs = r.dflat[...]
-        logits = dot_tt(r.embq[...], docs, best) / contrast_sharpness_factor
+        r.embq[...] = r.emb[0:QPD, :]
+        from_all(r.dbuf, r.s_doc, r.r_doc)
+        for j in range(groups):
+            r.dflat[pl.ds(j, 1), :] = r.dbuf[j]
+        docs, queries = r.dflat[...], r.embq[...]
+        logits = dot_tt(queries, docs, best) / contrast_sharpness_factor
         peak = jnp.max(logits, -1, keepdims=True)
         lse = peak + jnp.log(jnp.sum(jnp.exp(logits - peak), -1, keepdims=True))
         col = lax.broadcasted_iota(jnp.int32, (QPD, groups), 1)
@@ -1009,24 +1003,14 @@
             label = jnp.where(row == s, r.pos[me * QPD + s], label)
         hot = jnp.where(col == label, 1.0, 0.0)
         slope = (jnp.exp(logits - lse) - hot) / contrast_sharpness_factor
+        back = dot_t0(slope, queries, best)
+        for j in range(groups):
+            r.csend[j] = back[j : j + 1, :]
+        to_all(1, lambda j: r.csend.at[j], r.cbuf, r.s_slope, r.r_slope)
         r.dpool[0:QPD, :] = jnp.dot(slope, docs, preferred_element_type=F32, precision=best)
-
-    @pl.when(t == 1)
-    def _():
-        for j in range(groups):
-            r.qflat[pl.ds(j * QPD, QPD), :] = r.qbuf[j]
-        docs, queries = r.dflat[...], r.qflat[...]
-        logits = dot_tt(docs, queries, best) / contrast_sharpness_factor
-        peak = jnp.max(logits, 0, keepdims=True)
-        lse = peak + jnp.log(jnp.sum(jnp.exp(logits - peak), 0, keepdims=True))
-        row = lax.broadcasted_iota(jnp.int32, (groups, groups * QPD), 0)
-        hit = row == r.posv[...]
-        picked = jnp.sum(jnp.where(hit, logits, 0.0), 0, keepdims=True)
-        total = jnp.sum(lse - picked, -1, keepdims=True)
-        r.loss[...] = jnp.broadcast_to(total / (groups * QPD), (8, LANES))
-        slope = (jnp.exp(logits - lse) - jnp.where(hit, 1.0, 0.0)) / contrast_sharpness_factor
-        line_of = jnp.sum(jnp.where(row == me, slope, 0.0), 0, keepdims=True)
-        r.dpool[0:1, :] = jnp.dot(line_of, queries, preferred_element_type=F32, precision=best)
+        picked = jnp.sum(jnp.where(hot > 0.5, logits, 0.0), -1, keepdims=True)
+        total = jnp.sum(lse - picked, 0, keepdims=True)
+        r.ln[0] = jnp.where(row8 == 4, total, 0.0)
 
     slope = r.dpool[...]
     emb = r.emb[...]
@@ -1058,8 +1042,9 @@
     gain_two, bias_two = lax.fori_loop(0, blocks, norm_two_back, (zero_row, zero_row))
     swap_rows(2, r.dbr.at[mine], r.dbr.at[mine])
 
-    send(t == 1, copy(r.loss, r.lossr, r.s_loss.at[0], r.r_loss.at[0], dev_y), tail)
-    r.ln[0] = jnp.where(row8 == 2, gain_two, 0.0) + jnp.where(row8 == 3, bias_two, 0.0)
+    send(t == 0, copy(r.embq, r.qrecv, r.s_query.at[0], r.r_query.at[0], dev_y), tail)
+    r.ln[0] = (r.ln[0] + jnp.where(row8 == 2, gain_two, 0.0)
+               + jnp.where(row8 == 3, bias_two, 0.0))
 
     def hidden_back(rows_of):
         def body(j, carry):
@@ -1076,9 +1061,6 @@
 
         lax.fori_loop(0, line, body, 0)
 
-    hidden_back(mine)
-    got_rows(2, r.dbr.at[theirs])
-
     def along(step):
         for s in range(1, line):
             yield line - s, both(z == step, z < line - s), z + 1, 0
@@ -1091,14 +1073,16 @@
             total = total + ref[...].astype(F32)
         return total
 
-    def line_step(step, parts, sem, slot):
-        for dest, cond, nxt, way in along(step):
+    def line_step(step, parts, sem, slot, only_at=None):
+        for k, (dest, cond, nxt, way) in enumerate(along(step)):
+            if only_at is not None and k % (line - 1) != only_at:
+                continue
             into = slot(dest + 1 if way == 0 else dest)
             refs = parts(dest)
 
             def move(into=into, refs=refs, dest=dest, way=way):
                 if step:
-                    copy(into, into, r.s_loss.at[0], sem(1, way, dest), dev_x).wait_recv()
+                    copy(into, into, r.s_query.at[0], sem(1, way, dest), dev_x).wait_recv()
                     refs[0][...] = added(refs + (into,)).astype(BF)
                 else:
                     refs[0][...] = added(refs).astype(BF)
@@ -1114,7 +1098,7 @@
                 refs = parts(z)
                 for way in ways:
                     into = slot(z + 1 if way == 0 else z)
-                    copy(into, into, r.s_loss.at[0], sem(1, way, z), dev_x).wait_recv()
+                    copy(into, into, r.s_query.at[0], sem(1, way, z), dev_x).wait_recv()
                     refs = refs + (into,)
                 put[...] = added(refs).astype(BF)
 
@@ -1122,9 +1106,16 @@
 
     gd = r.gd
 
+    def down_half(s, rows_of):
+        return jnp.dot(r.hidt[pl.ds(s * stripe, stripe), rows_of], r.dbr[rows_of, :],
+                       preferred_element_type=F32)
+
+    def down_own(s):
+        gd[s] = down_half(s, mine).astype(BF).reshape(2, shard_ff, D)
+
     def down_grad(s):
-        gd[s] = jnp.dot(r.hidt[pl.ds(s * stripe, stripe), :], r.dbr[...],
-                        preferred_element_type=F32).astype(BF).reshape(2, shard_ff, D)
+        val = down_half(s, theirs) + gd[s].reshape(stripe, D).astype(F32)
+        gd[s] = val.astype(BF).reshape(2, shard_ff, D)
         send(None, copy(gd.at[s, 1 - c], r.gd_rc.at[s], r.gd_c.at[0, s],
                         r.gd_c.at[1, s], dev_c), tail)
 
@@ -1135,8 +1126,8 @@
         for s in range(line):
             got(None, r.gd_rc.at[s], r.gd_c.at[1, s])
 
-    def down_line(step):
-        line_step(step, down_parts, lambda *i: r.gd_z.at[i], lambda k: r.gd_rz.at[k])
+    def down_line(step, only_at=None):
+        line_step(step, down_parts, lambda *i: r.gd_z.at[i], lambda k: r.gd_rz.at[k], only_at)
 
     def down_end():
         line_end(down_parts, lambda *i: r.gd_z.at[i], lambda k: r.gd_rz.at[k], r.gd_f)
@@ -1151,7 +1142,7 @@
 
     def down_out():
         def total():
-            copy(r.gd_rx, r.gd_rx, r.s_loss.at[0], r.gd_x.at[1], dev_x).wait_recv()
+            copy(r.gd_rx, r.gd_rx, r.s_query.at[0], r.gd_x.at[1], dev_x).wait_recv()
             r.gd_f[...] = added((r.gd_f, r.gd_rx)).astype(BF)
 
         do(x == t, total)
@@ -1161,9 +1152,17 @@
     gg = r.gg
     part_gu = ff // 4
 
+    def gate_half(k, rows_of):
+        return jnp.dot(r.feedt[:, rows_of], r.dgu[rows_of, pl.ds(k * part_gu, part_gu)],
+                       preferred_element_type=F32)
+
+    def gate_own(k):
+        gg[:, :, :, :, pl.ds(k * part_gu, part_gu)] = gate_half(k, mine).astype(BF).reshape(
+            line, 2, 2, shard, part_gu)
+
     def gate_grad(k):
         span = pl.ds(k * part_gu, part_gu)
-        val = jnp.dot(r.feedt[...], r.dgu[:, span], preferred_element_type=F32)
+        val = gate_half(k, theirs) + gg[:, :, :, :, span].reshape(groups * shard, part_gu).astype(F32)
         gg[:, :, :, :, span] = val.astype(BF).reshape(line, 2, 2, shard, part_gu)
         send(None, copy(gg.at[:, :, 1 - c, :, span], r.gg_rc.at[:, :, :, span],
                         r.gg_c.at[0, k], r.gg_c.at[1, k], dev_c), tail)
@@ -1271,6 +1270,13 @@
     def back_own(span, val):
         r.bown[:, span] = val
 
+    hidden_back(mine)
+    feed_back(mine, back_own)
+    for s in range(line):
+        down_own(s)
+    for k in range(4):
+        gate_own(k)
+    got_rows(2, r.dbr.at[theirs])
     for s in range(line):
         down_grad(s)
     hidden_back(theirs)
@@ -1281,23 +1287,13 @@
     gate_grad(0)
     gate_grad(1)
     gate_cross(0)
-    down_line(1)
     gate_grad(2)
     gate_cross(1)
-    gate_line(0, 0)
     gate_grad(3)
+    settle(pending)
     gate_cross(2)
-    for step in range(2, line - 1):
-        down_line(step)
-    gate_line(1, 0)
-    gate_line(0, 1)
-    feed_back(mine, back_own)
     gate_cross(3)
-    down_end()
-    settle(pending)
-    gate_line(2, 0)
-    gate_line(1, 1)
-    gate_line(0, 2)
+    down_line(1, 0)
     got_rows(3, r.drecv)
 
     def norm_one_back(b, sums):
@@ -1317,7 +1313,7 @@
     r.ln[0] = (r.ln[0] + jnp.where(row8 == 0, gain_one, 0.0)
                   + jnp.where(row8 == 1, bias_one, 0.0))
 
-    ln_peers = [dev_c, dev_x, dev_y]
+    ln_peers = [dev_y, dev_c, dev_x]
     for bit in range(line.bit_length() - 1):
         apart = 1 << bit
         ln_peers.append(dev_z(z + apart * (1 - 2 * ((z // apart) % 2))))
@@ -1333,25 +1329,12 @@
 
     dqkv = r.dgu.at[pl.ds(0, count), pl.ds(0, 3 * D)]
     dmix = r.dgu.at[pl.ds(count, count), pl.ds(0, D)]
-
-    ln_send(0)
-    store_a(3, r.mixt, [r.datt[:, pl.ds(h * out_w, out_w)] for h in range(2)])
 
     def mixed_back(j, carry):
         val = sum(dot_tt(r.datt[:, pl.ds(h * out_w, out_w)],
                          rows_of_weight(wa, j, h * half_a + third, out_w)) for h in range(2))
         dmix[:, pl.ds(aligned(j * some, LANES), some)] = val.astype(BF)
         return carry
-
-    lax.fori_loop(0, line // 2, mixed_back, 0)
-    ln_add(0)
-    ln_send(1)
-    tower_a(3)
-    gate_line(3, 0)
-    gate_line(2, 1)
-    gate_line(1, 2)
-    down_out()
-    gate_end(0)
 
     def attend_back(p, carry):
         q2, k2, v2 = triple(p)
@@ -1367,38 +1350,9 @@
                           dot_t0(dscores, q2), dot_t0(probs.astype(BF), dm2)))
         dq, dk, dv = (jnp.where(first_head, a, b) for a, b in zip(*parts))
         dqkv[:, pl.ds(o, LANES)] = turn_back(dq * scale).astype(BF)
-        dqkv[:, pl.ds(D + o, LANES)] = turn_back(dk * scale).astype(BF)
+        dqkv[:, pl.ds(D + o, LANES)] = turn_back(dk).astype(BF)
         dqkv[:, pl.ds(2 * D + o, LANES)] = dv.astype(BF)
         return carry
-
-    lax.fori_loop(0, 2, attend_back, 0)
-    ln_add(1)
-    ln_send(2)
-    gate_line(3, 1)
-    gate_line(2, 2)
-    gate_end(1)
-    lax.fori_loop(2, 4, attend_back, 0)
-    ln_add(2)
-    ln_send(3)
-    cross_a(3)
-    gate_line(3, 2)
-    gate_end(2)
-    lax.fori_loop(4, pairs, attend_back, 0)
-    ln_add(3)
-    ln_send(4)
-    line_a(3, 0)
-    gate_end(3)
-    for k in range(3):
-        store_a(k, r.tokt, [dqkv[:, pl.ds(h * third + k * part_a, part_a)]
-                               for h in range(2)])
-    line_a(3, 1)
-    for k in range(3):
-        tower_a(k)
-    for k in range(4, last):
-        ln_add(k)
-        if k + 1 < last:
-            ln_send(k + 1)
-    r.o_vec[...] = r.ln[last]
 
     def token_back(j, carry):
         val = sum(dot_tt(dqkv[:, pl.ds(h * third, third)],
@@ -1407,53 +1361,91 @@
         r.o_tok[:, span] = r.n1[:, span] + val
         return carry
 
+    ln_send(0)
+    store_a(3, r.mixt, [r.datt[:, pl.ds(h * out_w, out_w)] for h in range(2)])
+    lax.fori_loop(0, line // 2, mixed_back, 0)
+    ln_add(0)
+    ln_send(1)
+    tower_a(3)
+    gate_line(0, 0)
+    lax.fori_loop(0, 2, attend_back, 0)
+    down_line(1, 1)
+    lax.fori_loop(2, 4, attend_back, 0)
+    gate_line(0, 1)
+    gate_line(1, 0)
+    down_line(2, 0)
+    lax.fori_loop(4, pairs, attend_back, 0)
+    for k in range(3):
+        store_a(k, r.tokt, [dqkv[:, pl.ds(h * third + k * part_a, part_a)] for h in range(2)])
+    for k in range(3):
+        tower_a(k)
+    ln_add(1)
+    gate_line(0, 2)
+    gate_line(1, 1)
     lax.fori_loop(0, line // 2, token_back, 0)
+    gate_line(2, 0)
+    cross_a(3)
+    down_end()
+    gate_end(0)
+    gate_line(1, 2)
+    gate_line(2, 1)
+    gate_line(3, 0)
+    line_a(3, 0)
+    cross_a(0)
+    gate_line(2, 2)
+    gate_end(1)
+    down_out()
+    gate_line(3, 1)
+    line_a(3, 1)
+    line_a(0, 0)
+    cross_a(1)
+    gate_end(2)
+    gate_line(3, 2)
     line_a(3, 2)
-    for k in range(3):
-        cross_a(k)
+    line_a(0, 1)
+    line_a(1, 0)
+    gate_end(3)
+    line_a(0, 2)
     end_a(3)
-    for step in range(line - 1):
-        for k in range(3):
-            line_a(k, step)
-    for k in range(3):
-        end_a(k)
+    cross_a(2)
+    ln_send(2)
+    line_a(1, 1)
+    end_a(0)
+    ln_add(2)
+    line_a(2, 0)
+    ln_send(3)
+    line_a(1, 2)
+    line_a(2, 1)
+    end_a(1)
+    for k in range(3, last):
+        ln_add(k)
+        if k + 1 < last:
+            ln_send(k + 1)
+    line_a(2, 2)
+    end_a(2)
+
+    r.o_vec[...] = r.ln[last]
+    r.o_loss[...] = r.ln[last][:, 0:LANES] * (1.0 / (groups * QPD))
+
+    r.o_d[...] = r.dbuf[me]
+
+    def sent(ssem):
+        def body(j, carry):
+            copy(r.embd, r.embd, ssem.at[j], r.r_query.at[0], dev_x).wait_send()
+            return carry
+
+        lax.fori_loop(0, groups, body, 0)
 
     @pl.when(t == 0)
     def _():
-        got(None, r.lossr, r.r_loss.at[0])
-        r.o_loss[...] = r.lossr[...]
         r.o_q[...] = r.embq[...]
+        sent(r.s_slope)
 
     @pl.when(t == 1)
     def _():
-        r.o_loss[...] = r.loss[...]
-        r.o_q[...] = r.qbuf[me]
-
-    r.o_d[...] = r.dbuf[me]
-
-    @pl.when(t == 0)
-    def _():
-        def sent(j, carry):
-            copy(r.embq, r.qbuf.at[me], r.s_query.at[j], r.r_query.at[me],
-                 {TOWER: 1, DP: j}).wait_send()
-            return carry
-
-        lax.fori_loop(0, groups, sent, 0)
-
-    @pl.when(t == 1)
-    def _():
-        def sent(j, carry):
-            copy(r.embd, r.dbuf.at[me], r.s_doc.at[0, j], r.r_doc.at[me],
-                 {TOWER: 0, DP: j}).wait_send()
-
-            @pl.when(j != me)
-            def _():
-                copy(r.embd, r.dbuf.at[me], r.s_doc.at[1, j], r.r_doc.at[me],
-                     {TOWER: 1, DP: j}).wait_send()
-
-            return carry
-
-        lax.fori_loop(0, groups, sent, 0)
+        got(None, r.qrecv, r.r_query.at[0])
+        r.o_q[...] = r.qrecv[...]
+        sent(r.s_doc)
 
     got(x != t, r.o_dn, r.gd_y.at[1])
     for k in range(4):
@@ -1481,7 +1473,7 @@
     o_tok[0] = tok_ref[...]
     o_q[...] = q_ref[...]
     o_d[...] = d_ref[...]
-    o_loss[...] = loss_ref[0:1, 0:1]
+    o_loss[...] = loss_ref[4:5, 0:1]
     first = lax.axis_index(DP) * plan.vec
     row = lax.broadcasted_iota(jnp.int32, (D, LANES), 0)
     col = lax.broadcasted_iota(jnp.int32, (D, LANES), 1)

time: 228 us -> 186 us (0.82)
  Pallas kernels: 225 us -> 184 us
    pallas_call x1, Pallas kernels: 221 us -> 180 us  [on_device_kernel(): pl.pallas_call(functools.partial(whole_step, plan), out_shape=(shape((cou...]
where the time goes in v2:
time: 186 us
  Pallas kernels  184 us (99%)
    pallas_call x1, Pallas kernels, on_device_kernel(): pl.pallas_call(functools.partial(whole_step, plan), out_shape=(shape((cou...  180 us

profile of v2, /device:TPU:0, one launch (start us, length us, event | category | flops | bytes accessed | tf_op | source)
XLA Modules:
  0.0 186.3 jit_solution(1568767800119352276)
XLA Ops:
  1.3 0.0 copy-start.3
  1.3 0.0 copy-start
  1.3 0.0 copy-start.1
  1.3 0.0 copy-start.2
  1.3 0.6 copy-done.3
  1.9 0.0 copy-done
  2.0 0.0 copy-done.1
  2.0 0.0 copy-done.2
  2.0 0.6 fusion.8.refs_7_
  2.6 180.1 %whole_step.1 = (f32[256,768]{1,0:T(8,128)}, bf16[48,3072]{1,0:T(8,128)(2,1)}, bf16[2,48,3072]{2,1,0:T(8,128)(2,1)}, bf16[192,768]{1,0:T(8,128)(2,1)}, f32[8,768...) custom-call(s32[4]{0:T(128)} %refs_0_.1, s32[1]{0:T(128)S(6)} %copy.28.refs_1_, s32[64]{0:T(128)} %refs_2_.1, ...), custom_call_target="tpu_custom_call" | custom-call | tf_op jit(solution)/shard_map/whole_step/pallas_call | solution.py:1496
  182.7 3.5 %finish.1 = (f32[1,1]{1,0:T(1,128)}, f32[4,768]{1,0:T(4,128)}, f32[1,768]{1,0:T(1,128)}, f32[1,256,768]{2,1,0:T(8,128)}, f32[48,2304]{1,0:T(8,128)}, /*index=5*/...) custom-call(bf16[48,3072]{1,0:T(8,128)(2,1)} %get-tuple-element.34.r, ...), custom_call_target="tpu_custom_call" | custom-call | tf_op jit(solution)/shard_map/finish/pallas_call | solution.py:1512
Async XLA Ops:
  1.3 0.7 copy-start.3
  1.3 0.7 copy-start
  1.3 0.7 copy-start.1
  1.3 0.7 copy-start.2

commit v3 on v2

--- a/solution.py
+++ b/solution.py
@@ -383,7 +383,7 @@
     dma = pltpu.SemaphoreType.DMA
     chunks_gu, chunks_a = 4, 4
     return dict(
-        loc=dma((20,)),
+        loc=dma((24,)),
         ra=dma((groups, 2)),
         sa_z=dma((2, line)),
         sa_x=dma((line, 2)),
@@ -399,6 +399,8 @@
         sd_c=dma((line,)),
         rv=dma((groups,)),
         sv=dma((groups,)),
+        s_back=dma((line,)),
+        r_back=dma((line,)),
         sx=dma((4,)),
         rx=dma((4,)),
         r_doc=dma((groups,)),
@@ -575,9 +577,11 @@
         local.append((cond, what))
 
     third = 3 * D // 2
+    half_d = D // 2
     for h in range(2):
-        near(r.i_qkv.at[:, pl.ds(h * third, third)],
-             wa.at[z, x, c, :, pl.ds(h * half_a, third)])
+        for k in range(3):
+            near(r.i_qkv.at[:, pl.ds(k * D + h * half_d, half_d)],
+                 wa.at[z, x, c, :, pl.ds(h * half_a + k * half_d, half_d)])
         near(r.i_out.at[:, pl.ds(h * out_w, out_w)],
              wa.at[z, x, c, :, pl.ds(h * half_a + third, out_w)])
     near(r.i_down, wd.at[z, c], x == t)
@@ -630,7 +634,7 @@
                 if step:
                     send_a(there, r.sa_y.at[zz, x], zz, x, t, dev_y)
                 else:
-                    send_a(None, r.sa_x.at[zz, 1 - t], zz, x, 1 - t, dev_x)
+                    send_a(x != t, r.sa_x.at[zz, 1 - t], zz, x, 1 - t, dev_x)
                 send_a(there, r.sa_c.at[zz, x, t], zz, x, t, dev_c)
         if step == 0:
             send_a(None, r.sa_c.at[z, x, 1 - t], z, x, 1 - t, dev_c)
@@ -641,24 +645,23 @@
     def a_cross(step):
         for zz, there, _, _, _ in around(step):
             got_a(there, zz, 1 - x, c, t)
-            if step:
-                send_a(there, r.sa_y.at[zz, 1 - x], zz, 1 - x, t, dev_y)
-            else:
-                got_a(None, zz, 1 - x, c, 1 - t)
-                send_a(None, r.sa_c.at[zz, 1 - x, 1 - t], zz, 1 - x, 1 - t, dev_c)
+            send_a(there if step else x == t, r.sa_y.at[zz, 1 - x], zz, 1 - x, t, dev_y)
             send_a(there, r.sa_c.at[zz, 1 - x, t], zz, 1 - x, t, dev_c)
 
     def a_tower(step):
+        if step == 0:
+            got_a(None, z, 1 - x, c, 1 - t)
+            send_a(None, r.sa_c.at[z, 1 - x, 1 - t], z, 1 - x, 1 - t, dev_c)
+            return
         for zz, there, _, _, _ in sides(step):
             for xx in (x, 1 - x):
                 got_a(there, zz, xx, c, 1 - t)
                 send_a(there, r.sa_c.at[zz, xx, 1 - t], zz, xx, 1 - t, dev_c)
 
-    def a_sibling():
+    def a_sibling(h):
         for zz in range(line):
             for xx in range(2):
-                for h in range(2):
-                    got_a(None, zz, xx, 1 - c, h)
+                got_a(None, zz, xx, 1 - c, h)
 
     def send_g(cond, sem, zz, xx, dev):
         ref = wg.at[zz, xx, c]
@@ -698,15 +701,19 @@
     def d_cross():
         send_d(x == t, r.sd_x.at[0], z, dev_x)
 
-    def d_round(step):
+    def d_start():
+        got_d(x != t, z, c)
+        for zz, _, on, nxt, way in sides(0):
+            send_d(on, r.sd_z.at[way, zz], zz, dev_z(nxt))
+        send_d(None, r.sd_c.at[z], z, dev_c)
+
+    def d_round(step, ends):
         for zz, there, on, nxt, way in sides(step):
-            if step:
-                got_d(there, zz, c)
-            elif way == 0:
-                got_d(x != t, z, c)
-            send_d(both(there, on), r.sd_z.at[way, zz], zz, dev_z(nxt))
-            if step or way == 0:
-                send_d(there, r.sd_c.at[zz], zz, dev_c)
+            cond = both(there, jnp.logical_not(on) if ends else on)
+            got_d(cond, zz, c)
+            if not ends:
+                send_d(cond, r.sd_z.at[way, zz], zz, dev_z(nxt))
+            send_d(cond, r.sd_c.at[zz], zz, dev_c)
 
     def d_sibling():
         for zz in range(line):
@@ -775,50 +782,36 @@
     def wide(ref, lo, n):
         return ref[:, :, :, :, pl.ds(lo, n)].reshape(groups * shard, n)
 
-    def qkv_lane(u):
-        split = 3 * D // 2 // LANES
-        return aligned(jnp.where(u < split, u, u + out_w // LANES) * LANES, LANES)
-
-    def widen_vec(j, acc):
-        row = lax.broadcasted_iota(jnp.int32, (LANES, D), 0)
-        col = lax.broadcasted_iota(jnp.int32, (LANES, D), 1)
-        pick = jnp.where(col == row + j * plan.vec, 1.0, 0.0).astype(BF)
-        return acc + jnp.dot(r.vt[j], pick, preferred_element_type=F32)
-
-    transpose_into(r.tokt, tok, D)
-    a_round(1)
-    a_cross(0)
-    for step in range(2, line):
-        a_round(step)
-        if step == 2:
-            g_line(0)
-        a_cross(step - 1)
-    g_spread(0)
-    d_cross()
-    lax.fori_loop(0, groups, v_wait, 0)
-    r.vec[...] = lax.fori_loop(0, groups, widen_vec, jnp.zeros((16, D), F32))
-    a_tower(1)
-    a_cross(line - 1)
-    g_line(1)
-    g_spread(1)
-    d_round(0)
-    for step in range(2, line):
-        a_tower(step)
-    a_sibling()
+    def widen_vec():
+        lane = lax.broadcasted_iota(jnp.int32, (16, LANES), 1)
+        parts = [jnp.zeros((16, LANES), F32) for _ in range(D // LANES)]
+        for j in range(groups):
+            block, first = divmod(j * plan.vec, LANES)
+            piece = r.vt[j].astype(F32)
+            if first:
+                piece = pltpu.roll(piece, first, 1)
+            parts[block] = parts[block] + jnp.where(lane >= first, piece, 0.0)
+            if first + plan.vec > LANES:
+                parts[block + 1] = parts[block + 1] + jnp.where(lane < first, piece, 0.0)
+        r.vec[...] = jnp.concatenate(parts, axis=1)
+
     pairs = D // LANES
+    half_pairs = pairs // 2
 
     scale = HEAD ** (-0.5)
 
-    def project(p, carry):
-        w = jnp.concatenate(
-            [wide(wa, qkv_lane(p + k * pairs), LANES) for k in range(3)], axis=1
-        )
-        packed = jnp.dot(tok[...], w, preferred_element_type=F32)
-        o = aligned(p * LANES, LANES)
-        r.qkv[:, pl.ds(o, LANES)] = (turn(packed[:, :LANES]) * scale).astype(BF)
-        r.qkv[:, pl.ds(D + o, LANES)] = turn(packed[:, LANES : 2 * LANES]).astype(BF)
-        r.qkv[:, pl.ds(2 * D + o, LANES)] = packed[:, 2 * LANES :].astype(BF)
-        return carry
+    def project(h):
+        for k in range(3):
+            packed = jnp.dot(tok[...], wide(wa, aligned(h * half_a + k * half_d, LANES), half_d),
+                             preferred_element_type=F32)
+            for i in range(half_pairs):
+                part = packed[:, i * LANES : (i + 1) * LANES]
+                if k < 2:
+                    part = turn(part)
+                if k == 0:
+                    part = part * scale
+                r.qkv[:, pl.ds(aligned(k * D + h * half_d + i * LANES, LANES), LANES)] = (
+                    part.astype(BF))
 
     def triple(p):
         o = aligned(p * LANES, LANES)
@@ -827,7 +820,7 @@
     def only(h, a):
         return jnp.where(first_head if h == 0 else jnp.logical_not(first_head), a, jnp.zeros_like(a))
 
-    def attend(p, carry):
+    def attend(p):
         q2, k2, v2 = triple(p)
         outs = []
         for h in range(2):
@@ -838,20 +831,44 @@
             outs.append(jnp.dot(probs.astype(BF), v2, preferred_element_type=F32))
         o = aligned(p * LANES, LANES)
         r.mixed[:, pl.ds(o, LANES)] = jnp.where(first_head, outs[0], outs[1]).astype(BF)
-        return carry
-
-    lax.fori_loop(0, pairs, project, 0)
+
+    def over_pairs(h, body, lo=0, hi=half_pairs):
+        def step(i, carry):
+            body(h * half_pairs + i)
+            return carry
+
+        lax.fori_loop(lo, hi, step, 0)
+
+    g_line(0)
+    transpose_into(r.tokt, tok, D)
+    a_round(1)
+    g_spread(0)
+    a_cross(0)
+    for step in range(2, line):
+        a_round(step)
+        a_cross(step - 1)
+    d_cross()
+    g_line(1)
+    g_spread(1)
+    a_cross(line - 1)
+    lax.fori_loop(0, groups, v_wait, 0)
+    widen_vec()
+    a_sibling(t)
+    project(t)
+    for step in range(2):
+        a_tower(step)
     g_line(2)
+    over_pairs(t, attend)
+    for step in range(2, line):
+        a_tower(step)
+    g_spread(2)
+    d_start()
+    a_sibling(1 - t)
+    project(1 - t)
     g_cross(0)
-    g_spread(2)
-    lax.fori_loop(0, pairs // 2, attend, 0)
-    for step in range(3, line):
-        g_line(step)
-    d_round(1)
-    g_cross(1)
-    for step in range(3, line):
-        g_spread(step)
-    lax.fori_loop(pairs // 2, pairs, attend, 0)
+    over_pairs(1 - t, attend, 0, 1)
+    d_round(1, False)
+    over_pairs(1 - t, attend, 1)
 
     for h in range(2):
         part = jnp.dot(r.mixed[...], wide(wa, h * half_a + 3 * D // 2, out_w),
@@ -888,9 +905,14 @@
 
     swap_rows(0, r.feed.at[mine], r.feed.at[mine])
     transpose_into(r.mixt, r.mixed, D)
+    for step in range(3, line):
+        g_line(step)
+        g_spread(step)
+    g_cross(1)
     for step in range(2, line):
         g_cross(step)
-        d_round(step)
+        if step < line - 1:
+            d_round(step, False)
     g_sibling()
 
     step_ff = 2 * LANES
@@ -908,6 +930,8 @@
 
     got_rows(0, r.feed.at[theirs])
     lax.fori_loop(0, half_ff // step_ff, gated, 0)
+    for step in range(1, line):
+        d_round(step, True)
     d_sibling()
 
     def down(rows_of, store):
@@ -1073,9 +1097,9 @@
             total = total + ref[...].astype(F32)
         return total
 
-    def line_step(step, parts, sem, slot, only_at=None):
+    def line_step(step, parts, sem, slot, nth):
         for k, (dest, cond, nxt, way) in enumerate(along(step)):
-            if only_at is not None and k % (line - 1) != only_at:
+            if k % (line - 1) != nth:
                 continue
             into = slot(dest + 1 if way == 0 else dest)
             refs = parts(dest)
@@ -1126,8 +1150,8 @@
         for s in range(line):
             got(None, r.gd_rc.at[s], r.gd_c.at[1, s])
 
-    def down_line(step, only_at=None):
-        line_step(step, down_parts, lambda *i: r.gd_z.at[i], lambda k: r.gd_rz.at[k], only_at)
+    def down_line(step, nth):
+        line_step(step, down_parts, lambda *i: r.gd_z.at[i], lambda k: r.gd_rz.at[k], nth)
 
     def down_end():
         line_end(down_parts, lambda *i: r.gd_z.at[i], lambda k: r.gd_rz.at[k], r.gd_f)
@@ -1181,11 +1205,14 @@
         return lambda dest: (gg.at[dest, x, c, :, span], r.gg_rc.at[dest, x, :, span],
                              r.gg_rx.at[dest, :, span])
 
-    def gate_line(k, step):
+    def gate_ready(k):
         span = pl.ds(k * part_gu, part_gu)
-        if step == 0:
-            got(None, r.gg_rx.at[:, :, span], r.gg_x.at[1, k])
-        line_step(step, gate_parts(k), lambda a, *i: r.gg_z.at[(a, k) + i], lambda s: r.gg_rz.at[s, :, span])
+        got(None, r.gg_rx.at[:, :, span], r.gg_x.at[1, k])
+
+    def gate_line(k, step, nth):
+        span = pl.ds(k * part_gu, part_gu)
+        line_step(step, gate_parts(k), lambda a, *i: r.gg_z.at[(a, k) + i],
+                  lambda s: r.gg_rz.at[s, :, span], nth)
 
     def gate_end(k):
         span = pl.ds(k * part_gu, part_gu)
@@ -1196,26 +1223,28 @@
                         r.gg_y.at[1, k], dev_y), tail)
 
     ga = wg
-    part_a = half_a // 4
+    sizes = (3 * LANES, 3 * LANES, 3 * LANES, out_w)
+    starts = (0, 3 * LANES, 6 * LANES, third)
 
     def cols_a(k, h):
-        return pl.ds(aligned(h * half_a + k * part_a, LANES), part_a)
-
-    def store_a(k, left, right):
-        for h in range(2):
-            val = jnp.dot(left[...], right[h], preferred_element_type=F32)
-            ga[:, :, :, :, cols_a(k, h)] = val.astype(BF).reshape(line, 2, 2, shard, part_a)
-            send(None, copy(ga.at[:, :, 1 - c, :, cols_a(k, h)],
-                            r.ga_rc.at[:, :, :, cols_a(k, h)],
-                            r.ga_c.at[0, h, k], r.ga_c.at[1, h, k], dev_c), tail)
+        return pl.ds(aligned(h * half_a + starts[k], LANES), sizes[k])
+
+    def store_a(k, h, left, right):
+        val = jnp.dot(left[...], right, preferred_element_type=F32)
+        ga[:, :, :, :, cols_a(k, h)] = val.astype(BF).reshape(line, 2, 2, shard, sizes[k])
+        send(None, copy(ga.at[:, :, 1 - c, :, cols_a(k, h)],
+                        r.ga_rc.at[:, :, :, cols_a(k, h)],
+                        r.ga_c.at[0, h, k], r.ga_c.at[1, h, k], dev_c), tail)
+
+    def store_qkv(k, h):
+        store_a(k, h, r.tokt, dqkv[:, pl.ds(aligned(h * third + starts[k], LANES), sizes[k])])
 
     def span_a(k):
-        return pl.ds(k * part_a, part_a)
+        return pl.ds(starts[k], sizes[k])
 
     def tower_a(k):
-        for h in range(2):
-            got(None, r.ga_rc.at[:, :, :, cols_a(k, h)], r.ga_c.at[1, h, k])
         gone = cols_a(k, 1 - t)
+        got(None, r.ga_rc.at[:, :, :, gone], r.ga_c.at[1, 1 - t, k])
         for s in range(line):
             for xx in range(2):
                 ref = ga.at[s, xx, c, :, gone]
@@ -1226,6 +1255,7 @@
     def cross_a(k):
         got(None, r.ga_rt.at[:, :, :, span_a(k)], r.ga_t.at[1, k])
         here = cols_a(k, t)
+        got(None, r.ga_rc.at[:, :, :, here], r.ga_c.at[1, t, k])
         for s in range(line):
             ref = ga.at[s, 1 - x, c, :, here]
             ref[...] = added((ref, r.ga_rc.at[s, 1 - x, :, here],
@@ -1239,10 +1269,12 @@
                              r.ga_rt.at[dest, x, :, span_a(k)],
                              r.ga_rx.at[dest, :, span_a(k)])
 
-    def line_a(k, step):
-        if step == 0:
-            got(None, r.ga_rx.at[:, :, span_a(k)], r.ga_x.at[1, k])
-        line_step(step, parts_a(k), lambda a, *i: r.ga_z.at[(a, k) + i], lambda s: r.ga_rz.at[s, :, span_a(k)])
+    def ready_a(k):
+        got(None, r.ga_rx.at[:, :, span_a(k)], r.ga_x.at[1, k])
+
+    def line_a(k, step, nth):
+        line_step(step, parts_a(k), lambda a, *i: r.ga_z.at[(a, k) + i],
+                  lambda s: r.ga_rz.at[s, :, span_a(k)], nth)
 
     def end_a(k):
         line_end(parts_a(k), lambda a, *i: r.ga_z.at[(a, k) + i], lambda s: r.ga_rz.at[s, :, span_a(k)],
@@ -1256,46 +1288,25 @@
     def rows_of_weight(ref, j, lo, n):
         return ref[pl.ds(2 * j, 2), :, :, :, pl.ds(lo, n)].reshape(some, n)
 
-    def feed_back(rows_of, store):
-        def body(j, carry):
-            store(pl.ds(aligned(j * some, LANES), some),
-                  dot_tt(r.dgu[rows_of, :], rows_of_weight(wg, j, 0, ff)))
-            return carry
-
-        lax.fori_loop(0, line // 2, body, 0)
-
-    def back_send(span, val):
+    def feed_part(rows_of, j, store):
+        store(j, pl.ds(j * some, some), dot_tt(r.dgu[rows_of, :], rows_of_weight(wg, j, 0, ff)))
+
+    def back_send(j, span, val):
         r.dsend[:, span] = val.astype(BF)
-
-    def back_own(span, val):
+        send(None, copy(r.dsend.at[:, span], r.drecv.at[:, span], r.s_back.at[j], r.r_back.at[j],
+                        dev_y), tail)
+
+    def back_own(j, span, val):
         r.bown[:, span] = val
 
     hidden_back(mine)
-    feed_back(mine, back_own)
+    for j in range(line // 2):
+        feed_part(mine, j, back_own)
     for s in range(line):
         down_own(s)
     for k in range(4):
         gate_own(k)
     got_rows(2, r.dbr.at[theirs])
-    for s in range(line):
-        down_grad(s)
-    hidden_back(theirs)
-    down_arrive()
-    down_line(0)
-    feed_back(theirs, back_send)
-    swap_rows(3, r.dsend, r.drecv)
-    gate_grad(0)
-    gate_grad(1)
-    gate_cross(0)
-    gate_grad(2)
-    gate_cross(1)
-    gate_grad(3)
-    settle(pending)
-    gate_cross(2)
-    gate_cross(3)
-    down_line(1, 0)
-    got_rows(3, r.drecv)
-
     def norm_one_back(b, sums):
         part = pl.ds(aligned(b * quarter, quarter), quarter)
         top = r.n1[part, :] + r.bown[part, :] + r.drecv[part, :].astype(F32)
@@ -1309,9 +1320,12 @@
         return (sums[0] + jnp.sum(top * hat, 0, keepdims=True),
                 sums[1] + jnp.sum(top, 0, keepdims=True))
 
-    gain_one, bias_one = lax.fori_loop(0, blocks, norm_one_back, (zero_row, zero_row))
-    r.ln[0] = (r.ln[0] + jnp.where(row8 == 0, gain_one, 0.0)
-                  + jnp.where(row8 == 1, bias_one, 0.0))
+    def norm_back():
+        for j in range(line // 2):
+            got(None, r.drecv.at[:, pl.ds(j * some, some)], r.r_back.at[j])
+        gain_one, bias_one = lax.fori_loop(0, blocks, norm_one_back, (zero_row, zero_row))
+        r.ln[0] = (r.ln[0] + jnp.where(row8 == 0, gain_one, 0.0)
+                   + jnp.where(row8 == 1, bias_one, 0.0))
 
     ln_peers = [dev_y, dev_c, dev_x]
     for bit in range(line.bit_length() - 1):
@@ -1319,13 +1333,20 @@
         ln_peers.append(dev_z(z + apart * (1 - 2 * ((z // apart) % 2))))
     last = len(ln_peers)
 
-    def ln_send(k):
-        send(None, copy(r.ln.at[k], r.lnr.at[k], r.s_ln.at[k], r.r_ln.at[k],
-                        ln_peers[k]), tail)
-
-    def ln_add(k):
-        got(None, r.lnr.at[k], r.r_ln.at[k])
-        r.ln[k + 1] = r.ln[k] + r.lnr[k]
+    def small_sums(k):
+        if k:
+            got(None, r.lnr.at[k - 1], r.r_ln.at[k - 1])
+            r.ln[k] = r.ln[k - 1] + r.lnr[k - 1]
+        if k < last:
+            send(None, copy(r.ln.at[k], r.lnr.at[k], r.s_ln.at[k], r.r_ln.at[k],
+                            ln_peers[k]), tail)
+
+    def out_grad():
+        for h in range(2):
+            store_a(3, h, r.mixt, r.datt[:, pl.ds(h * out_w, out_w)])
+
+    def mix_back():
+        lax.fori_loop(0, line // 2, mixed_back, 0)
 
     dqkv = r.dgu.at[pl.ds(0, count), pl.ds(0, 3 * D)]
     dmix = r.dgu.at[pl.ds(count, count), pl.ds(0, D)]
@@ -1336,7 +1357,7 @@
         dmix[:, pl.ds(aligned(j * some, LANES), some)] = val.astype(BF)
         return carry
 
-    def attend_back(p, carry):
+    def attend_back(p):
         q2, k2, v2 = triple(p)
         o = aligned(p * LANES, LANES)
         dm2 = dmix[:, pl.ds(o, LANES)]
@@ -1349,10 +1370,10 @@
             parts.append((jnp.dot(dscores, k2, preferred_element_type=F32),
                           dot_t0(dscores, q2), dot_t0(probs.astype(BF), dm2)))
         dq, dk, dv = (jnp.where(first_head, a, b) for a, b in zip(*parts))
-        dqkv[:, pl.ds(o, LANES)] = turn_back(dq * scale).astype(BF)
-        dqkv[:, pl.ds(D + o, LANES)] = turn_back(dk).astype(BF)
-        dqkv[:, pl.ds(2 * D + o, LANES)] = dv.astype(BF)
-        return carry
+        half = p // half_pairs
+        o = half * third + (p - half * half_pairs) * LANES
+        for k, part in enumerate((turn_back(dq * scale), turn_back(dk), dv)):
+            dqkv[:, pl.ds(aligned(o + k * half_d, LANES), LANES)] = part.astype(BF)
 
     def token_back(j, carry):
         val = sum(dot_tt(dqkv[:, pl.ds(h * third, third)],
@@ -1361,68 +1382,124 @@
         r.o_tok[:, span] = r.n1[:, span] + val
         return carry
 
-    ln_send(0)
-    store_a(3, r.mixt, [r.datt[:, pl.ds(h * out_w, out_w)] for h in range(2)])
-    lax.fori_loop(0, line // 2, mixed_back, 0)
-    ln_add(0)
-    ln_send(1)
+    hidden_back(theirs)
+    gate_grad(0)
+    feed_part(theirs, 0, back_send)
+    down_grad(3)
+    down_grad(0)
+    down_grad(1)
+    gate_cross(0)
+    down_grad(2)
+    feed_part(theirs, 1, back_send)
+    down_arrive()
+    down_line(0, 0)
+    gate_grad(1)
+    gate_cross(1)
+    gate_grad(3)
+    gate_grad(2)
+    down_line(0, 1)
+    norm_back()
+    settle(pending)
+    out_grad()
+    small_sums(0)
+    gate_cross(2)
+    mix_back()
+    over_pairs(1 - t, attend_back, 0, 2)
+    gate_ready(0)
     tower_a(3)
-    gate_line(0, 0)
-    lax.fori_loop(0, 2, attend_back, 0)
+    over_pairs(1 - t, attend_back, 2, 3)
+    gate_ready(1)
+    gate_line(0, 0, 1)
+    down_line(1, 0)
+    gate_cross(3)
+    store_qkv(0, 1 - t)
+    gate_line(0, 0, 0)
+    gate_line(0, 0, 2)
+    store_qkv(2, 1 - t)
+    gate_line(1, 0, 0)
+    store_qkv(1, 1 - t)
+    over_pairs(t, attend_back, 0, 1)
     down_line(1, 1)
-    lax.fori_loop(2, 4, attend_back, 0)
-    gate_line(0, 1)
-    gate_line(1, 0)
+    down_line(0, 2)
+    over_pairs(t, attend_back, 1, 2)
+    tower_a(0)
     down_line(2, 0)
-    lax.fori_loop(4, pairs, attend_back, 0)
-    for k in range(3):
-        store_a(k, r.tokt, [dqkv[:, pl.ds(h * third + k * part_a, part_a)] for h in range(2)])
-    for k in range(3):
-        tower_a(k)
-    ln_add(1)
-    gate_line(0, 2)
-    gate_line(1, 1)
+    over_pairs(t, attend_back, 2, 3)
+    tower_a(2)
+    store_qkv(0, t)
+    gate_ready(2)
+    store_qkv(2, t)
+    cross_a(3)
+    store_qkv(1, t)
+    gate_line(2, 0, 1)
+    gate_line(1, 0, 2)
+    gate_ready(3)
+    gate_line(0, 1, 0)
+    tower_a(1)
+    cross_a(0)
+    down_end()
+    ready_a(3)
+    gate_line(2, 0, 0)
+    gate_line(1, 1, 0)
+    gate_line(3, 0, 0)
+    gate_line(0, 1, 1)
+    line_a(3, 0, 1)
+    line_a(3, 0, 0)
+    gate_line(3, 0, 1)
+    gate_line(2, 1, 1)
+    gate_line(0, 2, 0)
+    gate_line(1, 0, 1)
     lax.fori_loop(0, line // 2, token_back, 0)
-    gate_line(2, 0)
-    cross_a(3)
-    down_end()
+    gate_line(3, 1, 0)
     gate_end(0)
-    gate_line(1, 2)
-    gate_line(2, 1)
-    gate_line(3, 0)
-    line_a(3, 0)
-    cross_a(0)
-    gate_line(2, 2)
+    ready_a(0)
+    small_sums(1)
+    gate_line(2, 1, 0)
+    line_a(0, 0, 0)
+    cross_a(2)
+    gate_line(3, 0, 2)
+    down_out()
+    cross_a(1)
+    gate_line(3, 2, 0)
+    gate_line(2, 2, 0)
+    gate_line(1, 1, 1)
+    gate_line(1, 2, 0)
+    gate_line(2, 0, 2)
+    line_a(0, 1, 0)
+    ready_a(2)
+    line_a(3, 1, 0)
+    line_a(2, 0, 0)
+    line_a(2, 0, 1)
+    line_a(0, 0, 1)
+    small_sums(2)
+    line_a(3, 1, 1)
+    line_a(2, 1, 0)
+    ready_a(1)
+    gate_line(3, 1, 1)
+    line_a(1, 0, 0)
+    line_a(1, 0, 1)
+    line_a(3, 0, 2)
+    gate_end(2)
+    line_a(3, 2, 0)
+    line_a(0, 1, 1)
     gate_end(1)
-    down_out()
-    gate_line(3, 1)
-    line_a(3, 1)
-    line_a(0, 0)
-    cross_a(1)
-    gate_end(2)
-    gate_line(3, 2)
-    line_a(3, 2)
-    line_a(0, 1)
-    line_a(1, 0)
+    line_a(1, 1, 0)
+    line_a(0, 0, 2)
+    line_a(2, 0, 2)
+    line_a(0, 2, 0)
+    line_a(2, 1, 1)
     gate_end(3)
-    line_a(0, 2)
+    line_a(1, 0, 2)
+    line_a(1, 1, 1)
+    line_a(2, 2, 0)
+    small_sums(3)
     end_a(3)
-    cross_a(2)
-    ln_send(2)
-    line_a(1, 1)
+    line_a(1, 2, 0)
     end_a(0)
-    ln_add(2)
-    line_a(2, 0)
-    ln_send(3)
-    line_a(1, 2)
-    line_a(2, 1)
+    end_a(2)
+    small_sums(4)
     end_a(1)
-    for k in range(3, last):
-        ln_add(k)
-        if k + 1 < last:
-            ln_send(k + 1)
-    line_a(2, 2)
-    end_a(2)
+    small_sums(5)
 
     r.o_vec[...] = r.ln[last]
     r.o_loss[...] = r.ln[last][:, 0:LANES] * (1.0 / (groups * QPD))
@@ -1462,7 +1539,9 @@
     third, half_a, half_ff, stripe = 3 * D // 2, plan.half_a, plan.half_ff, plan.stripe
     out_w = half_a - third
     for h in range(2):
-        o_qkv[:, h * third : (h + 1) * third] = a_ref[:, h * half_a : h * half_a + third].astype(F32)
+        for k in range(3):
+            o_qkv[:, pl.ds(k * D + h * (D // 2), D // 2)] = (
+                a_ref[:, pl.ds(h * half_a + k * (D // 2), D // 2)].astype(F32))
         o_out[:, h * out_w : (h + 1) * out_w] = (
             a_ref[:, h * half_a + third : (h + 1) * half_a].astype(F32))
         for s in range(plan.line):
@@ -1526,7 +1605,7 @@
 
 def fits(plan, towers):
     line = plan.line
-    return (towers == 2 and plan.groups % 4 == 0 and line & (line - 1) == 0 and line > 1
+    return (towers == 2 and plan.groups % 4 == 0 and line == 4
             and plan.shard % 16 == 0 and plan.shard_ff % 16 == 0 and plan.stripe % LANES == 0
             and plan.count == QPD * QLEN)
 

time: 186 us -> 173 us (0.930)
  Pallas kernels: 184 us -> 170 us
    pallas_call x1, Pallas kernels: 180 us -> 166 us  [on_device_kernel(): pl.pallas_call(functools.partial(whole_step, plan), out_shape=(shape((cou...]
where the time goes in v3:
time: 173 us
  Pallas kernels  170 us (98%)
    pallas_call x1, Pallas kernels, on_device_kernel(): pl.pallas_call(functools.partial(whole_step, plan), out_shape=(shape((cou...  166 us
    pallas_call x1, Pallas kernels, on_device_kernel(): pl.pallas_call(functools.partial(finish, plan), out_shape=(shape((1, 1),...  3.49 us

profile of v3, /device:TPU:0, one launch (start us, length us, event | category | flops | bytes accessed | tf_op | source)
XLA Modules:
  0.0 172.7 jit_solution(17046222645983235520)
XLA Ops:
  1.3 0.0 copy-start.3
  1.3 0.0 copy-start
  1.3 0.0 copy-start.1
  1.3 0.0 copy-start.2
  1.3 0.6 copy-done.3
  1.9 0.0 copy-done
  2.0 0.0 copy-done.1
  2.0 0.0 copy-done.2
  2.0 0.6 fusion.8.refs_7_
  2.6 166.4 %whole_step.1 = (f32[256,768]{1,0:T(8,128)}, bf16[48,3072]{1,0:T(8,128)(2,1)}, bf16[2,48,3072]{2,1,0:T(8,128)(2,1)}, bf16[192,768]{1,0:T(8,128)(2,1)}, f32[8,768...) custom-call(s32[4]{0:T(128)} %refs_0_.1, s32[1]{0:T(128)S(6)} %copy.28.refs_1_, s32[64]{0:T(128)} %refs_2_.1, ...), custom_call_target="tpu_custom_call" | custom-call | tf_op jit(solution)/shard_map/whole_step/pallas_call | solution.py:1575
  169.1 3.5 %finish.1 = (f32[1,1]{1,0:T(1,128)}, f32[4,768]{1,0:T(4,128)}, f32[1,768]{1,0:T(1,128)}, f32[1,256,768]{2,1,0:T(8,128)}, f32[48,2304]{1,0:T(8,128)}, /*index=5*/...) custom-call(bf16[48,3072]{1,0:T(8,128)(2,1)} %get-tuple-element.34.r, ...), custom_call_target="tpu_custom_call" | custom-call | tf_op jit(solution)/shard_map/finish/pallas_call | solution.py:1591
Async XLA Ops:
  1.3 0.7 copy-start.3
  1.3 0.7 copy-start
  1.3 0.7 copy-start.1
  1.3 0.7 copy-start.2

commit v4 on v3

--- a/solution.py
+++ b/solution.py
@@ -383,22 +383,24 @@
     dma = pltpu.SemaphoreType.DMA
     chunks_gu, chunks_a = 4, 4
     return dict(
-        loc=dma((24,)),
+        loc=dma((40,)),
         ra=dma((groups, 2)),
         sa_z=dma((2, line)),
         sa_x=dma((line, 2)),
         sa_y=dma((line, 2)),
         sa_c=dma((line, 2, 2)),
-        rg=dma((groups,)),
-        sg_z=dma((2, line)),
-        sg_x=dma((line,)),
-        sg_c=dma((line, 2)),
+        rg=dma((groups, 2)),
+        sg_z=dma((2, line, 2)),
+        sg_x=dma((line, 2)),
+        sg_c=dma((line, 2, 2)),
         rd=dma((line, 2)),
         sd_x=dma((1,)),
         sd_z=dma((2, line)),
         sd_c=dma((line,)),
         rv=dma((groups,)),
         sv=dma((groups,)),
+        s_part=dma((D // (2 * LANES),)),
+        r_part=dma((D // (2 * LANES),)),
         s_back=dma((line,)),
         r_back=dma((line,)),
         sx=dma((4,)),
@@ -424,7 +426,7 @@
         ga_x=dma((2, chunks_a)),
         ga_z=dma((2, chunks_a, 2, line)),
         ga_y=dma((2, chunks_a)),
-        fin=dma((9,)),
+        fin=dma((10,)),
     )
 
 
@@ -436,8 +438,9 @@
         wa=v((line, 2, 2, shard, plan.width_a), BF),
         wg=v((line, 2, 2, shard, plan.ff), BF),
         wd=v((line, 2, plan.shard_ff, D), BF),
-        vt=v((groups, 16, LANES), BF),
-        vec=v((16, D), F32),
+        tok=v((count, D), BF),
+        vt=v((groups, 8, LANES), F32),
+        vec=v((8, D), F32),
         cos=v((count, LANES), F32),
         sin=v((count, LANES), F32),
         hide=v((count, count), F32),
@@ -499,11 +502,13 @@
     qlen: Any
     dlen: Any
     pos: Any
-    posv: Any
-    tok: Any
+    i_tok: Any
     tcos: Any
     tsin: Any
-    tile: Any
+    g_one: Any
+    b_one: Any
+    g_two: Any
+    b_two: Any
     i_qkv: Any
     i_out: Any
     i_gate: Any
@@ -585,11 +590,25 @@
         near(r.i_out.at[:, pl.ds(h * out_w, out_w)],
              wa.at[z, x, c, :, pl.ds(h * half_a + third, out_w)])
     near(r.i_down, wd.at[z, c], x == t)
-    near(r.tile, r.vt.at[me])
+    near(r.i_tok, r.tok)
+    for s in range(QPD):
+        begin = aligned(s * QLEN * t, QLEN)
+        near(r.tcos.at[pl.ds(begin, QLEN)], r.cos.at[pl.ds(s * QLEN, QLEN)])
+        near(r.tsin.at[pl.ds(begin, QLEN)], r.sin.at[pl.ds(s * QLEN, QLEN)])
+    part_ff = half_ff // 2
+    per_part = line // 2
+
+    def stripe_at(k, s):
+        return (2 * (s // per_part) + k) * part_ff + (s % per_part) * stripe
+
     for s in range(line):
         for k, ref in enumerate((r.i_gate, r.i_up)):
             near(ref.at[:, pl.ds(aligned((2 * s + t) * stripe, LANES), stripe)],
-                 wg.at[z, x, c, :, pl.ds(k * half_ff + s * stripe, stripe)])
+                 wg.at[z, x, c, :, pl.ds(stripe_at(k, s), stripe)])
+
+    r.vt[me] = jnp.zeros((8, LANES), F32)
+    for k, ref in enumerate((r.g_one, r.b_one, r.g_two, r.b_two)):
+        r.vt[me, pl.ds(k, 1), pl.ds(0, plan.vec)] = ref[...].astype(F32)
 
     barrier = pltpu.get_barrier_semaphore()
 
@@ -621,75 +640,74 @@
         got(cond, piece_a(zz, xx, cc, h), r.ra.at[at(zz, xx, cc), h])
 
     def sides(step):
-        yield z - step, z >= step, z < line - 1, z + 1, 0
-        yield z + step, z < line - step, z > 0, z - 1, 1
-
-    def a_round(step):
-        for zz, there, on, nxt, way in sides(step):
-            if step:
-                got_a(there, zz, x, c, t)
-            send_a(both(there, on), r.sa_z.at[way, zz], zz, x, t, dev_z(nxt))
-            if step or way == 0:
-                send_a(there, r.sa_x.at[zz, t], zz, x, t, dev_x)
-                if step:
-                    send_a(there, r.sa_y.at[zz, x], zz, x, t, dev_y)
-                else:
-                    send_a(x != t, r.sa_x.at[zz, 1 - t], zz, x, 1 - t, dev_x)
-                send_a(there, r.sa_c.at[zz, x, t], zz, x, t, dev_c)
-        if step == 0:
-            send_a(None, r.sa_c.at[z, x, 1 - t], z, x, 1 - t, dev_c)
-
-    def around(step):
-        return list(sides(step))[: 1 if step == 0 else 2]
-
-    def a_cross(step):
-        for zz, there, _, _, _ in around(step):
-            got_a(there, zz, 1 - x, c, t)
-            send_a(there if step else x == t, r.sa_y.at[zz, 1 - x], zz, 1 - x, t, dev_y)
-            send_a(there, r.sa_c.at[zz, 1 - x, t], zz, 1 - x, t, dev_c)
-
-    def a_tower(step):
-        if step == 0:
-            got_a(None, z, 1 - x, c, 1 - t)
-            send_a(None, r.sa_c.at[z, 1 - x, 1 - t], z, 1 - x, 1 - t, dev_c)
-            return
-        for zz, there, _, _, _ in sides(step):
-            for xx in (x, 1 - x):
-                got_a(there, zz, xx, c, 1 - t)
-                send_a(there, r.sa_c.at[zz, xx, 1 - t], zz, xx, 1 - t, dev_c)
+        return ((z - step, z >= step, z < line - 1, z + 1), (z + step, z < line - step, z > 0, z - 1))
+
+    def a_start():
+        for way, (_, _, on, nxt) in enumerate(sides(0)):
+            send_a(on, r.sa_z.at[way, z], z, x, t, dev_z(nxt))
+        send_a(None, r.sa_x.at[z, t], z, x, t, dev_x)
+        send_a(x != t, r.sa_x.at[z, 1 - t], z, x, 1 - t, dev_x)
+        send_a(None, r.sa_c.at[z, x, t], z, x, t, dev_c)
+        send_a(None, r.sa_c.at[z, x, 1 - t], z, x, 1 - t, dev_c)
+
+    def a_round(step, way):
+        zz, there, on, nxt = sides(step)[way]
+        got_a(there, zz, x, c, t)
+        send_a(both(there, on), r.sa_z.at[way, zz], zz, x, t, dev_z(nxt))
+        send_a(there, r.sa_x.at[zz, t], zz, x, t, dev_x)
+        send_a(there, r.sa_y.at[zz, x], zz, x, t, dev_y)
+        send_a(there, r.sa_c.at[zz, x, t], zz, x, t, dev_c)
+
+    def a_cross(step, way):
+        zz, there, _, _ = sides(step)[way]
+        got_a(there, zz, 1 - x, c, t)
+        send_a(there if step else x == t, r.sa_y.at[zz, 1 - x], zz, 1 - x, t, dev_y)
+        send_a(there, r.sa_c.at[zz, 1 - x, t], zz, 1 - x, t, dev_c)
+
+    def a_tower(step, way):
+        zz, there, _, _ = sides(step)[way]
+        for xx in (x, 1 - x) if step else (1 - x,):
+            got_a(there, zz, xx, c, 1 - t)
+            send_a(there, r.sa_c.at[zz, xx, 1 - t], zz, xx, 1 - t, dev_c)
 
     def a_sibling(h):
         for zz in range(line):
             for xx in range(2):
                 got_a(None, zz, xx, 1 - c, h)
 
-    def send_g(cond, sem, zz, xx, dev):
-        ref = wg.at[zz, xx, c]
-        send(cond, copy(ref, ref, sem, r.rg.at[at(zz, xx, c)], dev))
-
-    def got_g(cond, zz, xx, cc):
-        got(cond, wg.at[zz, xx, cc], r.rg.at[at(zz, xx, cc)])
-
-    def g_line(step):
-        for zz, there, on, nxt, way in sides(step):
-            if step:
-                got_g(there, zz, x, c)
-            send_g(both(there, on), r.sg_z.at[way, zz], zz, x, dev_z(nxt))
-
-    def g_spread(step):
-        for zz, there, _, _, _ in around(step):
-            send_g(there, r.sg_x.at[zz], zz, x, dev_x)
-            send_g(there, r.sg_c.at[zz, x], zz, x, dev_c)
-
-    def g_cross(step):
-        for zz, there, _, _, _ in around(step):
-            got_g(there, zz, 1 - x, c)
-            send_g(there, r.sg_c.at[zz, 1 - x], zz, 1 - x, dev_c)
-
-    def g_sibling():
+    def piece_g(zz, xx, cc, h):
+        return wg.at[zz, xx, cc, :, pl.ds(h * half_ff, half_ff)]
+
+    def send_g(cond, sem, zz, xx, h, dev):
+        ref = piece_g(zz, xx, c, h)
+        send(cond, copy(ref, ref, sem, r.rg.at[at(zz, xx, c), h], dev))
+
+    def got_g(cond, zz, xx, cc, h):
+        got(cond, piece_g(zz, xx, cc, h), r.rg.at[at(zz, xx, cc), h])
+
+    def g_start(h):
+        for way, (_, _, on, nxt) in enumerate(sides(0)):
+            send_g(on, r.sg_z.at[way, z, h], z, x, h, dev_z(nxt))
+
+    def g_line(step, way, h):
+        zz, there, on, nxt = sides(step)[way]
+        got_g(there, zz, x, c, h)
+        send_g(both(there, on), r.sg_z.at[way, zz, h], zz, x, h, dev_z(nxt))
+
+    def g_spread(step, way, h):
+        zz, there, _, _ = sides(step)[way]
+        send_g(there, r.sg_x.at[zz, h], zz, x, h, dev_x)
+        send_g(there, r.sg_c.at[zz, x, h], zz, x, h, dev_c)
+
+    def g_cross(step, way, h):
+        zz, there, _, _ = sides(step)[way]
+        got_g(there, zz, 1 - x, c, h)
+        send_g(there, r.sg_c.at[zz, 1 - x, h], zz, 1 - x, h, dev_c)
+
+    def g_sibling(h):
         for zz in range(line):
             for xx in range(2):
-                got_g(None, zz, xx, 1 - c)
+                got_g(None, zz, xx, 1 - c, h)
 
     def send_d(cond, sem, zz, dev):
         ref = wd.at[zz, c]
@@ -703,17 +721,17 @@
 
     def d_start():
         got_d(x != t, z, c)
-        for zz, _, on, nxt, way in sides(0):
-            send_d(on, r.sd_z.at[way, zz], zz, dev_z(nxt))
+        for way, (_, _, on, nxt) in enumerate(sides(0)):
+            send_d(on, r.sd_z.at[way, z], z, dev_z(nxt))
         send_d(None, r.sd_c.at[z], z, dev_c)
 
-    def d_round(step, ends):
-        for zz, there, on, nxt, way in sides(step):
-            cond = both(there, jnp.logical_not(on) if ends else on)
-            got_d(cond, zz, c)
-            if not ends:
-                send_d(cond, r.sd_z.at[way, zz], zz, dev_z(nxt))
-            send_d(cond, r.sd_c.at[zz], zz, dev_c)
+    def d_round(step, way, ends):
+        zz, there, on, nxt = sides(step)[way]
+        cond = both(there, jnp.logical_not(on) if ends else on)
+        got_d(cond, zz, c)
+        if not ends:
+            send_d(cond, r.sd_z.at[way, zz], zz, dev_z(nxt))
+        send_d(cond, r.sd_c.at[zz], zz, dev_c)
 
     def d_sibling():
         for zz in range(line):
@@ -735,7 +753,7 @@
 
         return carry
 
-    a_round(0)
+    a_start()
     lax.fori_loop(0, groups, v_send, 0)
 
     tok = r.tok
@@ -755,9 +773,6 @@
         length = jnp.full((quarter, 1), r.qlen[s] * (1 - t) + r.dlen[0] * t, jnp.int32)
         slot = lax.broadcasted_iota(jnp.int32, (quarter, 1), 0) + s * quarter * t
         r.pw[part, :] = jnp.where(slot < length, 1.0 / length.astype(F32), 0.0)
-        begin = aligned(s * quarter * t, quarter)
-        r.cos[part, :] = r.tcos[pl.ds(begin, quarter), :]
-        r.sin[part, :] = r.tsin[pl.ds(begin, quarter), :]
     lanes = lax.broadcasted_iota(jnp.int32, (count, LANES), 1)
     first_head = lanes < HEAD
     low_half = (lanes & (HEAD - 1)) < HEAD // 2
@@ -783,11 +798,11 @@
         return ref[:, :, :, :, pl.ds(lo, n)].reshape(groups * shard, n)
 
     def widen_vec():
-        lane = lax.broadcasted_iota(jnp.int32, (16, LANES), 1)
-        parts = [jnp.zeros((16, LANES), F32) for _ in range(D // LANES)]
+        lane = lax.broadcasted_iota(jnp.int32, (8, LANES), 1)
+        parts = [jnp.zeros((8, LANES), F32) for _ in range(D // LANES)]
         for j in range(groups):
             block, first = divmod(j * plan.vec, LANES)
-            piece = r.vt[j].astype(F32)
+            piece = r.vt[j]
             if first:
                 piece = pltpu.roll(piece, first, 1)
             parts[block] = parts[block] + jnp.where(lane >= first, piece, 0.0)
@@ -839,41 +854,15 @@
 
         lax.fori_loop(lo, hi, step, 0)
 
-    g_line(0)
-    transpose_into(r.tokt, tok, D)
-    a_round(1)
-    g_spread(0)
-    a_cross(0)
-    for step in range(2, line):
-        a_round(step)
-        a_cross(step - 1)
-    d_cross()
-    g_line(1)
-    g_spread(1)
-    a_cross(line - 1)
-    lax.fori_loop(0, groups, v_wait, 0)
-    widen_vec()
-    a_sibling(t)
-    project(t)
-    for step in range(2):
-        a_tower(step)
-    g_line(2)
-    over_pairs(t, attend)
-    for step in range(2, line):
-        a_tower(step)
-    g_spread(2)
-    d_start()
-    a_sibling(1 - t)
-    project(1 - t)
-    g_cross(0)
-    over_pairs(1 - t, attend, 0, 1)
-    d_round(1, False)
-    over_pairs(1 - t, attend, 1)
-
-    for h in range(2):
-        part = jnp.dot(r.mixed[...], wide(wa, h * half_a + 3 * D // 2, out_w),
-                       preferred_element_type=F32)
-        r.h1[:, pl.ds(h * out_w, out_w)] = tok[:, pl.ds(h * out_w, out_w)].astype(F32) + part
+    def vectors():
+        lax.fori_loop(0, groups, v_wait, 0)
+        widen_vec()
+
+    def out_project():
+        for h in range(2):
+            part = jnp.dot(r.mixed[...], wide(wa, h * half_a + third, out_w),
+                           preferred_element_type=F32)
+            r.h1[:, pl.ds(h * out_w, out_w)] = tok[:, pl.ds(h * out_w, out_w)].astype(F32) + part
 
     def moments(h):
         centred = h - jnp.mean(h, -1, keepdims=True)
@@ -893,7 +882,6 @@
             normed.astype(BF))
         return carry
 
-    lax.fori_loop(0, blocks, norm_one, 0)
     mine = pl.ds(aligned(t * count, count), count)
     theirs = pl.ds(aligned((1 - t) * count, count), count)
 
@@ -903,57 +891,148 @@
     def got_rows(k, ref):
         got(None, ref, r.rx.at[k])
 
-    swap_rows(0, r.feed.at[mine], r.feed.at[mine])
-    transpose_into(r.mixt, r.mixed, D)
-    for step in range(3, line):
-        g_line(step)
-        g_spread(step)
-    g_cross(1)
-    for step in range(2, line):
-        g_cross(step)
-        if step < line - 1:
-            d_round(step, False)
-    g_sibling()
+    def norm_rows():
+        lax.fori_loop(0, blocks, norm_one, 0)
+        swap_rows(0, r.feed.at[mine], r.feed.at[mine])
 
     step_ff = 2 * LANES
 
-    def gated(j, carry):
-        o = aligned(j * step_ff, step_ff)
-        gate = jnp.dot(r.feed[...], wide(wg, o, step_ff), preferred_element_type=F32)
-        up = jnp.dot(r.feed[...], wide(wg, half_ff + o, step_ff), preferred_element_type=F32)
-        r.gate[:, pl.ds(o, step_ff)] = gate
-        r.up[:, pl.ds(o, step_ff)] = up
-        hidden = (gate * jax.nn.sigmoid(gate) * up).astype(BF)
-        r.dgu[:, pl.ds(o, step_ff)] = hidden
-        r.hidt[pl.ds(o, step_ff), :] = hidden.T
-        return carry
-
-    got_rows(0, r.feed.at[theirs])
-    lax.fori_loop(0, half_ff // step_ff, gated, 0)
-    for step in range(1, line):
-        d_round(step, True)
-    d_sibling()
+    steps_part = part_ff // step_ff
+
+    def gated(part):
+        def body(j, carry):
+            o = aligned(part * part_ff + j * step_ff, step_ff)
+            w = 2 * part * part_ff + j * step_ff
+            gate = jnp.dot(r.feed[...], wide(wg, aligned(w, step_ff), step_ff),
+                           preferred_element_type=F32)
+            up = jnp.dot(r.feed[...], wide(wg, aligned(w + part_ff, step_ff), step_ff),
+                         preferred_element_type=F32)
+            r.gate[:, pl.ds(o, step_ff)] = gate
+            r.up[:, pl.ds(o, step_ff)] = up
+            hidden = (gate * jax.nn.sigmoid(gate) * up).astype(BF)
+            r.dgu[:, pl.ds(o, step_ff)] = hidden
+            r.hidt[pl.ds(o, step_ff), :] = hidden.T
+            return carry
+
+        lax.fori_loop(0, steps_part, body, 0)
 
     def down(rows_of, store):
-        def body(j, carry):
-            o = aligned(j * step_ff, step_ff)
+        def body(j):
+            o = j * step_ff
             w = wd[:, :, :, pl.ds(o, step_ff)].reshape(half_ff, step_ff)
             store(o, jnp.dot(r.dgu[rows_of, pl.ds(0, half_ff)], w, preferred_element_type=F32))
-            return carry
-
-        lax.fori_loop(0, D // step_ff, body, 0)
+
+        for j in range(D // step_ff):
+            body(j)
 
     def keep_send(o, val):
-        r.bsend[:, pl.ds(o, step_ff)] = val.astype(BF)
+        span = pl.ds(o, step_ff)
+        r.bsend[:, span] = val.astype(BF)
+        send(None, copy(r.bsend.at[:, span], r.brecv.at[:, span], r.s_part.at[o // step_ff],
+                        r.r_part.at[o // step_ff], dev_y), tail)
 
     def keep_own(o, val):
         r.bown[:, pl.ds(o, step_ff)] = val
 
+    g_start(0)
+    d_cross()
+    a_round(1, 0)
+    a_round(1, 1)
+    g_line(1, 0, 0)
+    g_line(1, 1, 0)
+    a_cross(0, 0)
+    a_round(2, 1)
+    a_round(2, 0)
+    a_cross(1, 0)
+    g_start(1)
+    g_spread(0, 0, 1)
+    a_cross(1, 1)
+    g_line(2, 1, 0)
+    g_line(2, 0, 0)
+    a_round(3, 0)
+    a_round(3, 1)
+    g_line(1, 0, 1)
+    a_cross(2, 0)
+    a_cross(2, 1)
+    g_spread(1, 1, 0)
+    g_line(1, 1, 1)
+    g_spread(2, 0, 0)
+    g_spread(2, 1, 0)
+    d_start()
+    a_tower(1, 0)
+    g_spread(1, 0, 0)
+    g_line(3, 0, 0)
+    g_spread(1, 0, 1)
+    g_spread(0, 0, 0)
+    a_cross(3, 0)
+    a_tower(0, 0)
+    a_cross(3, 1)
+    vectors()
+    g_line(2, 0, 1)
+    a_sibling(t)
+    g_spread(3, 0, 0)
+    project(t)
+    over_pairs(t, attend, 0, 1)
+    g_cross(0, 0, 1)
+    over_pairs(t, attend, 1, 2)
+    g_spread(1, 1, 1)
+    g_line(2, 1, 1)
+    g_line(3, 1, 0)
+    g_spread(3, 1, 0)
+    a_tower(3, 0)
+    over_pairs(t, attend, 2, 3)
+    a_tower(1, 1)
+    a_tower(3, 1)
+    a_tower(2, 0)
+    a_tower(2, 1)
+    d_round(1, 0, False)
+    a_sibling(1 - t)
+    project(1 - t)
+    over_pairs(1 - t, attend, 0, 1)
+    d_round(1, 1, False)
+    over_pairs(1 - t, attend, 1, 3)
+    out_project()
+    norm_rows()
+    g_spread(2, 0, 1)
+    g_cross(2, 1, 0)
+    d_round(2, 0, False)
+    g_line(3, 0, 1)
+    d_round(1, 1, True)
+    g_spread(3, 0, 1)
+    d_round(1, 0, True)
+    d_round(2, 0, True)
+    g_line(3, 1, 1)
+    g_cross(2, 0, 0)
+    g_cross(1, 0, 0)
+    g_cross(0, 0, 0)
+    g_cross(3, 0, 0)
+    g_spread(3, 1, 1)
+    g_cross(3, 1, 0)
+    g_spread(2, 1, 1)
+    g_cross(1, 1, 0)
+    d_round(2, 1, False)
+    g_sibling(0)
+    g_cross(3, 1, 1)
+    transpose_into(r.tokt, tok, D)
+    g_cross(1, 1, 1)
+    g_cross(1, 0, 1)
+    g_cross(2, 0, 1)
+    d_round(2, 1, True)
+    g_cross(3, 0, 1)
+    g_cross(2, 1, 1)
+    got_rows(0, r.feed.at[theirs])
+    gated(0)
+    g_sibling(1)
+    d_round(3, 1, True)
+    d_round(3, 0, True)
+    gated(1)
+    d_sibling()
+    transpose_into(r.mixt, r.mixed, D)
     down(theirs, keep_send)
-    swap_rows(1, r.bsend, r.brecv)
     down(mine, keep_own)
     transpose_into(r.feedt, r.feed, D)
-    got_rows(1, r.brecv)
+    for j in range(D // step_ff):
+        got(None, r.brecv.at[:, pl.ds(j * step_ff, step_ff)], r.r_part.at[j])
 
     r.pool[...] = jnp.zeros((8, D), F32)
 
@@ -1078,9 +1157,10 @@
             gate = r.gate[rows_of, pl.ds(o, stripe)]
             up = r.up[rows_of, pl.ds(o, stripe)]
             sig = jax.nn.sigmoid(gate)
-            r.dgu[rows_of, pl.ds(o, stripe)] = (
+            w_at = aligned((2 * (j // per_part)) * part_ff + (j % per_part) * stripe, LANES)
+            r.dgu[rows_of, pl.ds(w_at, stripe)] = (
                 slope * up * (sig * (1.0 + gate * (1.0 - sig)))).astype(BF)
-            r.dgu[rows_of, pl.ds(half_ff + o, stripe)] = (slope * (gate * sig)).astype(BF)
+            r.dgu[rows_of, pl.ds(aligned(w_at + part_ff, LANES), stripe)] = (slope * (gate * sig)).astype(BF)
             return carry
 
         lax.fori_loop(0, line, body, 0)
@@ -1379,7 +1459,7 @@
         val = sum(dot_tt(dqkv[:, pl.ds(h * third, third)],
                          rows_of_weight(wa, j, h * half_a, third)) for h in range(2))
         span = pl.ds(aligned(j * some, LANES), some)
-        r.o_tok[:, span] = r.n1[:, span] + val
+        r.xh2[:, span] = r.n1[:, span] + val
         return carry
 
     hidden_back(theirs)
@@ -1450,6 +1530,7 @@
     gate_line(0, 2, 0)
     gate_line(1, 0, 1)
     lax.fori_loop(0, line // 2, token_back, 0)
+    keep_out(9, r.xh2, r.o_tok)
     gate_line(3, 1, 0)
     gate_end(0)
     ready_a(0)
@@ -1546,8 +1627,10 @@
             a_ref[:, h * half_a + third : (h + 1) * half_a].astype(F32))
         for s in range(plan.line):
             to = pl.ds((2 * s + h) * stripe, stripe)
-            o_gate[:, to] = gu_ref[h, :, pl.ds(s * stripe, stripe)].astype(F32)
-            o_up[:, to] = gu_ref[h, :, pl.ds(half_ff + s * stripe, stripe)].astype(F32)
+            per_part, part_ff = plan.line // 2, half_ff // 2
+            lo = 2 * (s // per_part) * part_ff + (s % per_part) * stripe
+            o_gate[:, to] = gu_ref[h, :, pl.ds(lo, stripe)].astype(F32)
+            o_up[:, to] = gu_ref[h, :, pl.ds(lo + part_ff, stripe)].astype(F32)
     o_down[...] = dn_ref[...].astype(F32)
     o_tok[0] = tok_ref[...]
     o_q[...] = q_ref[...]
@@ -1566,8 +1649,6 @@
                      w_up, w_down, ln1_gain, first_layernorm_shift, ln2_gain, ln2_bias):
     count, groups, shard, vec = plan.count, plan.groups, plan.shard, plan.vec
     cosines, sines = rotary_constants(count)
-    tile = jnp.pad(jnp.stack([ln1_gain, first_layernorm_shift, ln2_gain, ln2_bias]),
-                   ((0, 12), (0, LANES - vec)))
     vmem = pl.BlockSpec(memory_space=pltpu.VMEM)
     smem = pl.BlockSpec(memory_space=pltpu.SMEM)
     hbm = pl.BlockSpec(memory_space=pl.ANY)
@@ -1579,13 +1660,14 @@
             shape((plan.shard_ff, D), BF), shape((8, D), F32), shape((QPD, D), F32),
             shape((1, D), F32), shape((8, LANES), F32),
         ),
-        in_specs=[smem, smem, smem, vmem, vmem, vmem, vmem, vmem] + [hbm] * 5,
-        out_specs=(vmem, hbm, hbm, hbm, vmem, vmem, vmem, vmem),
+        in_specs=[smem] * 3 + [hbm] * 3 + [vmem] * 4 + [hbm] * 5,
+        out_specs=(hbm, hbm, hbm, hbm, vmem, vmem, vmem, vmem),
         scratch_shapes=list(buffers(plan).values()) + list(semaphores(plan).values()),
         compiler_params=pltpu.CompilerParams(
             collective_id=0, has_side_effects=True, vmem_limit_bytes=63 * 1000 * 1000),
         name="whole_step",
-    )(query_lengths, doc_lengths, positives, positives[None], tokens[0], cosines, sines, tile,
+    )(query_lengths, doc_lengths, positives, tokens[0], cosines, sines, ln1_gain[None],
+      first_layernorm_shift[None], ln2_gain[None], ln2_bias[None],
       w_qkv, w_out, w_gate, w_up, w_down)
     o_tok, o_a, o_gu, o_dn, o_vec, o_q, o_d, o_loss = made
     outs = pl.pallas_call(

time: 173 us -> 165 us (0.954)
  Pallas kernels: 170 us -> 164 us
    pallas_call x1, Pallas kernels: 166 us -> 160 us  [on_device_kernel(): pl.pallas_call(functools.partial(whole_step, plan), out_shape=(shape((cou...]
where the time goes in v4:
time: 165 us
  Pallas kernels  164 us (99%)
    pallas_call x1, Pallas kernels, on_device_kernel(): pl.pallas_call(functools.partial(whole_step, plan), out_shape=(shape((cou...  160 us
    pallas_call x1, Pallas kernels, on_device_kernel(): pl.pallas_call(functools.partial(finish, plan), out_shape=(shape((1, 1),...  3.49 us

profile of v4, /device:TPU:0, one launch (start us, length us, event | category | flops | bytes accessed | tf_op | source)
XLA Modules:
  0.0 165.3 jit_solution(17740300173613497482)
XLA Ops:
  1.3 160.4 %whole_step.1 = (f32[256,768]{1,0:T(8,128)}, bf16[48,3072]{1,0:T(8,128)(2,1)}, bf16[2,48,3072]{2,1,0:T(8,128)(2,1)}, bf16[192,768]{1,0:T(8,128)(2,1)}, f32[8,768...) custom-call(s32[4]{0:T(128)} %refs_0_.1, s32[1]{0:T(128)S(6)} %copy.28.refs_1_, s32[64]{0:T(128)} %refs_2_.1, ...), custom_call_target="tpu_custom_call" | custom-call | tf_op jit(solution)/shard_map/whole_step/pallas_call | solution.py:1656
  161.7 3.5 %finish.1 = (f32[1,1]{1,0:T(1,128)}, f32[4,768]{1,0:T(4,128)}, f32[1,768]{1,0:T(1,128)}, f32[1,256,768]{2,1,0:T(8,128)}, f32[48,2304]{1,0:T(8,128)}, /*index=5*/...) custom-call(bf16[48,3072]{1,0:T(8,128)(2,1)} %get-tuple-element.34.r, ...), custom_call_target="tpu_custom_call" | custom-call | tf_op jit(solution)/shard_map/finish/pallas_call | solution.py:1673

commit v5 on v4

--- a/solution.py
+++ b/solution.py
@@ -409,6 +409,7 @@
         s_doc=dma((groups,)),
         r_slope=dma((groups,)),
         s_slope=dma((groups,)),
+        s_slope_q=dma((groups,)),
         r_query=dma((1,)),
         s_query=dma((1,)),
         s_ln=dma((line.bit_length() + 2,)),
@@ -464,6 +465,12 @@
         brecv=v((count, D), BF),
         xh2=v((count, D), F32),
         rs2=v((count, 1), F32),
+        xh2b=v((count, D), F32),
+        rs2b=v((count, 1), F32),
+        pwb=v((count, 1), F32),
+        brest=v((count, D), BF),
+        dpoolb=v((8, D), F32),
+        dpoolr=v((8, D), F32),
         dbr=v((pair, D), BF),
         dsend=v((count, D), BF),
         drecv=v((count, D), BF),
@@ -471,9 +478,9 @@
         pool=v((8, D), F32),
         dpool=v((8, D), F32),
         emb=v((8, D), F32),
-        embd=v((1, D), F32),
+        embd=v((1, D + LANES), F32),
         embq=v((QPD, D), F32),
-        dbuf=v((groups, 1, D), F32),
+        dbuf=v((groups, 1, D + LANES), F32),
         cbuf=v((groups, 1, D), F32),
         csend=v((groups, 1, D), F32),
         qrecv=v((QPD, D), F32),
@@ -770,9 +777,10 @@
     r.hide[...] = jnp.where(seen, 0.0, -1e30)
     for s in range(QPD):
         part = pl.ds(s * quarter, quarter)
-        length = jnp.full((quarter, 1), r.qlen[s] * (1 - t) + r.dlen[0] * t, jnp.int32)
-        slot = lax.broadcasted_iota(jnp.int32, (quarter, 1), 0) + s * quarter * t
-        r.pw[part, :] = jnp.where(slot < length, 1.0 / length.astype(F32), 0.0)
+        for tower, weights in ((t, r.pw), (1 - t, r.pwb)):
+            length = jnp.full((quarter, 1), r.qlen[s] * (1 - tower) + r.dlen[0] * tower, jnp.int32)
+            slot = lax.broadcasted_iota(jnp.int32, (quarter, 1), 0) + s * quarter * tower
+            weights[part, :] = jnp.where(slot < length, 1.0 / length.astype(F32), 0.0)
     lanes = lax.broadcasted_iota(jnp.int32, (count, LANES), 1)
     first_head = lanes < HEAD
     low_half = (lanes & (HEAD - 1)) < HEAD // 2
@@ -933,6 +941,23 @@
 
     def keep_own(o, val):
         r.bown[:, pl.ds(o, step_ff)] = val
+        r.dsend[:, pl.ds(o, step_ff)] = val.astype(BF)
+
+    rest = copy(r.dsend, r.brest, r.sx.at[1], r.rx.at[1], dev_y)
+
+    def norm_two_partner():
+        got_rows(1, r.brest)
+
+        def body(b, carry):
+            part = pl.ds(aligned(b * quarter, quarter), quarter)
+            feed = r.feed[pl.ds(aligned((1 - t) * count + b * quarter, quarter), quarter), :]
+            h = feed.astype(F32) + (r.bsend[part, :].astype(F32) + r.brest[part, :].astype(F32))
+            centred, inverse = moments(h)
+            r.xh2b[part, :] = centred * inverse
+            r.rs2b[part, :] = inverse
+            return carry
+
+        lax.fori_loop(0, blocks, body, 0)
 
     g_start(0)
     d_cross()
@@ -1030,6 +1055,7 @@
     transpose_into(r.mixt, r.mixed, D)
     down(theirs, keep_send)
     down(mine, keep_own)
+    do(t == 0, rest.start)
     transpose_into(r.feedt, r.feed, D)
     for j in range(D // step_ff):
         got(None, r.brecv.at[:, pl.ds(j * step_ff, step_ff)], r.r_part.at[j])
@@ -1063,38 +1089,86 @@
     r.dpool[...] = jnp.zeros((8, D), F32)
     r.ln[0] = jnp.zeros((8, D), F32)
 
-    def to_all(tower, src, dst, ssem, rsem):
+    def to_all(tower, src, dst, ssem, rsem, others=False):
         def give(step, carry):
             j = (me + step) % groups
             copy(src(j), dst.at[me], ssem.at[j], rsem.at[me], {TOWER: tower, DP: j}).start()
             return carry
 
-        lax.fori_loop(0, groups, give, 0)
-
-    def from_all(dst, ssem, rsem):
-        def take(j, carry):
+        lax.fori_loop(1 if others else 0, groups, give, 0)
+
+    def from_all(dst, ssem, rsem, others=False):
+        def take(step, carry):
+            j = (me + step) % groups
             copy(dst.at[j], dst.at[j], ssem.at[j], rsem.at[j], dev_x).wait_recv()
             return carry
 
-        lax.fori_loop(0, groups, take, 0)
-
-    @pl.when(t == 1)
-    def _():
-        r.embd[...] = r.emb[0:1, :]
-        r.dbuf[me] = r.emb[0:1, :]
-        to_all(0, lambda j: r.embd, r.dbuf, r.s_doc, r.r_doc)
-        from_all(r.cbuf, r.s_slope, r.r_slope)
+        lax.fori_loop(1 if others else 0, groups, take, 0)
+
+    zero_row = jnp.zeros((1, D), F32)
+
+    def norm_two_back(weights, slopes, hats, inverses, tower, own):
+        def body(b, sums):
+            part = pl.ds(aligned(b * quarter, quarter), quarter)
+            top = weights[part, :] * slopes[pl.ds(b, 1), :]
+            hat = hats[part, :]
+            inner = top * r.vec[2:3, :]
+            grad = inverses[part, :] * (
+                inner - jnp.mean(inner, -1, keepdims=True)
+                - hat * jnp.mean(inner * hat, -1, keepdims=True))
+            r.dbr[pl.ds(aligned(tower * count + b * quarter, quarter), quarter), :] = (
+                grad.astype(BF))
+            if not own:
+                return sums
+            r.n1[part, :] = grad
+            return (sums[0] + jnp.sum(top * hat, 0, keepdims=True),
+                    sums[1] + jnp.sum(top, 0, keepdims=True))
+
+        sums = lax.fori_loop(0, blocks, body, (zero_row, zero_row))
+        if own:
+            r.ln[0] = (r.ln[0] + jnp.where(row8 == 2, sums[0], 0.0)
+                       + jnp.where(row8 == 3, sums[1], 0.0))
+
+    def back_own():
+        norm_two_back(r.pw, r.dpool, r.xh2, r.rs2, t, True)
+
+    def back_partner():
+        norm_two_back(r.pwb, r.dpoolb, r.xh2b, r.rs2b, 1 - t, False)
+
+    def hidden_back(rows_of):
+        def body(j, carry):
+            o = aligned(j * stripe, LANES)
+            w = wd[j].reshape(stripe, D)
+            slope = dot_tt(r.dbr[rows_of, :], w)
+            gate = r.gate[rows_of, pl.ds(o, stripe)]
+            up = r.up[rows_of, pl.ds(o, stripe)]
+            sig = jax.nn.sigmoid(gate)
+            w_at = aligned((2 * (j // per_part)) * part_ff + (j % per_part) * stripe, LANES)
+            r.dgu[rows_of, pl.ds(w_at, stripe)] = (
+                slope * up * (sig * (1.0 + gate * (1.0 - sig)))).astype(BF)
+            r.dgu[rows_of, pl.ds(aligned(w_at + part_ff, LANES), stripe)] = (slope * (gate * sig)).astype(BF)
+            return carry
+
+        lax.fori_loop(0, line, body, 0)
+
+    def slope_back(slope, emb, scale_of):
+        return scale_of * (slope - emb * jnp.sum(slope * emb, -1, keepdims=True))
+
+    def doc_slope():
         total = r.cbuf[0]
         for j in range(1, groups):
             total = total + r.cbuf[j]
-        r.dpool[0:1, :] = total
+        return total
+
+    pool_slope = copy(r.dpool, r.dpoolr, r.sx.at[2], r.rx.at[2], dev_y)
+    tail.append((t == 0, pool_slope))
 
     @pl.when(t == 0)
     def _():
         r.embq[...] = r.emb[0:QPD, :]
         from_all(r.dbuf, r.s_doc, r.r_doc)
         for j in range(groups):
-            r.dflat[pl.ds(j, 1), :] = r.dbuf[j]
+            r.dflat[pl.ds(j, 1), :] = r.dbuf[j, :, pl.ds(0, D)]
         docs, queries = r.dflat[...], r.embq[...]
         logits = dot_tt(queries, docs, best) / contrast_sharpness_factor
         peak = jnp.max(logits, -1, keepdims=True)
@@ -1110,60 +1184,49 @@
         for j in range(groups):
             r.csend[j] = back[j : j + 1, :]
         to_all(1, lambda j: r.csend.at[j], r.cbuf, r.s_slope, r.r_slope)
+        to_all(0, lambda j: r.csend.at[j], r.cbuf, r.s_slope_q, r.r_slope, True)
+        r.cbuf[me] = r.csend[me]
         r.dpool[0:QPD, :] = jnp.dot(slope, docs, preferred_element_type=F32, precision=best)
+        r.dpool[...] = slope_back(r.dpool[...], r.emb[...], shrink)
+        pool_slope.start()
         picked = jnp.sum(jnp.where(hot > 0.5, logits, 0.0), -1, keepdims=True)
         total = jnp.sum(lse - picked, 0, keepdims=True)
         r.ln[0] = jnp.where(row8 == 4, total, 0.0)
-
-    slope = r.dpool[...]
-    emb = r.emb[...]
-    dpool = shrink * (slope - emb * jnp.sum(slope * emb, -1, keepdims=True))
+        back_own()
+
+    @pl.when(t == 1)
+    def _():
+        r.embd[:, 0:D] = r.emb[0:1, :]
+        r.embd[:, D:] = jnp.broadcast_to(shrink[0:1, :], (1, LANES))
+        r.dbuf[me] = r.embd[...]
+        to_all(0, lambda j: r.embd, r.dbuf, r.s_doc, r.r_doc)
+        rest.start()
+        norm_two_partner()
+        got_rows(2, r.dpoolr)
+        r.dpoolb[...] = r.dpoolr[...]
+        back_partner()
+
+    hidden_back(pl.ds(0, count))
+
+    @pl.when(t == 1)
+    def _():
+        from_all(r.cbuf, r.s_slope, r.r_slope)
+        row = slope_back(doc_slope(), r.emb[0:1, :], shrink[0:1, :])
+        r.dpool[...] = jnp.broadcast_to(row, (8, D))
+        back_own()
 
     @pl.when(t == 0)
     def _():
-        r.dpool[...] = dpool
-
-    @pl.when(t == 1)
-    def _():
-        r.dpool[...] = jnp.broadcast_to(dpool[0:1, :], (8, D))
-
-    def norm_two_back(b, sums):
-        part = pl.ds(aligned(b * quarter, quarter), quarter)
-        top = r.pw[part, :] * r.dpool[pl.ds(b, 1), :]
-        hat = r.xh2[part, :]
-        inner = top * r.vec[2:3, :]
-        grad = r.rs2[part, :] * (
-            inner - jnp.mean(inner, -1, keepdims=True)
-            - hat * jnp.mean(inner * hat, -1, keepdims=True))
-        r.n1[part, :] = grad
-        r.dbr[pl.ds(aligned(t * count + b * quarter, quarter), quarter), :] = (
-            grad.astype(BF))
-        return (sums[0] + jnp.sum(top * hat, 0, keepdims=True),
-                sums[1] + jnp.sum(top, 0, keepdims=True))
-
-    zero_row = jnp.zeros((1, D), F32)
-    gain_two, bias_two = lax.fori_loop(0, blocks, norm_two_back, (zero_row, zero_row))
-    swap_rows(2, r.dbr.at[mine], r.dbr.at[mine])
-
+        norm_two_partner()
+        from_all(r.cbuf, r.s_slope_q, r.r_slope, True)
+        doc = r.dbuf[me]
+        row = slope_back(doc_slope(), doc[:, 0:D], doc[:, D : D + 1])
+        r.dpoolb[...] = jnp.broadcast_to(row, (8, D))
+        back_partner()
+
+    hidden_back(pl.ds(count, count))
+    rest.wait_send()
     send(t == 0, copy(r.embq, r.qrecv, r.s_query.at[0], r.r_query.at[0], dev_y), tail)
-    r.ln[0] = (r.ln[0] + jnp.where(row8 == 2, gain_two, 0.0)
-               + jnp.where(row8 == 3, bias_two, 0.0))
-
-    def hidden_back(rows_of):
-        def body(j, carry):
-            o = aligned(j * stripe, LANES)
-            w = wd[j].reshape(stripe, D)
-            slope = dot_tt(r.dbr[rows_of, :], w)
-            gate = r.gate[rows_of, pl.ds(o, stripe)]
-            up = r.up[rows_of, pl.ds(o, stripe)]
-            sig = jax.nn.sigmoid(gate)
-            w_at = aligned((2 * (j // per_part)) * part_ff + (j % per_part) * stripe, LANES)
-            r.dgu[rows_of, pl.ds(w_at, stripe)] = (
-                slope * up * (sig * (1.0 + gate * (1.0 - sig)))).astype(BF)
-            r.dgu[rows_of, pl.ds(aligned(w_at + part_ff, LANES), stripe)] = (slope * (gate * sig)).astype(BF)
-            return carry
-
-        lax.fori_loop(0, line, body, 0)
 
     def along(step):
         for s in range(1, line):
@@ -1210,15 +1273,9 @@
 
     gd = r.gd
 
-    def down_half(s, rows_of):
-        return jnp.dot(r.hidt[pl.ds(s * stripe, stripe), rows_of], r.dbr[rows_of, :],
-                       preferred_element_type=F32)
-
-    def down_own(s):
-        gd[s] = down_half(s, mine).astype(BF).reshape(2, shard_ff, D)
-
     def down_grad(s):
-        val = down_half(s, theirs) + gd[s].reshape(stripe, D).astype(F32)
+        val = jnp.dot(r.hidt[pl.ds(s * stripe, stripe), :], r.dbr[...],
+                      preferred_element_type=F32)
         gd[s] = val.astype(BF).reshape(2, shard_ff, D)
         send(None, copy(gd.at[s, 1 - c], r.gd_rc.at[s], r.gd_c.at[0, s],
                         r.gd_c.at[1, s], dev_c), tail)
@@ -1256,17 +1313,9 @@
     gg = r.gg
     part_gu = ff // 4
 
-    def gate_half(k, rows_of):
-        return jnp.dot(r.feedt[:, rows_of], r.dgu[rows_of, pl.ds(k * part_gu, part_gu)],
-                       preferred_element_type=F32)
-
-    def gate_own(k):
-        gg[:, :, :, :, pl.ds(k * part_gu, part_gu)] = gate_half(k, mine).astype(BF).reshape(
-            line, 2, 2, shard, part_gu)
-
     def gate_grad(k):
         span = pl.ds(k * part_gu, part_gu)
-        val = gate_half(k, theirs) + gg[:, :, :, :, span].reshape(groups * shard, part_gu).astype(F32)
+        val = jnp.dot(r.feedt[...], r.dgu[:, span], preferred_element_type=F32)
         gg[:, :, :, :, span] = val.astype(BF).reshape(line, 2, 2, shard, part_gu)
         send(None, copy(gg.at[:, :, 1 - c, :, span], r.gg_rc.at[:, :, :, span],
                         r.gg_c.at[0, k], r.gg_c.at[1, k], dev_c), tail)
@@ -1376,17 +1425,9 @@
         send(None, copy(r.dsend.at[:, span], r.drecv.at[:, span], r.s_back.at[j], r.r_back.at[j],
                         dev_y), tail)
 
-    def back_own(j, span, val):
+    def feed_own(j, span, val):
         r.bown[:, span] = val
 
-    hidden_back(mine)
-    for j in range(line // 2):
-        feed_part(mine, j, back_own)
-    for s in range(line):
-        down_own(s)
-    for k in range(4):
-        gate_own(k)
-    got_rows(2, r.dbr.at[theirs])
     def norm_one_back(b, sums):
         part = pl.ds(aligned(b * quarter, quarter), quarter)
         top = r.n1[part, :] + r.bown[part, :] + r.drecv[part, :].astype(F32)
@@ -1462,148 +1503,150 @@
         r.xh2[:, span] = r.n1[:, span] + val
         return carry
 
-    hidden_back(theirs)
     gate_grad(0)
     feed_part(theirs, 0, back_send)
+    down_grad(1)
+    down_grad(0)
+    gate_cross(0)
     down_grad(3)
-    down_grad(0)
-    down_grad(1)
-    gate_cross(0)
     down_grad(2)
     feed_part(theirs, 1, back_send)
     down_arrive()
     down_line(0, 0)
     gate_grad(1)
+    down_line(0, 1)
+    gate_grad(2)
+    feed_part(mine, 0, feed_own)
     gate_cross(1)
     gate_grad(3)
-    gate_grad(2)
-    down_line(0, 1)
+    down_line(0, 2)
+    feed_part(mine, 1, feed_own)
+    gate_ready(0)
     norm_back()
     settle(pending)
     out_grad()
+    gate_cross(3)
     small_sums(0)
+    down_line(1, 0)
+    mix_back()
+    over_pairs(1 - t, attend_back, 0, 1)
+    tower_a(3)
     gate_cross(2)
-    mix_back()
-    over_pairs(1 - t, attend_back, 0, 2)
-    gate_ready(0)
-    tower_a(3)
-    over_pairs(1 - t, attend_back, 2, 3)
+    over_pairs(1 - t, attend_back, 1, 3)
+    store_qkv(0, 1 - t)
+    over_pairs(t, attend_back, 0, 1)
+    store_qkv(1, 1 - t)
+    over_pairs(t, attend_back, 1, 2)
+    gate_line(0, 0, 0)
+    down_line(1, 1)
+    tower_a(0)
+    gate_line(0, 0, 1)
+    down_line(2, 0)
+    gate_ready(3)
+    tower_a(1)
+    over_pairs(t, attend_back, 2, 3)
+    cross_a(3)
+    store_qkv(2, 1 - t)
+    gate_line(3, 0, 0)
+    store_qkv(0, t)
+    gate_line(0, 0, 2)
+    store_qkv(2, t)
+    gate_ready(2)
+    gate_line(2, 0, 0)
+    gate_line(3, 0, 1)
+    tower_a(2)
+    gate_line(0, 1, 0)
+    cross_a(0)
+    ready_a(3)
+    gate_line(0, 2, 0)
+    gate_line(3, 1, 0)
+    gate_line(0, 1, 1)
+    down_end()
     gate_ready(1)
-    gate_line(0, 0, 1)
-    down_line(1, 0)
-    gate_cross(3)
-    store_qkv(0, 1 - t)
-    gate_line(0, 0, 0)
-    gate_line(0, 0, 2)
-    store_qkv(2, 1 - t)
     gate_line(1, 0, 0)
-    store_qkv(1, 1 - t)
-    over_pairs(t, attend_back, 0, 1)
-    down_line(1, 1)
-    down_line(0, 2)
-    over_pairs(t, attend_back, 1, 2)
-    tower_a(0)
-    down_line(2, 0)
-    over_pairs(t, attend_back, 2, 3)
-    tower_a(2)
-    store_qkv(0, t)
-    gate_ready(2)
-    store_qkv(2, t)
-    cross_a(3)
+    gate_line(2, 1, 0)
     store_qkv(1, t)
-    gate_line(2, 0, 1)
-    gate_line(1, 0, 2)
-    gate_ready(3)
-    gate_line(0, 1, 0)
-    tower_a(1)
-    cross_a(0)
-    down_end()
-    ready_a(3)
-    gate_line(2, 0, 0)
-    gate_line(1, 1, 0)
-    gate_line(3, 0, 0)
-    gate_line(0, 1, 1)
+    line_a(3, 1, 0)
+    line_a(3, 0, 0)
     line_a(3, 0, 1)
-    line_a(3, 0, 0)
-    gate_line(3, 0, 1)
-    gate_line(2, 1, 1)
-    gate_line(0, 2, 0)
-    gate_line(1, 0, 1)
     lax.fori_loop(0, line // 2, token_back, 0)
     keep_out(9, r.xh2, r.o_tok)
-    gate_line(3, 1, 0)
+    gate_line(3, 1, 1)
+    cross_a(1)
     gate_end(0)
+    line_a(3, 2, 0)
+    small_sums(1)
+    gate_line(2, 2, 0)
+    gate_line(2, 0, 1)
+    gate_line(1, 0, 1)
+    gate_line(1, 1, 0)
+    line_a(3, 0, 2)
+    gate_line(2, 0, 2)
     ready_a(0)
-    small_sums(1)
-    gate_line(2, 1, 0)
+    down_out()
+    gate_line(3, 0, 2)
+    gate_line(2, 1, 1)
     line_a(0, 0, 0)
+    line_a(3, 1, 1)
+    gate_line(1, 1, 1)
+    line_a(0, 0, 1)
+    gate_line(3, 2, 0)
     cross_a(2)
-    gate_line(3, 0, 2)
-    down_out()
-    cross_a(1)
-    gate_line(3, 2, 0)
-    gate_line(2, 2, 0)
-    gate_line(1, 1, 1)
+    gate_end(2)
+    ready_a(1)
+    small_sums(2)
+    line_a(1, 0, 0)
     gate_line(1, 2, 0)
-    gate_line(2, 0, 2)
+    line_a(1, 0, 2)
     line_a(0, 1, 0)
+    line_a(1, 0, 1)
+    line_a(1, 1, 0)
     ready_a(2)
-    line_a(3, 1, 0)
     line_a(2, 0, 0)
+    end_a(3)
+    line_a(1, 1, 1)
+    gate_end(3)
+    gate_line(1, 0, 2)
+    line_a(0, 2, 0)
     line_a(2, 0, 1)
-    line_a(0, 0, 1)
-    small_sums(2)
-    line_a(3, 1, 1)
     line_a(2, 1, 0)
-    ready_a(1)
-    gate_line(3, 1, 1)
-    line_a(1, 0, 0)
-    line_a(1, 0, 1)
-    line_a(3, 0, 2)
-    gate_end(2)
-    line_a(3, 2, 0)
+    line_a(0, 0, 2)
+    line_a(1, 2, 0)
     line_a(0, 1, 1)
+    line_a(2, 0, 2)
     gate_end(1)
-    line_a(1, 1, 0)
-    line_a(0, 0, 2)
-    line_a(2, 0, 2)
-    line_a(0, 2, 0)
+    small_sums(3)
     line_a(2, 1, 1)
-    gate_end(3)
-    line_a(1, 0, 2)
-    line_a(1, 1, 1)
     line_a(2, 2, 0)
-    small_sums(3)
-    end_a(3)
-    line_a(1, 2, 0)
     end_a(0)
+    end_a(1)
+    small_sums(4)
     end_a(2)
-    small_sums(4)
-    end_a(1)
     small_sums(5)
 
     r.o_vec[...] = r.ln[last]
     r.o_loss[...] = r.ln[last][:, 0:LANES] * (1.0 / (groups * QPD))
 
-    r.o_d[...] = r.dbuf[me]
-
-    def sent(ssem):
-        def body(j, carry):
-            copy(r.embd, r.embd, ssem.at[j], r.r_query.at[0], dev_x).wait_send()
+    r.o_d[...] = r.dbuf[me, :, pl.ds(0, D)]
+
+    def sent(ssem, src, others=False):
+        def body(step, carry):
+            copy(src, src, ssem.at[(me + step) % groups], r.r_query.at[0], dev_x).wait_send()
             return carry
 
-        lax.fori_loop(0, groups, body, 0)
+        lax.fori_loop(1 if others else 0, groups, body, 0)
 
     @pl.when(t == 0)
     def _():
         r.o_q[...] = r.embq[...]
-        sent(r.s_slope)
+        sent(r.s_slope, r.csend.at[0])
+        sent(r.s_slope_q, r.csend.at[0], True)
 
     @pl.when(t == 1)
     def _():
         got(None, r.qrecv, r.r_query.at[0])
         r.o_q[...] = r.qrecv[...]
-        sent(r.s_doc)
+        sent(r.s_doc, r.embd)
 
     got(x != t, r.o_dn, r.gd_y.at[1])
     for k in range(4):

time: 165 us -> 160 us (0.970)
  Pallas kernels: 164 us -> 158 us
    pallas_call x1, Pallas kernels: 160 us -> 155 us  [on_device_kernel(): pl.pallas_call(functools.partial(whole_step, plan), out_shape=(shape((cou...]
where the time goes in v5:
time: 160 us
  Pallas kernels  158 us (99%)
    pallas_call x1, Pallas kernels, on_device_kernel(): pl.pallas_call(functools.partial(whole_step, plan), out_shape=(shape((cou...  155 us
    pallas_call x1, Pallas kernels, on_device_kernel(): pl.pallas_call(functools.partial(finish, plan), out_shape=(shape((1, 1),...  3.49 us

profile of v5, /device:TPU:0, one launch (start us, length us, event | category | flops | bytes accessed | tf_op | source)
XLA Modules:
  0.0 159.8 jit_solution(18152790035818325039)
XLA Ops:
  1.3 154.9 %whole_step.1 = (f32[256,768]{1,0:T(8,128)}, bf16[48,3072]{1,0:T(8,128)(2,1)}, bf16[2,48,3072]{2,1,0:T(8,128)(2,1)}, bf16[192,768]{1,0:T(8,128)(2,1)}, f32[8,768...) custom-call(s32[4]{0:T(128)} %refs_0_.1, s32[1]{0:T(128)S(6)} %copy.28.refs_1_, s32[64]{0:T(128)} %refs_2_.1, ...), custom_call_target="tpu_custom_call" | custom-call | tf_op jit(solution)/shard_map/whole_step/pallas_call | solution.py:1699
  156.2 3.5 %finish.1 = (f32[1,1]{1,0:T(1,128)}, f32[4,768]{1,0:T(4,128)}, f32[1,768]{1,0:T(1,128)}, f32[1,256,768]{2,1,0:T(8,128)}, f32[48,2304]{1,0:T(8,128)}, /*index=5*/...) custom-call(bf16[48,3072]{1,0:T(8,128)(2,1)} %get-tuple-element.34.r, ...), custom_call_target="tpu_custom_call" | custom-call | tf_op jit(solution)/shard_map/finish/pallas_call | solution.py:1716

commit v6 on v5

--- a/solution.py
+++ b/solution.py
@@ -393,12 +393,13 @@
         sg_z=dma((2, line, 2)),
         sg_x=dma((line, 2)),
         sg_c=dma((line, 2, 2)),
-        rd=dma((line, 2)),
-        sd_x=dma((1,)),
-        sd_z=dma((2, line)),
-        sd_c=dma((line,)),
+        rd=dma((line, 2, 2)),
+        sd_x=dma((2,)),
+        sd_z=dma((2, line, 2)),
+        sd_c=dma((line, 2)),
         rv=dma((groups,)),
         sv=dma((groups,)),
+        turn=pltpu.SemaphoreType.REGULAR,
         s_part=dma((D // (2 * LANES),)),
         r_part=dma((D // (2 * LANES),)),
         s_back=dma((line,)),
@@ -716,33 +717,35 @@
             for xx in range(2):
                 got_g(None, zz, xx, 1 - c, h)
 
-    def send_d(cond, sem, zz, dev):
-        ref = wd.at[zz, c]
-        send(cond, copy(ref, ref, sem, r.rd.at[zz, c], dev))
-
-    def got_d(cond, zz, cc):
-        got(cond, wd.at[zz, cc], r.rd.at[zz, cc])
-
-    def d_cross():
-        send_d(x == t, r.sd_x.at[0], z, dev_x)
-
-    def d_start():
-        got_d(x != t, z, c)
+    part_d = (pl.ds(0, 4 * LANES), pl.ds(4 * LANES, D - 4 * LANES))
+
+    def send_d(cond, sem, zz, h, dev):
+        ref = wd.at[zz, c, :, part_d[h]]
+        send(cond, copy(ref, ref, sem, r.rd.at[zz, c, h], dev))
+
+    def got_d(cond, zz, cc, h):
+        got(cond, wd.at[zz, cc, :, part_d[h]], r.rd.at[zz, cc, h])
+
+    def d_cross(h):
+        send_d(x == t, r.sd_x.at[h], z, h, dev_x)
+
+    def d_start(h):
+        got_d(x != t, z, c, h)
         for way, (_, _, on, nxt) in enumerate(sides(0)):
-            send_d(on, r.sd_z.at[way, z], z, dev_z(nxt))
-        send_d(None, r.sd_c.at[z], z, dev_c)
-
-    def d_round(step, way, ends):
+            send_d(on, r.sd_z.at[way, z, h], z, h, dev_z(nxt))
+        send_d(None, r.sd_c.at[z, h], z, h, dev_c)
+
+    def d_round(step, way, ends, h):
         zz, there, on, nxt = sides(step)[way]
         cond = both(there, jnp.logical_not(on) if ends else on)
-        got_d(cond, zz, c)
+        got_d(cond, zz, c, h)
         if not ends:
-            send_d(cond, r.sd_z.at[way, zz], zz, dev_z(nxt))
-        send_d(cond, r.sd_c.at[zz], zz, dev_c)
-
-    def d_sibling():
+            send_d(cond, r.sd_z.at[way, zz, h], zz, h, dev_z(nxt))
+        send_d(cond, r.sd_c.at[zz, h], zz, h, dev_c)
+
+    def d_sibling(h):
         for zz in range(line):
-            got_d(None, zz, 1 - c)
+            got_d(None, zz, 1 - c, h)
 
     def v_send(j, carry):
         @pl.when(j != me)
@@ -917,20 +920,18 @@
                          preferred_element_type=F32)
             r.gate[:, pl.ds(o, step_ff)] = gate
             r.up[:, pl.ds(o, step_ff)] = up
-            hidden = (gate * jax.nn.sigmoid(gate) * up).astype(BF)
-            r.dgu[:, pl.ds(o, step_ff)] = hidden
-            r.hidt[pl.ds(o, step_ff), :] = hidden.T
+            r.dgu[:, pl.ds(o, step_ff)] = (gate * jax.nn.sigmoid(gate) * up).astype(BF)
             return carry
 
         lax.fori_loop(0, steps_part, body, 0)
 
-    def down(rows_of, store):
+    def down(rows_of, store, which=range(D // (2 * LANES))):
         def body(j):
             o = j * step_ff
             w = wd[:, :, :, pl.ds(o, step_ff)].reshape(half_ff, step_ff)
             store(o, jnp.dot(r.dgu[rows_of, pl.ds(0, half_ff)], w, preferred_element_type=F32))
 
-        for j in range(D // step_ff):
+        for j in which:
             body(j)
 
     def keep_send(o, val):
@@ -959,106 +960,132 @@
 
         lax.fori_loop(0, blocks, body, 0)
 
+    d_cross(1)
+    g_start(1)
+    a_round(1, 0)
+    a_cross(0, 0)
+    a_round(1, 1)
+    g_spread(0, 0, 0)
+    d_cross(0)
     g_start(0)
-    d_cross()
-    a_round(1, 0)
-    a_round(1, 1)
-    g_line(1, 0, 0)
-    g_line(1, 1, 0)
-    a_cross(0, 0)
+    a_cross(1, 0)
     a_round(2, 1)
     a_round(2, 0)
-    a_cross(1, 0)
-    g_start(1)
+    a_round(3, 0)
+    g_line(1, 0, 1)
+    vectors()
+    transpose_into(r.tokt, tok, D)
+    g_line(1, 0, 0)
+    g_line(1, 1, 1)
+    g_line(1, 1, 0)
+    a_cross(1, 1)
+    a_round(3, 1)
+    a_tower(1, 0)
+    g_spread(1, 1, 1)
+    g_spread(1, 0, 0)
+    d_start(1)
+    g_line(2, 1, 1)
+    d_round(1, 0, False, 1)
+    a_tower(0, 0)
     g_spread(0, 0, 1)
-    a_cross(1, 1)
-    g_line(2, 1, 0)
-    g_line(2, 0, 0)
-    a_round(3, 0)
-    a_round(3, 1)
-    g_line(1, 0, 1)
     a_cross(2, 0)
     a_cross(2, 1)
-    g_spread(1, 1, 0)
-    g_line(1, 1, 1)
+    a_cross(3, 0)
+    a_tower(1, 1)
+    g_line(2, 0, 1)
+    g_spread(2, 1, 1)
+    g_line(2, 0, 0)
+    a_cross(3, 1)
+    d_round(1, 1, False, 1)
+    d_round(2, 0, False, 1)
+    a_sibling(t)
+    project(t)
+    over_pairs(t, attend, 0, 1)
+    g_line(2, 1, 0)
+    d_start(0)
+    over_pairs(t, attend, 1, 2)
+    a_tower(2, 1)
+    a_tower(2, 0)
     g_spread(2, 0, 0)
     g_spread(2, 1, 0)
-    d_start()
-    a_tower(1, 0)
-    g_spread(1, 0, 0)
-    g_line(3, 0, 0)
     g_spread(1, 0, 1)
-    g_spread(0, 0, 0)
-    a_cross(3, 0)
-    a_tower(0, 0)
-    a_cross(3, 1)
-    vectors()
-    g_line(2, 0, 1)
-    a_sibling(t)
-    g_spread(3, 0, 0)
-    project(t)
-    over_pairs(t, attend, 0, 1)
-    g_cross(0, 0, 1)
-    over_pairs(t, attend, 1, 2)
-    g_spread(1, 1, 1)
-    g_line(2, 1, 1)
-    g_line(3, 1, 0)
-    g_spread(3, 1, 0)
+    a_tower(3, 1)
+    over_pairs(t, attend, 2, 3)
+    g_line(3, 1, 1)
     a_tower(3, 0)
-    over_pairs(t, attend, 2, 3)
-    a_tower(1, 1)
-    a_tower(3, 1)
-    a_tower(2, 0)
-    a_tower(2, 1)
-    d_round(1, 0, False)
+    g_cross(0, 0, 0)
+    g_spread(3, 1, 1)
+    g_cross(1, 1, 1)
+    d_round(1, 1, True, 1)
     a_sibling(1 - t)
     project(1 - t)
-    over_pairs(1 - t, attend, 0, 1)
-    d_round(1, 1, False)
-    over_pairs(1 - t, attend, 1, 3)
+    over_pairs(1 - t, attend, 0, 2)
+    g_line(3, 0, 1)
+    over_pairs(1 - t, attend, 2, 3)
+    d_round(1, 1, False, 0)
+    g_spread(2, 0, 1)
     out_project()
+    g_line(3, 1, 0)
+    d_round(2, 1, True, 1)
+    g_spread(3, 1, 0)
     norm_rows()
-    g_spread(2, 0, 1)
+    g_line(3, 0, 0)
+    g_spread(3, 0, 1)
+    g_cross(2, 1, 1)
+    d_round(2, 0, True, 1)
+    g_cross(1, 0, 0)
+    d_round(1, 0, True, 1)
+    d_round(2, 1, False, 1)
+    transpose_into(r.mixt, r.mixed, D)
+    d_round(1, 0, False, 0)
+    g_spread(1, 1, 0)
+    d_round(2, 1, False, 0)
+    d_round(1, 1, True, 0)
+    g_cross(2, 0, 0)
+    g_cross(2, 0, 1)
+    g_cross(3, 1, 0)
+    g_cross(3, 1, 1)
+    d_round(2, 0, False, 0)
+    g_spread(3, 0, 0)
     g_cross(2, 1, 0)
-    d_round(2, 0, False)
-    g_line(3, 0, 1)
-    d_round(1, 1, True)
-    g_spread(3, 0, 1)
-    d_round(1, 0, True)
-    d_round(2, 0, True)
-    g_line(3, 1, 1)
-    g_cross(2, 0, 0)
-    g_cross(1, 0, 0)
-    g_cross(0, 0, 0)
+    g_cross(0, 0, 1)
+    d_round(3, 1, True, 1)
+    g_cross(3, 0, 1)
+    g_cross(1, 0, 1)
+    g_sibling(1)
+    d_round(3, 0, True, 1)
+    d_round(2, 1, True, 0)
+    d_round(2, 0, True, 0)
+    d_round(1, 0, True, 0)
     g_cross(3, 0, 0)
-    g_spread(3, 1, 1)
-    g_cross(3, 1, 0)
-    g_spread(2, 1, 1)
     g_cross(1, 1, 0)
-    d_round(2, 1, False)
+    got_rows(0, r.feed.at[theirs])
+    gated(1)
     g_sibling(0)
-    g_cross(3, 1, 1)
-    transpose_into(r.tokt, tok, D)
-    g_cross(1, 1, 1)
-    g_cross(1, 0, 1)
-    g_cross(2, 0, 1)
-    d_round(2, 1, True)
-    g_cross(3, 0, 1)
-    g_cross(2, 1, 1)
-    got_rows(0, r.feed.at[theirs])
     gated(0)
-    g_sibling(1)
-    d_round(3, 1, True)
-    d_round(3, 0, True)
-    gated(1)
-    d_sibling()
-    transpose_into(r.mixt, r.mixed, D)
-    down(theirs, keep_send)
+    d_sibling(1)
+    down(theirs, keep_send, (2,))
+    d_round(3, 1, True, 0)
+    d_round(3, 0, True, 0)
+    d_sibling(0)
+    down(theirs, keep_send, (0, 1))
     down(mine, keep_own)
-    do(t == 0, rest.start)
     transpose_into(r.feedt, r.feed, D)
+    transpose_into(r.hidt, r.dgu, half_ff)
+
+    def factors(j, carry):
+        span = pl.ds(aligned(j * LANES, LANES), LANES)
+        gate, up = r.gate[:, span], r.up[:, span]
+        sig = jax.nn.sigmoid(gate)
+        r.gate[:, span] = gate * sig
+        r.up[:, span] = up * (sig * (1.0 + gate * (1.0 - sig)))
+        return carry
+
+    lax.fori_loop(0, half_ff // LANES, factors, 0)
     for j in range(D // step_ff):
         got(None, r.brecv.at[:, pl.ds(j * step_ff, step_ff)], r.r_part.at[j])
+        if j == 0:
+            do(t == 0, rest.start)
 
     r.pool[...] = jnp.zeros((8, D), F32)
 
@@ -1140,13 +1167,11 @@
             o = aligned(j * stripe, LANES)
             w = wd[j].reshape(stripe, D)
             slope = dot_tt(r.dbr[rows_of, :], w)
-            gate = r.gate[rows_of, pl.ds(o, stripe)]
-            up = r.up[rows_of, pl.ds(o, stripe)]
-            sig = jax.nn.sigmoid(gate)
             w_at = aligned((2 * (j // per_part)) * part_ff + (j % per_part) * stripe, LANES)
             r.dgu[rows_of, pl.ds(w_at, stripe)] = (
-                slope * up * (sig * (1.0 + gate * (1.0 - sig)))).astype(BF)
-            r.dgu[rows_of, pl.ds(aligned(w_at + part_ff, LANES), stripe)] = (slope * (gate * sig)).astype(BF)
+                slope * r.up[rows_of, pl.ds(o, stripe)]).astype(BF)
+            r.dgu[rows_of, pl.ds(aligned(w_at + part_ff, LANES), stripe)] = (
+                slope * r.gate[rows_of, pl.ds(o, stripe)]).astype(BF)
             return carry
 
         lax.fori_loop(0, line, body, 0)
@@ -1200,6 +1225,8 @@
         r.embd[:, D:] = jnp.broadcast_to(shrink[0:1, :], (1, LANES))
         r.dbuf[me] = r.embd[...]
         to_all(0, lambda j: r.embd, r.dbuf, r.s_doc, r.r_doc)
+        pl.semaphore_signal(r.turn, inc=1, device_id=dev_c, device_id_type=MESH)
+        pl.semaphore_wait(r.turn, 1)
         rest.start()
         norm_two_partner()
         got_rows(2, r.dpoolr)

time: 160 us -> 158 us (0.988)
    pallas_call x1, Pallas kernels: 155 us -> 153 us  [on_device_kernel(): pl.pallas_call(functools.partial(whole_step, plan), out_shape=(shape((cou...]
where the time goes in v6:
time: 158 us
  Pallas kernels  157 us (99%)
    pallas_call x1, Pallas kernels, on_device_kernel(): pl.pallas_call(functools.partial(whole_step, plan), out_shape=(shape((cou...  153 us
    pallas_call x1, Pallas kernels, on_device_kernel(): pl.pallas_call(functools.partial(finish, plan), out_shape=(shape((1, 1),...  3.49 us

profile of v6, /device:TPU:0, one launch (start us, length us, event | category | flops | bytes accessed | tf_op | source)
XLA Modules:
  0.0 158.1 jit_solution(5441903743224727091)
XLA Ops:
  1.3 153.1 %whole_step.1 = (f32[256,768]{1,0:T(8,128)}, bf16[48,3072]{1,0:T(8,128)(2,1)}, bf16[2,48,3072]{2,1,0:T(8,128)(2,1)}, bf16[192,768]{1,0:T(8,128)(2,1)}, f32[8,768...) custom-call(s32[4]{0:T(128)} %refs_0_.1, s32[1]{0:T(128)S(6)} %copy.28.refs_1_, s32[64]{0:T(128)} %refs_2_.1, ...), custom_call_target="tpu_custom_call" | custom-call | tf_op jit(solution)/shard_map/whole_step/pallas_call | solution.py:1726
  154.4 3.5 %finish.1 = (f32[1,1]{1,0:T(1,128)}, f32[4,768]{1,0:T(4,128)}, f32[1,768]{1,0:T(1,128)}, f32[1,256,768]{2,1,0:T(8,128)}, f32[48,2304]{1,0:T(8,128)}, /*index=5*/...) custom-call(bf16[48,3072]{1,0:T(8,128)(2,1)} %get-tuple-element.34.r, ...), custom_call_target="tpu_custom_call" | custom-call | tf_op jit(solution)/shard_map/finish/pallas_call | solution.py:1743

commit v7 on v6

--- a/solution.py
+++ b/solution.py
@@ -620,19 +620,11 @@
 
     barrier = pltpu.get_barrier_semaphore()
 
-    def greet(j, carry):
-        other = jnp.logical_or(j // groups != t, j % groups != me)
-
-        @pl.when(other)
-        def _():
-            pl.semaphore_signal(
-                barrier, inc=1, device_id={TOWER: j // groups, DP: j % groups},
-                device_id_type=MESH,
-            )
-
-        return carry
-
-    lax.fori_loop(0, 2 * groups, greet, 0)
+    for step in range(1, 2 * groups):
+        other = (t * groups + me + step) % (2 * groups)
+        pl.semaphore_signal(
+            barrier, inc=1, device_id={TOWER: other // groups, DP: other % groups},
+            device_id_type=MESH)
     pl.semaphore_wait(barrier, 2 * groups - 1)
     for cond, what in local:
         do(cond, what.wait)
@@ -1651,7 +1643,10 @@
     end_a(2)
     small_sums(5)
 
-    r.o_vec[...] = r.ln[last]
+    lane_row = lax.broadcasted_iota(jnp.int32, (D, LANES), 0)
+    lane_col = lax.broadcasted_iota(jnp.int32, (D, LANES), 1)
+    pick = jnp.where(lane_row == me * plan.vec + lane_col, 1.0, 0.0)
+    r.o_vec[...] = jnp.dot(r.ln[last], pick, preferred_element_type=F32, precision=best)
     r.o_loss[...] = r.ln[last][:, 0:LANES] * (1.0 / (groups * QPD))
 
     r.o_d[...] = r.dbuf[me, :, pl.ds(0, D)]
@@ -1706,13 +1701,8 @@
     o_q[...] = q_ref[...]
     o_d[...] = d_ref[...]
     o_loss[...] = loss_ref[4:5, 0:1]
-    first = lax.axis_index(DP) * plan.vec
-    row = lax.broadcasted_iota(jnp.int32, (D, LANES), 0)
-    col = lax.broadcasted_iota(jnp.int32, (D, LANES), 1)
-    pick = jnp.where(row == first + col, 1.0, 0.0)
-    own = jnp.dot(vec_ref[...], pick, preferred_element_type=F32, precision=exact_product_accuracy)
     for k, out in enumerate(o_vecs):
-        out[...] = own[k : k + 1, 0 : plan.vec]
+        out[...] = vec_ref[k : k + 1, 0 : plan.vec]
 
 
 def on_device_kernel(plan, tokens, query_lengths, doc_lengths, positives, w_qkv, w_out, w_gate,
@@ -1727,7 +1717,7 @@
         functools.partial(whole_step, plan),
         out_shape=(
             shape((count, D), F32), shape((shard, plan.width_a), BF), shape((2, shard, plan.ff), BF),
-            shape((plan.shard_ff, D), BF), shape((8, D), F32), shape((QPD, D), F32),
+            shape((plan.shard_ff, D), BF), shape((8, LANES), F32), shape((QPD, D), F32),
             shape((1, D), F32), shape((8, LANES), F32),
         ),
         in_specs=[smem] * 3 + [hbm] * 3 + [vmem] * 4 + [hbm] * 5,

time: 158 us -> 158 us (level)
  no operation moved by 1% of the time
where the time goes in v7:
time: 158 us
  Pallas kernels  156 us (99%)
    pallas_call x1, Pallas kernels, on_device_kernel(): pl.pallas_call(functools.partial(whole_step, plan), out_shape=(shape((cou...  153 us
    pallas_call x1, Pallas kernels, on_device_kernel(): pl.pallas_call(functools.partial(finish, plan), out_shape=(shape((1, 1),...  3.26 us

profile of v7, /device:TPU:0, one launch (start us, length us, event | category | flops | bytes accessed | tf_op | source)
XLA Modules:
  0.0 157.7 jit_solution(5381493999241657351)
XLA Ops:
  1.3 153.0 %whole_step.1 = (f32[256,768]{1,0:T(8,128)}, bf16[48,3072]{1,0:T(8,128)(2,1)}, bf16[2,48,3072]{2,1,0:T(8,128)(2,1)}, bf16[192,768]{1,0:T(8,128)(2,1)}, f32[8,128...) custom-call(s32[4]{0:T(128)} %refs_0_.1, s32[1]{0:T(128)S(6)} %copy.28.refs_1_, s32[64]{0:T(128)} %refs_2_.1, ...), custom_call_target="tpu_custom_call" | custom-call | tf_op jit(solution)/shard_map/whole_step/pallas_call | solution.py:1716
  154.4 3.3 %finish.1 = (f32[1,1]{1,0:T(1,128)}, f32[4,768]{1,0:T(4,128)}, f32[1,768]{1,0:T(1,128)}, f32[1,256,768]{2,1,0:T(8,128)}, f32[48,2304]{1,0:T(8,128)}, /*index=5*/...) custom-call(bf16[48,3072]{1,0:T(8,128)(2,1)} %get-tuple-element.34.r, ...), custom_call_target="tpu_custom_call" | custom-call | tf_op jit(solution)/shard_map/finish/pallas_call | solution.py:1733
